TPU v7x, 128 devices: a whole 4x4x4 slice. The times are simulated.
128 devices in a mesh: expert: 16 (over z, x), wshard: 8 (over y, core).
Axes of the slice: x: 4, y: 4, z: 4, core: 2. Of those that a mesh axis runs over, the one named last changes fastest.
Arguments:
- inputs: float32 [128, 197, 768], P(('expert', 'wshard')), may hold values from -6 to 6
- routes: int32 [2, 128, 197, 2], P(None, ('expert', 'wshard')), may hold values from 0 to 15, all different within a row; in each aligned block of 197 rows (0 to 196, 197 to 393, ..., all dimensions but the last counted through in order) at most 25 rows name the same one
- first_gain: bfloat16 [2, 768], P(None, 'wshard'), may hold values from 0.5 to 1.5
- first_bias: bfloat16 [2, 768], P(None, 'wshard'), may hold values from -3 to 3
- qkv_weight: bfloat16 [2, 768, 2304], P(None, 'wshard'), may hold values from -0.21875 to 0.21875
- proj_weight: bfloat16 [2, 768, 768], P(None, 'wshard'), may hold values from -0.75 to 0.75
- second_gain: bfloat16 [2, 768], P(None, 'wshard'), may hold values from 0.5 to 1.5
- second_bias: bfloat16 [2, 768], P(None, 'wshard'), may hold values from -3 to 3
- router_weight: bfloat16 [2, 768, 16], P(None, 'wshard'), may hold values from -0.4375 to 0.4375
- hidden_weight: bfloat16 [2, 16, 768, 3072], P(None, 'expert', None, 'wshard'), may hold values from -0.21875 to 0.21875
- output_weight: bfloat16 [2, 16, 3072, 768], P(None, 'expert', 'wshard'), may hold values from -0.875 to 0.875
- cotangent: float32 [128, 197, 768], P(('expert', 'wshard')), may hold values from -6 to 6
Outputs:
- outputs: float32 [128, 197, 768], P(('expert', 'wshard'))
- input_grad: float32 [128, 197, 768], P(('expert', 'wshard'))
- first_gain_grad: float32 [2, 768], P(None, 'wshard')
- first_bias_grad: float32 [2, 768], P(None, 'wshard')
- qkv_weight_grad: float32 [2, 768, 2304], P(None, 'wshard')
- proj_weight_grad: float32 [2, 768, 768], P(None, 'wshard')
- second_gain_grad: float32 [2, 768], P(None, 'wshard')
- second_bias_grad: float32 [2, 768], P(None, 'wshard')
- router_weight_grad: float32 [2, 768, 16], P(None, 'wshard')
- hidden_weight_grad: float32 [2, 16, 768, 3072], P(None, 'expert', None, 'wshard')
- output_weight_grad: float32 [2, 16, 3072, 768], P(None, 'expert', 'wshard')
Inputs may be any that keep to these rules, and one draw needn't show every extreme that they name: `routes`: each token names two different experts. In each layer the tokens of one image name any one expert at most 25 times over both choices, and that many somewhere.
All inputs are finite; a program needn't handle non-finite values.
Results may differ from a plain program's by a relative error of at most 0.035.
Values may be sent and summed in bfloat16 or wider, within the bound.
No kernel may reach another device: no remote copies, remote signals or barrier semaphores. Data moves between devices by JAX's collectives and lax.ppermute only.
A program may use at most 192 MiB of HBM per device.

v0:
```python
import math

import jax
import jax.numpy as jnp
from jax import lax
from jax.sharding import PartitionSpec as P

HEADS = 12
RECV = 400


EPSILON = 1e-06
ROOT_HALF = 0.7071067811865476
INV_ROOT_TAU = 0.3989422804014327


def standardize(rows):
    center = jnp.mean(rows, axis=-1, keepdims=True)
    shifted = rows - center
    variance = jnp.mean(shifted * shifted, axis=-1, keepdims=True)
    inverse = lax.rsqrt(variance + EPSILON)
    return (shifted * inverse, inverse)


def norm_backward(grad_in, normed, inverse, gain):
    scaled = grad_in * gain.astype(jnp.float32)
    first = jnp.mean(scaled, axis=-1, keepdims=True)
    second = jnp.mean(scaled * normed, axis=-1, keepdims=True)
    return inverse * (scaled - first - normed * second)


def gelu_value(pre):
    return 0.5 * pre * (1.0 + jax.scipy.special.erf(pre * ROOT_HALF))


def gelu_slope(pre):
    return (
        0.5 * (1.0 + jax.scipy.special.erf(pre * ROOT_HALF))
        + pre * jnp.exp(-0.5 * pre * pre) * INV_ROOT_TAU
    )


def slot_table(flat_routes, count):
    onehot = (flat_routes[..., None] == jnp.arange(count, dtype=jnp.int32)).astype(jnp.int32)
    before = jnp.cumsum(onehot, axis=-2) - onehot
    return jnp.sum(before * onehot, axis=-1)


def matmul(left, right):
    return jnp.dot(left, right, preferred_element_type=jnp.float32)


def per_device(
    inputs,
    routes,
    first_gain,
    first_bias,
    qkv_weight,
    proj_weight,
    second_gain,
    second_bias,
    router_weight,
    hidden_weight,
    output_weight,
    cotangent,
):
    experts = lax.axis_size("expert")
    state = inputs[0]
    length, width = state.shape
    head_size = width // HEADS
    scale = 1.0 / math.sqrt(head_size)
    capacity = RECV // experts
    row_count = experts * capacity
    depth = routes.shape[0]
    expert_ids = jnp.arange(experts, dtype=jnp.int32)
    saved = []
    for layer in range(depth):
        gathered = (
            lax.all_gather(first_gain[layer], "wshard", axis=0, tiled=True),
            lax.all_gather(first_bias[layer], "wshard", axis=0, tiled=True),
            lax.all_gather(qkv_weight[layer], "wshard", axis=0, tiled=True),
            lax.all_gather(proj_weight[layer], "wshard", axis=0, tiled=True),
            lax.all_gather(second_gain[layer], "wshard", axis=0, tiled=True),
            lax.all_gather(second_bias[layer], "wshard", axis=0, tiled=True),
            lax.all_gather(router_weight[layer], "wshard", axis=0, tiled=True),
        )
        gain_one, bias_one, qkv_full, proj_full, gain_two, bias_two, router_full = gathered
        normed_one, inverse_one = standardize(state)
        attn_in = (normed_one * gain_one.astype(jnp.float32) + bias_one.astype(jnp.float32)).astype(
            jnp.bfloat16
        )
        qkv = matmul(attn_in, qkv_full).astype(jnp.bfloat16)
        query = qkv[:, :width].reshape(length, HEADS, head_size)
        keys = qkv[:, width : 2 * width].reshape(length, HEADS, head_size)
        values = qkv[:, 2 * width :].reshape(length, HEADS, head_size)
        scores = jnp.einsum("shd,thd->hst", query, keys, preferred_element_type=jnp.float32) * scale
        log_total = jnp.log(jnp.sum(jnp.exp(scores), axis=-1, keepdims=True))
        probs_low = jnp.exp(scores - log_total).astype(jnp.bfloat16)
        mixed = jnp.einsum("hst,thd->shd", probs_low, values, preferred_element_type=jnp.float32)
        mixed = mixed.reshape(length, width).astype(jnp.bfloat16)
        middle = state + matmul(mixed, proj_full)
        normed_two, inverse_two = standardize(middle)
        moe_in = (normed_two * gain_two.astype(jnp.float32) + bias_two.astype(jnp.float32)).astype(
            jnp.bfloat16
        )
        logits = matmul(moe_in, router_full)
        raised = jnp.exp(logits)
        router_probs = raised / jnp.sum(raised, axis=-1, keepdims=True)
        chosen = routes[layer, 0]
        choice_mask = (chosen[..., None] == expert_ids).astype(jnp.float32)
        gates = jnp.sum(choice_mask * router_probs[:, None, :], axis=-1)
        flat = chosen.reshape(-1)
        position = flat * capacity + slot_table(flat, experts)
        sent = (
            jnp.zeros((row_count, width), jnp.bfloat16)
            .at[position]
            .set(jnp.repeat(moe_in, 2, axis=0))
        )
        received = lax.all_to_all(
            sent.reshape(experts, capacity, width),
            "expert",
            split_axis=0,
            concat_axis=0,
            tiled=True,
        )
        received = received.reshape(row_count, width)
        full_hidden, full_output = (
            lax.all_gather(hidden_weight[layer, 0], "wshard", axis=1, tiled=True),
            lax.all_gather(output_weight[layer, 0], "wshard", axis=0, tiled=True),
        )
        pre = matmul(received, full_hidden)
        act = gelu_value(pre).astype(jnp.bfloat16)
        result = matmul(act, full_output).astype(jnp.bfloat16)
        kept = (received, pre, act, full_hidden, full_output)
        returned = lax.all_to_all(
            result.reshape(experts, capacity, width),
            "expert",
            split_axis=0,
            concat_axis=0,
            tiled=True,
        )
        picked = returned.reshape(row_count, width)[position].reshape(length, 2, width)
        state = middle + jnp.sum(gates[..., None] * picked.astype(jnp.float32), axis=1)
        saved.append(
            (
                gathered,
                normed_one,
                inverse_one,
                attn_in,
                query,
                keys,
                values,
                log_total,
                mixed,
                normed_two,
                inverse_two,
                moe_in,
                router_probs,
                choice_mask,
                gates,
                position,
                picked,
                kept,
            )
        )
    grad = cotangent[0]
    layer_parts = []
    expert_parts = []
    for layer in reversed(range(depth)):
        (
            gathered,
            normed_one,
            inverse_one,
            attn_in,
            query,
            keys,
            values,
            log_total,
            mixed,
            normed_two,
            inverse_two,
            moe_in,
            router_probs,
            choice_mask,
            gates,
            position,
            picked,
            kept,
        ) = saved[layer]
        gain_one, bias_one, qkv_full, proj_full, gain_two, bias_two, router_full = gathered
        gate_grad = jnp.sum(grad[:, None, :] * picked.astype(jnp.float32), axis=-1)
        routed_grad = (
            (gates[..., None] * grad[:, None, :]).astype(jnp.bfloat16).reshape(2 * length, width)
        )
        grad_sent = jnp.zeros((row_count, width), jnp.bfloat16).at[position].set(routed_grad)
        grad_received = lax.all_to_all(
            grad_sent.reshape(experts, capacity, width),
            "expert",
            split_axis=0,
            concat_axis=0,
            tiled=True,
        )
        grad_received = grad_received.reshape(row_count, width)
        rows_kept, pre, act, full_hidden, full_output = kept
        act_grad = matmul(grad_received, full_output.T)
        output_whole = matmul(act.T, grad_received)
        pre_grad = (act_grad * gelu_slope(pre)).astype(jnp.bfloat16)
        hidden_whole = matmul(rows_kept.T, pre_grad)
        row_grad = matmul(pre_grad, full_hidden.T).astype(jnp.bfloat16)
        hidden_part, output_part = (
            lax.psum_scatter(
                hidden_whole.astype(jnp.bfloat16), "wshard", scatter_dimension=1, tiled=True
            ).astype(jnp.float32),
            lax.psum_scatter(
                output_whole.astype(jnp.bfloat16), "wshard", scatter_dimension=0, tiled=True
            ).astype(jnp.float32),
        )
        back = lax.all_to_all(
            row_grad.reshape(experts, capacity, width),
            "expert",
            split_axis=0,
            concat_axis=0,
            tiled=True,
        )
        back = back.reshape(row_count, width)[position].reshape(length, 2, width)
        prob_grad = jnp.sum(choice_mask * gate_grad[..., None], axis=1)
        logit_grad = router_probs * (
            prob_grad - jnp.sum(router_probs * prob_grad, axis=-1, keepdims=True)
        )
        logit_grad = logit_grad.astype(jnp.bfloat16)
        router_grad = matmul(moe_in.T, logit_grad)
        moe_in_grad = jnp.sum(back.astype(jnp.float32), axis=1) + matmul(logit_grad, router_full.T)
        second_gain_grad = jnp.sum(moe_in_grad * normed_two, axis=0)
        second_bias_grad = jnp.sum(moe_in_grad, axis=0)
        middle_grad = grad + norm_backward(moe_in_grad, normed_two, inverse_two, gain_two)
        middle_low = middle_grad.astype(jnp.bfloat16)
        proj_grad = matmul(mixed.T, middle_low)
        mixed_grad = (
            matmul(middle_low, proj_full.T).astype(jnp.bfloat16).reshape(length, HEADS, head_size)
        )
        scores = jnp.einsum("shd,thd->hst", query, keys, preferred_element_type=jnp.float32) * scale
        probs = jnp.exp(scores - log_total)
        probs_low = probs.astype(jnp.bfloat16)
        values_grad = jnp.einsum(
            "hst,shd->thd", probs_low, mixed_grad, preferred_element_type=jnp.float32
        )
        prob_grad_att = jnp.einsum(
            "shd,thd->hst", mixed_grad, values, preferred_element_type=jnp.float32
        )
        score_grad = probs * (
            prob_grad_att - jnp.sum(probs * prob_grad_att, axis=-1, keepdims=True)
        )
        score_low = (score_grad * scale).astype(jnp.bfloat16)
        query_grad = jnp.einsum("hst,thd->shd", score_low, keys, preferred_element_type=jnp.float32)
        keys_grad = jnp.einsum("hst,shd->thd", score_low, query, preferred_element_type=jnp.float32)
        qkv_grad = jnp.concatenate(
            [
                query_grad.reshape(length, width),
                keys_grad.reshape(length, width),
                values_grad.reshape(length, width),
            ],
            axis=-1,
        ).astype(jnp.bfloat16)
        qkv_grad_weight = matmul(attn_in.T, qkv_grad)
        attn_in_grad = matmul(qkv_grad, qkv_full.T)
        first_gain_grad = jnp.sum(attn_in_grad * normed_one, axis=0)
        first_bias_grad = jnp.sum(attn_in_grad, axis=0)
        grad = middle_grad + norm_backward(attn_in_grad, normed_one, inverse_one, gain_one)
        shares = (
            lax.psum_scatter(
                first_gain_grad.astype(jnp.bfloat16), "wshard", scatter_dimension=0, tiled=True
            ).astype(jnp.float32),
            lax.psum_scatter(
                first_bias_grad.astype(jnp.bfloat16), "wshard", scatter_dimension=0, tiled=True
            ).astype(jnp.float32),
            lax.psum_scatter(
                qkv_grad_weight.astype(jnp.bfloat16), "wshard", scatter_dimension=0, tiled=True
            ).astype(jnp.float32),
            lax.psum_scatter(
                proj_grad.astype(jnp.bfloat16), "wshard", scatter_dimension=0, tiled=True
            ).astype(jnp.float32),
            lax.psum_scatter(
                second_gain_grad.astype(jnp.bfloat16), "wshard", scatter_dimension=0, tiled=True
            ).astype(jnp.float32),
            lax.psum_scatter(
                second_bias_grad.astype(jnp.bfloat16), "wshard", scatter_dimension=0, tiled=True
            ).astype(jnp.float32),
            lax.psum_scatter(
                router_grad.astype(jnp.bfloat16), "wshard", scatter_dimension=0, tiled=True
            ).astype(jnp.float32),
        )
        totals = (
            lax.psum(shares[0].astype(jnp.bfloat16), "expert").astype(jnp.float32),
            lax.psum(shares[1].astype(jnp.bfloat16), "expert").astype(jnp.float32),
            lax.psum(shares[2].astype(jnp.bfloat16), "expert").astype(jnp.float32),
            lax.psum(shares[3].astype(jnp.bfloat16), "expert").astype(jnp.float32),
            lax.psum(shares[4].astype(jnp.bfloat16), "expert").astype(jnp.float32),
            lax.psum(shares[5].astype(jnp.bfloat16), "expert").astype(jnp.float32),
            lax.psum(shares[6].astype(jnp.bfloat16), "expert").astype(jnp.float32),
        )
        layer_parts.append(totals)
        expert_parts.append((hidden_part, output_part))
    layer_parts = list(reversed(layer_parts))
    expert_parts = list(reversed(expert_parts))
    stacked = [jnp.stack([entry[index] for entry in layer_parts]) for index in range(7)]
    hidden_grads = jnp.stack([entry[0] for entry in expert_parts])[:, None]
    output_grads = jnp.stack([entry[1] for entry in expert_parts])[:, None]
    return (
        state[None],
        grad[None],
        stacked[0],
        stacked[1],
        stacked[2],
        stacked[3],
        stacked[4],
        stacked[5],
        stacked[6],
        hidden_grads,
        output_grads,
    )


def solution(mesh):
    in_specs = (
        P(("expert", "wshard"), None, None),
        P(None, ("expert", "wshard"), None, None),
        P(None, "wshard"),
        P(None, "wshard"),
        P(None, "wshard", None),
        P(None, "wshard", None),
        P(None, "wshard"),
        P(None, "wshard"),
        P(None, "wshard", None),
        P(None, "expert", None, "wshard"),
        P(None, "expert", "wshard", None),
        P(("expert", "wshard"), None, None),
    )
    out_specs = (
        P(("expert", "wshard"), None, None),
        P(("expert", "wshard"), None, None),
        P(None, "wshard"),
        P(None, "wshard"),
        P(None, "wshard", None),
        P(None, "wshard", None),
        P(None, "wshard"),
        P(None, "wshard"),
        P(None, "wshard", None),
        P(None, "expert", None, "wshard"),
        P(None, "expert", "wshard", None),
    )
    return jax.shard_map(
        per_device, mesh=mesh, in_specs=in_specs, out_specs=out_specs, check_vma=False
    )
```

profile of v0, /device:TPU:24, one launch (start us, length us, event | category | flops | bytes accessed | tf_op | source)
XLA Modules:
  0.0 863.3 jit_solution(12180014499083563032)
XLA Ops:
  19.5 22.7 %all-reduce.21 = (bf16[768]{0:T(1024)(128)(2,1)S(1)}, bf16[768]{0:T(1024)(128)(2,1)S(1)}, bf16[768]{0:T(1024)(128)(2,1)S(1)}, bf16[768]{0:T(1024)(128)(2,1)S(1)}...) all-reduce(bf16[768]{0:T(1024)(128)(2,1)S(1)} %dynamic-update-slice, ...), channel_id=3, replica_groups=mesh['expert'=16,'wshard'=8] {'wshard'}, use_global_device_ids=true, to_apply=%add.3 | all-reduce | flops 6144 | bytes 24576
  57.8 8.3 all-gather.29.cloned.1.call-done
  73.5 6.9 all-to-all-start
  81.0 13.7 %all-gather.6 = bf16[1,768,16]{2,0,1:T(2,128)(2,1)S(1)} all-gather(bf16[1,96,16]{2,0,1:T(2,128)(2,1)S(1)} %copy.249), channel_id=8, replica_groups=mesh['expert'=16,'wshard'=8] {'wshard'}, dimensions={1}, use_global_device_ids=true | all-gather | bytes 27648 | tf_op jit(solution)/shard_map/all_gather | solution.py:85
  95.5 8.6 all-gather.31.cloned.1.call-done
  104.1 6.7 multiply_convert_fusion.1
  110.8 29.8 %all-gather.33.cloned.1.call-done = bf16[1,1,3072,768]{3,2,1,0:T(8,128)(2,1)} async-done(((bf16[1,1,384,768]{3,2,1,0:T(8,128)(2,1)}), bf16[1,1,3072,768]{3,2,1,0:T(8,128)(2,1)}) %all-gather.33.cloned.1.call-update) | async-done | bytes 4718608 | tf_op jit(solution)/shard_map/all_gather | solution.py:129
  140.6 5.1 fusion.73
  146.9 7.0 all-to-all-start.1
  153.9 13.6 %all-gather.15 = bf16[1,768,16]{2,0,1:T(2,128)(2,1)S(1)} all-gather(bf16[1,96,16]{2,0,1:T(2,128)(2,1)S(1)} %copy.250), channel_id=17, replica_groups=mesh['expert'=16,'wshard'=8] {'wshard'}, dimensions={1}, use_global_device_ids=true | all-gather | bytes 27648 | tf_op jit(solution)/shard_map/all_gather | solution.py:85
  193.5 5.1 all-gather.37.cloned.1.call-done
  210.6 6.9 all-to-all-start.2
  227.5 4.8 all-to-all-done.2
  232.3 4.3 all-to-all-start.4
  238.0 6.8 multiply_convert_fusion
  244.8 26.7 %all-gather.41.cloned.1.call-done = bf16[1,1,3072,768]{3,2,1,0:T(8,128)(2,1)} async-done(((bf16[1,1,384,768]{3,2,1,0:T(8,128)(2,1)}), bf16[1,1,3072,768]{3,2,1,0:T(8,128)(2,1)}) %all-gather.41.cloned.1.call-update) | async-done | bytes 4718608 | tf_op jit(solution)/shard_map/all_gather | solution.py:129
  271.5 5.1 fusion.79
  277.7 7.0 all-to-all-start.3
  286.1 5.8 fusion.9
  293.4 5.3 fusion.76
  300.9 7.6 all-to-all-start.5
  315.5 4.7 multiply_reduce_fusion.3
  340.6 5.5 fusion.88
  346.1 5.4 fusion.91
  351.6 4.3 convolution_convert_fusion.11
  369.5 4.8 all-to-all-start.6
  376.8 11.2 %all-to-all-done.6 = bf16[16,25,768]{2,1,0:T(8,128)(2,1)} async-done(((bf16[16,25,768]{2,1,0:T(8,128)(2,1)}), bf16[16,25,768]{2,1,0:T(8,128)(2,1)}, u32[]{:S(2)}, u32[]{:S(2)}) %all-to-all-start.6) | async-done | bytes 614432 | tf_op jit(solution)/shard_map/all_to_all | solution.py:196
  389.4 5.8 fusion.15
  396.5 5.4 fusion.70
  404.2 4.4 all-to-all-start.7
  410.6 10.8 %all-to-all-done.7 = bf16[16,25,768]{2,1,0:T(8,128)(2,1)} async-done(((bf16[16,25,768]{2,1,0:T(8,128)(2,1)}), bf16[16,25,768]{2,1,0:T(8,128)(2,1)}, u32[]{:S(2)}, u32[]{:S(2)}) %all-to-all-start.7) | async-done | bytes 614432 | tf_op jit(solution)/shard_map/all_to_all | solution.py:218
  451.0 5.4 fusion.82
  456.5 5.5 fusion.85
  469.1 6.0 convolution_convert_fusion.2
  475.1 6.6 copy.245
  481.9 16.4 %reduce-scatter.21.cloned.1.call-done = bf16[96,2304]{1,0:T(8,128)(2,1)} async-done(((bf16[768,2304]{1,0:T(8,128)(2,1)}), bf16[96,2304]{1,0:T(8,128)(2,1)}) %reduce-scatter.21.cloned.1.call-update) | async-done | bytes 442384 | tf_op jit(solution)/shard_map/reduce_scatter | solution.py:276
  498.3 37.8 %reduce-scatter.19.cloned.1.call-done = bf16[96,2304]{1,0:T(8,128)(2,1)} async-done(((bf16[768,2304]{1,0:T(8,128)(2,1)}), bf16[96,2304]{1,0:T(8,128)(2,1)}) %reduce-scatter.19.cloned.1.call-update) | async-done | bytes 442384 | tf_op jit(solution)/shard_map/reduce_scatter | solution.py:276
  536.2 6.1 convolution_convert_fusion.3
  542.2 6.7 copy.243
  550.0 6.6 convolution_convert_fusion
  557.7 6.5 convolution_convert_fusion.1
  569.5 30.8 %reduce-scatter.31.cloned.1.call-done = bf16[96,16]{1,0:T(8,128)(2,1)} async-done(((bf16[768,16]{1,0:T(8,128)(2,1)}), bf16[96,16]{1,0:T(8,128)(2,1)}) %reduce-scatter.31.cloned.1.call-update) | async-done | bytes 3088
  606.5 23.2 %all-reduce.20 = (bf16[768]{0:T(1024)(128)(2,1)S(1)}, bf16[768]{0:T(1024)(128)(2,1)S(1)}, bf16[768]{0:T(1024)(128)(2,1)S(1)}, bf16[768]{0:T(1024)(128)(2,1)S(1)}...) all-reduce(bf16[768]{0:T(1024)(128)(2,1)S(1)} %get-tuple-element.81, ...), channel_id=21, replica_groups=mesh['expert'=16,'wshard'=8] {'wshard'}, use_global_device_ids=true, to_apply=%region_48.49.clone | all-reduce | flops 6144 | bytes 24576
  630.4 74.8 %all-reduce.18 = (bf16[1,96]{1,0:T(2,128)(2,1)S(1)}, bf16[1,96]{1,0:T(2,128)(2,1)S(1)}, bf16[1,96]{1,0:T(2,128)(2,1)S(1)}, bf16[1,96]{1,0:T(2,128)(2,1)S(1)}, bf...) all-reduce(bf16[1,96]{1,0:T(2,128)(2,1)S(1)} %dynamic-slice_bitcast, ...), channel_id=1, replica_groups=mesh['expert'=16,'wshard'=8] {'expert'}, use_global_device_ids=true, to_apply=%region_49.50 | all-reduce | flops 3840 | bytes 15360 | tf_op jit(solution)/shard_map/psum | solution.py:293
  709.4 24.3 %all-reduce.24.cloned.1.call-done = (bf16[1,96,2304]{2,1,0:T(8,128)(2,1)}, bf16[1,96,2304]{2,1,0:T(8,128)(2,1)}, bf16[1,96,768]{2,1,0:T(8,128)(2,1)}, bf16[1,96,768]{2,1,0:T(8,128)(2,1)}) async-done(((bf16[1,96,2304]{2,1,0:T(8,128)(2,1)}, bf16[1,96,2304]{2,1,0:T(8,128)(2,1)}, bf16[1,96,768]{2,1,0:T(8,128)(2,1)}, bf16[1,96,768]{2,1,0:T(8,128)(2,1)}), (bf16[1,96,2304]{2,1,0:T(8,128)(2,1)}, ...) | async-done | bytes 1179664 | tf_op jit(solution)/shard_map/psum | solution.py:295
  738.0 32.8 %reduce-scatter.35.cloned.1.call-done = bf16[384,768]{1,0:T(8,128)(2,1)} async-done(((bf16[3072,768]{1,0:T(8,128)(2,1)}), bf16[384,768]{1,0:T(8,128)(2,1)}) %reduce-scatter.35.cloned.1.call-update) | async-done | bytes 589840
  772.1 39.2 %reduce-scatter.29.cloned.1.call-done = bf16[384,768]{1,0:T(8,128)(2,1)} async-done(((bf16[3072,768]{1,0:T(8,128)(2,1)}), bf16[384,768]{1,0:T(8,128)(2,1)}) %reduce-scatter.29.cloned.1.call-update) | async-done | bytes 589840 | tf_op jit(solution)/shard_map/reduce_scatter | solution.py:214
  811.3 40.7 %reduce-scatter.27.cloned.1.call-done = bf16[384,768]{1,0:T(8,128)(2,1)} async-done(((bf16[3072,768]{1,0:T(8,128)(2,1)}), bf16[384,768]{1,0:T(8,128)(2,1)}) %reduce-scatter.27.cloned.1.call-update) | async-done | bytes 589840 | tf_op jit(solution)/shard_map/reduce_scatter | solution.py:214
  (449 shorter events, 206.5 us)
Async XLA Ops:
  7.2 40.9 %all-gather.27.cloned.1.call-start = ((), (), s32[]{:S(2)}) async-start(), calls=%async_computation.24 | async-start | bytes 3981312 | tf_op jit(solution)/shard_map/all_gather | solution.py:81
  9.5 56.6 %all-gather.29.cloned.1.call-start = ((), (), s32[]{:S(2)}) async-start(), calls=%async_computation.25 | async-start | bytes 1327104 | tf_op jit(solution)/shard_map/all_gather | solution.py:82
  11.3 92.8 %all-gather.31.cloned.1.call-start = ((), (), s32[]{:S(2)}) async-start(), calls=%async_computation.26 | async-start | bytes 5308416 | tf_op jit(solution)/shard_map/all_gather | solution.py:128
  12.6 29.7 %copy-start = (f32[1,197,768]{2,0,1:T(1,128)S(1)}, f32[1,197,768]{2,0,1:T(1,128)}, u32[]{:S(2)}) copy-start(f32[1,197,768]{2,0,1:T(1,128)} %param.12) | copy-start | bytes 1815556
  12.6 128.0 %all-gather.33.cloned.1.call-start = ((), (), s32[]{:S(2)}) async-start(), calls=%async_computation.27 | async-start | bytes 5308416 | tf_op jit(solution)/shard_map/all_gather | solution.py:129
  13.8 29.8 %copy-start.79 = (s32[2,1,197,2]{2,3,1,0:T(2,128)S(1)}, s32[2,1,197,2]{2,3,1,0:T(2,128)}, u32[]{:S(2)}) copy-start(s32[2,1,197,2]{2,3,1,0:T(2,128)} %param.13) | copy-start | bytes 9460
  13.8 166.9 %all-gather.35.cloned.1.call-start = ((), (), s32[]{:S(2)}) async-start(), calls=%async_computation.28 | async-start | bytes 3981312 | tf_op jit(solution)/shard_map/all_gather | solution.py:81
  14.4 184.2 %all-gather.37.cloned.1.call-start = ((), (), s32[]{:S(2)}) async-start(), calls=%async_computation.29 | async-start | bytes 1327104 | tf_op jit(solution)/shard_map/all_gather | solution.py:82
  15.0 223.0 %all-gather.39.cloned.1.call-start = ((), (), s32[]{:S(2)}) async-start(), calls=%async_computation.30 | async-start | bytes 5308416 | tf_op jit(solution)/shard_map/all_gather | solution.py:128
  15.7 255.8 %all-gather.41.cloned.1.call-start = ((), (), s32[]{:S(2)}) async-start(), calls=%async_computation.31 | async-start | bytes 5308416 | tf_op jit(solution)/shard_map/all_gather | solution.py:129
  43.6 24.7 %copy-start.34 = (f32[768]{0:T(1024)}, f32[768]{0:T(1024)S(1)}, u32[]{:S(2)}) copy-start(f32[768]{0:T(1024)S(1)} %convert_element_type.356) | copy-start | bytes 9220
  44.2 127.8 %copy-start.46 = (s32[197,2]{0,1:T(2,128)}, s32[197,2]{0,1:T(2,128)S(1)}, u32[]{:S(2)}) copy-start(s32[197,2]{0,1:T(2,128)S(1)} %get-tuple-element.146) | copy-start | bytes 4732
  48.1 46.5 %copy-start.76 = (s32[394,1]{0,1:T(1,128)}, s32[394,1]{0,1:T(1,128)S(1)}, u32[]{:S(2)}) copy-start(s32[394,1]{0,1:T(1,128)S(1)} %compare_select_fusion.1) | copy-start | bytes 4732
  54.8 11.3 %copy-start.10 = (f32[12,197,197]{1,2,0:T(8,128)}, f32[12,197,197]{1,2,0:T(8,128)S(1)}, u32[]{:S(2)}) copy-start(f32[12,197,197]{1,2,0:T(8,128)S(1)} %fusion.194) | copy-start | bytes 5588500
  68.8 11.6 %copy-start.78 = (bf16[2,96,16]{1,2,0:T(8,128)(2,1)S(1)}, bf16[2,96,16]{1,2,0:T(8,128)(2,1)}, u32[]{:S(2)}) copy-start(bf16[2,96,16]{1,2,0:T(8,128)(2,1)} %param.20) | copy-start | bytes 18436
  73.5 21.8 %all-to-all-start = ((bf16[16,25,768]{2,1,0:T(8,128)(2,1)}), bf16[16,25,768]{2,1,0:T(8,128)(2,1)S(1)}, u32[]{:S(2)}, u32[]{:S(2)}) async-start(bf16[16,25,768]{2,1,0:T(8,128)(2,1)} %reshape.366), calls=%async_computation | async-start | bytes 1572864 | tf_op jit(solution)/shard_map/all_to_all | solution.py:119
  94.6 80.2 %copy-start.52 = (s32[1024]{0:T(1024)}, s32[1024]{0:T(1024)S(1)}, u32[]{:S(2)}) copy-start(s32[1024]{0:T(1024)S(1)} %pad_clamp_fusion.1) | copy-start | bytes 12292
  94.7 16.1 %copy-start.77 = (s32[394,1]{0,1:T(1,128)}, s32[394,1]{0,1:T(1,128)S(1)}, u32[]{:S(2)}) copy-start(s32[394,1]{0,1:T(1,128)S(1)} %compare_select_fusion) | copy-start | bytes 4732
  95.5 15.3 %copy-start.24 = (bf16[400,768]{1,0:T(8,128)(2,1)}, bf16[400,768]{1,0:T(8,128)(2,1)S(1)}, u32[]{:S(2)}) copy-start(bf16[400,768]{1,0:T(8,128)(2,1)S(1)} %reshape.367) | copy-start | bytes 1843204
  145.8 22.8 %copy-start.12 = (f32[1,197,768]{2,0,1:T(1,128)S(1)}, f32[1,197,768]{2,0,1:T(1,128)}, u32[]{:S(2)}) copy-start(f32[1,197,768]{2,0,1:T(1,128)} %param.23) | copy-start | bytes 1815556
  146.9 26.6 %all-to-all-start.1 = ((bf16[16,25,768]{2,1,0:T(8,128)(2,1)}), bf16[16,25,768]{2,1,0:T(8,128)(2,1)}, u32[]{:S(2)}, u32[]{:S(2)}) async-start(bf16[16,25,768]{2,1,0:T(8,128)(2,1)} %reshape.368), calls=%async_computation.1 | async-start | bytes 1572864 | tf_op jit(solution)/shard_map/all_to_all | solution.py:135
  167.7 13.1 %copy-start.40 = (f32[768]{0:T(1024)}, f32[768]{0:T(1024)S(1)}, u32[]{:S(2)}) copy-start(f32[768]{0:T(1024)S(1)} %convert_element_type.358) | copy-start | bytes 9220
  167.7 13.1 %copy-start.67 = (f32[768]{0:T(1024)}, f32[768]{0:T(1024)S(1)}, u32[]{:S(2)}) copy-start(f32[768]{0:T(1024)S(1)} %convert_element_type.359) | copy-start | bytes 9220
  167.7 33.0 %copy-start.36 = (f32[768]{0:T(1024)}, f32[768]{0:T(1024)S(1)}, u32[]{:S(2)}) copy-start(f32[768]{0:T(1024)S(1)} %convert_element_type.360) | copy-start | bytes 9220
  200.9 16.5 %copy-start.6 = (bf16[197,768]{1,0:T(8,128)(2,1)}, bf16[197,768]{1,0:T(8,128)(2,1)S(1)}, u32[]{:S(2)}) copy-start(bf16[197,768]{1,0:T(8,128)(2,1)S(1)} %add_convert_fusion) | copy-start | bytes 907780
  202.1 16.2 %copy-start.48 = (s32[197,2]{0,1:T(2,128)S(1)}, s32[197,2]{0,1:T(2,128)}, u32[]{:S(2)}) copy-start(s32[197,2]{0,1:T(2,128)} %get-tuple-element.145) | copy-start | bytes 4732
  210.6 21.7 %all-to-all-start.2 = ((bf16[16,25,768]{2,1,0:T(8,128)(2,1)}), bf16[16,25,768]{2,1,0:T(8,128)(2,1)}, u32[]{:S(2)}, u32[]{:S(2)}) async-start(bf16[16,25,768]{2,1,0:T(8,128)(2,1)} %reshape.376), calls=%async_computation.2 | async-start | bytes 1572864 | tf_op jit(solution)/shard_map/all_to_all | solution.py:119
  232.3 45.5 %all-to-all-start.4 = ((bf16[16,25,768]{2,1,0:T(8,128)(2,1)}), bf16[16,25,768]{2,1,0:T(8,128)(2,1)}, u32[]{:S(2)}, u32[]{:S(2)}) async-start(bf16[16,25,768]{2,1,0:T(8,128)(2,1)} %reshape.380), calls=%async_computation.4 | async-start | bytes 1572864 | tf_op jit(solution)/shard_map/all_to_all | solution.py:196
  277.7 23.2 %all-to-all-start.3 = ((bf16[16,25,768]{2,1,0:T(8,128)(2,1)}), bf16[16,25,768]{2,1,0:T(8,128)(2,1)}, u32[]{:S(2)}, u32[]{:S(2)}) async-start(bf16[16,25,768]{2,1,0:T(8,128)(2,1)} %reshape.378), calls=%async_computation.3 | async-start | bytes 1572864 | tf_op jit(solution)/shard_map/all_to_all | solution.py:135
  300.9 22.0 %all-to-all-start.5 = ((bf16[16,25,768]{2,1,0:T(8,128)(2,1)}), bf16[16,25,768]{2,1,0:T(8,128)(2,1)}, u32[]{:S(2)}, u32[]{:S(2)}) async-start(bf16[16,25,768]{2,1,0:T(8,128)(2,1)} %reshape.382), calls=%async_computation.5 | async-start | bytes 1572864 | tf_op jit(solution)/shard_map/all_to_all | solution.py:218
  320.3 12.3 %copy-start.32 = (bf16[197,16]{0,1:T(8,128)(2,1)}, bf16[197,16]{0,1:T(8,128)(2,1)S(1)}, u32[]{:S(2)}) copy-start(bf16[197,16]{0,1:T(8,128)(2,1)S(1)} %multiply_convert_fusion.9) | copy-start | bytes 18916
  369.5 18.5 %all-to-all-start.6 = ((bf16[16,25,768]{2,1,0:T(8,128)(2,1)}), bf16[16,25,768]{2,1,0:T(8,128)(2,1)}, u32[]{:S(2)}, u32[]{:S(2)}) async-start(bf16[16,25,768]{2,1,0:T(8,128)(2,1)} %reshape.388), calls=%async_computation.6 | async-start | bytes 1572864 | tf_op jit(solution)/shard_map/all_to_all | solution.py:196
  374.2 107.6 %reduce-scatter.25.cloned.1.call-start = ((), (), s32[]{:S(2)}) async-start(), calls=%async_computation.21 | async-start | bytes 1327104 | tf_op jit(solution)/shard_map/reduce_scatter | solution.py:279
  404.2 18.5 %copy-start.53 = (s32[1024]{0:T(1024)S(1)}, s32[1024]{0:T(1024)}, u32[]{:S(2)}) copy-start(s32[1024]{0:T(1024)} %copy-done.52) | copy-start | bytes 12292
  404.2 17.2 %all-to-all-start.7 = ((bf16[16,25,768]{2,1,0:T(8,128)(2,1)}), bf16[16,25,768]{2,1,0:T(8,128)(2,1)}, u32[]{:S(2)}, u32[]{:S(2)}) async-start(bf16[16,25,768]{2,1,0:T(8,128)(2,1)} %reshape.390), calls=%async_computation.7 | async-start | bytes 1572864 | tf_op jit(solution)/shard_map/all_to_all | solution.py:218
  408.6 73.3 %reduce-scatter.23.cloned.1.call-start = ((), (), s32[]{:S(2)}) async-start(), calls=%async_computation.20 | async-start | bytes 1327104 | tf_op jit(solution)/shard_map/reduce_scatter | solution.py:279
  433.5 64.7 %reduce-scatter.21.cloned.1.call-start = ((), (), s32[]{:S(2)}) async-start(), calls=%async_computation.19 | async-start | bytes 3981312 | tf_op jit(solution)/shard_map/reduce_scatter | solution.py:276
  437.7 98.3 %reduce-scatter.19.cloned.1.call-start = ((), (), s32[]{:S(2)}) async-start(), calls=%async_computation.18 | async-start | bytes 3981312 | tf_op jit(solution)/shard_map/reduce_scatter | solution.py:276
  451.0 10.9 %copy-start.70 = (f32[197]{0:T(256)S(1)}, f32[197]{0:T(256)}, u32[]{:S(2)}) copy-start(f32[197]{0:T(256)} %copy-done.69) | copy-start | bytes 2368
  466.0 102.7 %reduce-scatter.33.cloned.1.call-start = ((), (), s32[]{:S(2)}) async-start(), calls=%async_computation.33 | async-start | bytes 221184
  468.0 132.4 %reduce-scatter.31.cloned.1.call-start = ((), (), s32[]{:S(2)}) async-start(), calls=%async_computation.32 | async-start | bytes 221184
  469.0 239.0 %reduce-scatter.37.cloned.1.call-start = ((), (), s32[]{:S(2)}) async-start(), calls=%async_computation.35 | async-start | bytes 5308416
  481.8 54.4 %copy-start.25 = (bf16[400,768]{1,0:T(8,128)(2,1)S(1)}, bf16[400,768]{1,0:T(8,128)(2,1)}, u32[]{:S(2)}) copy-start(bf16[400,768]{1,0:T(8,128)(2,1)} %copy-done.24) | copy-start | bytes 1843204
  481.8 251.9 %all-reduce.24.cloned.1.call-start = ((), (), s32[]{:S(2)}) async-start(), calls=%async_computation.36 | async-start | bytes 2359296 | tf_op jit(solution)/shard_map/psum | solution.py:295
  536.1 234.7 %reduce-scatter.35.cloned.1.call-start = ((), (), s32[]{:S(2)}) async-start(), calls=%async_computation.34 | async-start | bytes 5308416
  549.0 262.3 %reduce-scatter.29.cloned.1.call-start = ((), (), s32[]{:S(2)}) async-start(), calls=%async_computation.23 | async-start | bytes 5308416 | tf_op jit(solution)/shard_map/reduce_scatter | solution.py:214
  556.7 295.3 %reduce-scatter.27.cloned.1.call-start = ((), (), s32[]{:S(2)}) async-start(), calls=%async_computation.22 | async-start | bytes 5308416 | tf_op jit(solution)/shard_map/reduce_scatter | solution.py:214
  564.2 36.9 %copy-start.87 = (bf16[12,64,197]{2,1,0:T(8,128)(2,1)S(1)}, bf16[12,64,197]{2,1,0:T(8,128)(2,1)}, u32[]{:S(2)}) copy-start(bf16[12,64,197]{2,1,0:T(8,128)(2,1)} %fusion.82) | copy-start | bytes 907780
  (72 other events, 338.1 us)
Sparse Core Ops, SparseCore 0:
  10.3 30.1 all-gather.26
  42.7 23.3 all-gather.28
  68.4 35.7 all-gather.30
  106.2 34.3 all-gather.32
  142.1 31.2 all-gather.34
  175.0 23.5 all-gather.36
  200.8 34.0 all-gather.38
  237.1 34.3 all-gather.40
  378.0 30.9 reduce-scatter.24
  433.7 27.0 reduce-scatter.22
  463.2 35.0 reduce-scatter.20
  500.7 35.3 reduce-scatter.18
  539.0 29.6 reduce-scatter.32
  571.1 29.2 reduce-scatter.30
  602.6 37.1 reduce-scatter.36
  643.4 90.2 all-reduce.23
  736.0 34.7 reduce-scatter.34
  773.0 38.2 reduce-scatter.28
  813.7 38.2 reduce-scatter.26
where the time goes:
time: 879 us; the launch traced here: 863 us
  waiting for transfers between devices  334 us (38%)
  matrix products  159 us (18%)
  blocking collectives  148 us (17%)
  local copies, waits for them, and re-layouts  113 us (13%)
  starting transfers between devices  50.2 us (6%)
  other arithmetic  41.4 us (5%)
  between operations  17.4 us (2%)
    dot_general x30, matrix products, matmul(): return jnp.dot(left, right, preferred_element_type=jnp.float32)  105 us
    reduce_scatter x2, waiting for transfers between devices, per_device(): lax.psum_scatter(output_whole.astype(jnp.bfloat16), 'wshard', scatter_dim...  79.8 us
    psum x1, blocking collectives, per_device(): lax.psum(shares[0].astype(jnp.bfloat16), 'expert').astype(jnp.float32)  74.8 us
    unnamed x23, waiting for transfers between devices  68.3 us
    all_gather x2, waiting for transfers between devices, per_device(): lax.all_gather(output_weight[layer, 0], 'wshard', axis=0, tiled=True)  56.5 us
    reduce_scatter x2, waiting for transfers between devices, per_device(): lax.psum_scatter(qkv_grad_weight.astype(jnp.bfloat16), 'wshard', scatter_...  54.2 us
    unnamed x2, blocking collectives  45.9 us
    unnamed x220, local copies, waits for them, and re-layouts  35.7 us
  transfers between devices with their start and end apart: 27, of which 17 were waited for; matrix products, arithmetic and copies ran while one was open for 29% of the time, Pallas kernels for 0%

commit v1 on v0

v1 whole, which is shorter than its diff:
```python
import math

import jax
import jax.numpy as jnp
from jax import lax
from jax.experimental import pallas as pl
from jax.experimental.pallas import tpu as pltpu
from jax.sharding import PartitionSpec as P

HEADS = 12
SLOTS = 32
BLOCKS = 8
MISC = 128

EPSILON = 1e-06
ROOT_HALF = 0.7071067811865476
INV_ROOT_TAU = 0.3989422804014327


def standardize(rows):
    center = jnp.mean(rows, axis=-1, keepdims=True)
    shifted = rows - center
    variance = jnp.mean(shifted * shifted, axis=-1, keepdims=True)
    inverse = lax.rsqrt(variance + EPSILON)
    return (shifted * inverse, inverse)


def norm_backward(grad_in, normed, inverse, gain):
    scaled = grad_in * gain.astype(jnp.float32)
    first = jnp.mean(scaled, axis=-1, keepdims=True)
    second = jnp.mean(scaled * normed, axis=-1, keepdims=True)
    return inverse * (scaled - first - normed * second)


def matmul(left, right):
    return jnp.dot(left, right, preferred_element_type=jnp.float32)


def dot_nt(left, right):
    return lax.dot_general(
        left, right, (((1,), (1,)), ((), ())), preferred_element_type=jnp.float32
    )


def dot_tn(left, right):
    return lax.dot_general(
        left, right, (((0,), (0,)), ((), ())), preferred_element_type=jnp.float32
    )


def ffn_forward_kernel(rows_ref, weight_ref, pre_ref, out_ref, total):
    step = pl.program_id(0)
    width = rows_ref.shape[1]
    pre = dot_nt(rows_ref[...], weight_ref[:, :width])
    pre_ref[...] = pre
    act = (0.5 * pre * (1.0 + lax.erf(pre * ROOT_HALF))).astype(jnp.bfloat16)
    part = matmul(act, weight_ref[:, width:])

    @pl.when(step == 0)
    def _():
        total[...] = part

    @pl.when(step > 0)
    def _():
        total[...] += part

    @pl.when(step == pl.num_programs(0) - 1)
    def _():
        out_ref[...] = total[...].astype(out_ref.dtype)


def ffn_forward(rows, weight):
    count, width = rows.shape
    hidden = weight.shape[0]
    block = hidden // BLOCKS
    return pl.pallas_call(
        ffn_forward_kernel,
        grid=(BLOCKS,),
        in_specs=[
            pl.BlockSpec((count, width), lambda j: (0, 0)),
            pl.BlockSpec((block, 2 * width), lambda j: (j, 0)),
        ],
        out_specs=[
            pl.BlockSpec((count, block), lambda j: (0, j)),
            pl.BlockSpec((count, width), lambda j: (0, 0)),
        ],
        out_shape=[
            jax.ShapeDtypeStruct((count, hidden), jnp.float32),
            jax.ShapeDtypeStruct((count, width), jnp.bfloat16),
        ],
        scratch_shapes=[pltpu.VMEM((count, width), jnp.float32)],
        name="ffn_forward",
    )(rows, weight)


def ffn_backward_kernel(rows_ref, grads_ref, pre_ref, weight_ref, weight_grad_ref, out_ref, total):
    step = pl.program_id(0)
    width = rows_ref.shape[1]
    pre = pre_ref[...]
    phi = 0.5 * (1.0 + lax.erf(pre * ROOT_HALF))
    act = (pre * phi).astype(jnp.bfloat16)
    grads = grads_ref[...]
    act_grad = dot_nt(grads, weight_ref[:, width:])
    slope = phi + pre * jnp.exp(-0.5 * pre * pre) * INV_ROOT_TAU
    pre_grad = (act_grad * slope).astype(jnp.bfloat16)
    weight_grad_ref[:, :width] = dot_tn(pre_grad, rows_ref[...]).astype(jnp.bfloat16)
    weight_grad_ref[:, width:] = dot_tn(act, grads).astype(jnp.bfloat16)
    part = matmul(pre_grad, weight_ref[:, :width])

    @pl.when(step == 0)
    def _():
        total[...] = part

    @pl.when(step > 0)
    def _():
        total[...] += part

    @pl.when(step == pl.num_programs(0) - 1)
    def _():
        out_ref[...] = total[...].astype(out_ref.dtype)


def ffn_backward(rows, grads, pre, weight):
    count, width = rows.shape
    hidden = weight.shape[0]
    block = hidden // BLOCKS
    return pl.pallas_call(
        ffn_backward_kernel,
        grid=(BLOCKS,),
        in_specs=[
            pl.BlockSpec((count, width), lambda j: (0, 0)),
            pl.BlockSpec((count, width), lambda j: (0, 0)),
            pl.BlockSpec((count, block), lambda j: (0, j)),
            pl.BlockSpec((block, 2 * width), lambda j: (j, 0)),
        ],
        out_specs=[
            pl.BlockSpec((block, 2 * width), lambda j: (j, 0)),
            pl.BlockSpec((count, width), lambda j: (0, 0)),
        ],
        out_shape=[
            jax.ShapeDtypeStruct((hidden, 2 * width), jnp.bfloat16),
            jax.ShapeDtypeStruct((count, width), jnp.bfloat16),
        ],
        scratch_shapes=[pltpu.VMEM((count, width), jnp.float32)],
        name="ffn_backward",
    )(rows, grads, pre, weight)


def exchange(rows, experts):
    count, width = rows.shape
    moved = lax.all_to_all(
        rows.reshape(experts, count // experts, width),
        "expert",
        split_axis=0,
        concat_axis=0,
        tiled=True,
    )
    return moved.reshape(count, width)


def sum_over_experts(share, experts):
    count, width = share.shape
    parts = lax.all_to_all(
        share.reshape(experts, count // experts, width),
        "expert",
        split_axis=0,
        concat_axis=0,
        tiled=True,
    )
    total = jnp.sum(parts.astype(jnp.float32), axis=0).astype(jnp.bfloat16)
    spread = lax.all_to_all(
        jnp.broadcast_to(total[None], parts.shape),
        "expert",
        split_axis=0,
        concat_axis=0,
        tiled=True,
    )
    return spread.reshape(count, width).astype(jnp.float32)


def routing(chosen, experts):
    length = chosen.shape[0]
    masks = (chosen.T[:, :, None] == jnp.arange(experts, dtype=jnp.int32)).astype(jnp.bfloat16)
    named = masks[0] + masks[1]
    earlier = jnp.tril(jnp.ones((length, length), jnp.bfloat16), -1)
    before = matmul(earlier, named)
    slots = jnp.sum(before[None] * masks.astype(jnp.float32), axis=-1).astype(jnp.int32)
    position = chosen.T * SLOTS + slots
    return (position[:, :, None] == jnp.arange(experts * SLOTS, dtype=jnp.int32)).astype(
        jnp.bfloat16
    )


def unpack_attn(packed, width, experts):
    base = 4 * width
    vectors = packed[:, base + experts : base + experts + 4].T
    return (
        vectors[0],
        vectors[1],
        packed[:, : 3 * width],
        packed[:, 3 * width : base],
        vectors[2],
        vectors[3],
        packed[:, base : base + experts],
    )


def per_device(
    inputs,
    routes,
    first_gain,
    first_bias,
    qkv_weight,
    proj_weight,
    second_gain,
    second_bias,
    router_weight,
    hidden_weight,
    output_weight,
    cotangent,
):
    experts = lax.axis_size("expert")
    state = inputs[0]
    length, width = state.shape
    head_size = width // HEADS
    scale = 1.0 / math.sqrt(head_size)
    attn_pack = [
        jnp.concatenate(
            [
                qkv_weight[layer],
                proj_weight[layer],
                router_weight[layer],
                first_gain[layer][:, None],
                first_bias[layer][:, None],
                second_gain[layer][:, None],
                second_bias[layer][:, None],
                jnp.zeros((qkv_weight.shape[1], MISC - experts - 4), jnp.bfloat16),
            ],
            axis=1,
        )
        for layer in range(routes.shape[0])
    ]
    expert_pack = [
        jnp.concatenate([hidden_weight[layer, 0].T, output_weight[layer, 0]], axis=1)
        for layer in range(routes.shape[0])
    ]
    depth = routes.shape[0]
    expert_ids = jnp.arange(experts, dtype=jnp.int32)
    saved = []
    for layer in range(depth):
        attn_full = lax.all_gather(attn_pack[layer], "wshard", axis=0, tiled=True)
        gathered = unpack_attn(attn_full, width, experts)
        gain_one, bias_one, qkv_full, proj_full, gain_two, bias_two, router_full = gathered
        normed_one, inverse_one = standardize(state)
        attn_in = (normed_one * gain_one.astype(jnp.float32) + bias_one.astype(jnp.float32)).astype(
            jnp.bfloat16
        )
        qkv = matmul(attn_in, qkv_full).astype(jnp.bfloat16)
        query = qkv[:, :width].reshape(length, HEADS, head_size)
        keys = qkv[:, width : 2 * width].reshape(length, HEADS, head_size)
        values = qkv[:, 2 * width :].reshape(length, HEADS, head_size)
        scores = jnp.einsum("shd,thd->hst", query, keys, preferred_element_type=jnp.float32) * scale
        log_total = jnp.log(jnp.sum(jnp.exp(scores), axis=-1, keepdims=True))
        probs_low = jnp.exp(scores - log_total).astype(jnp.bfloat16)
        mixed = jnp.einsum("hst,thd->shd", probs_low, values, preferred_element_type=jnp.float32)
        mixed = mixed.reshape(length, width).astype(jnp.bfloat16)
        middle = state + matmul(mixed, proj_full)
        normed_two, inverse_two = standardize(middle)
        moe_in = (normed_two * gain_two.astype(jnp.float32) + bias_two.astype(jnp.float32)).astype(
            jnp.bfloat16
        )
        logits = matmul(moe_in, router_full)
        raised = jnp.exp(logits)
        router_probs = raised / jnp.sum(raised, axis=-1, keepdims=True)
        chosen = routes[layer, 0]
        choice_mask = (chosen[..., None] == expert_ids).astype(jnp.float32)
        gates = jnp.sum(choice_mask * router_probs[:, None, :], axis=-1)
        select = routing(chosen, experts)
        select_any = select[0] + select[1]
        sent = dot_tn(select_any, moe_in).astype(jnp.bfloat16)
        received = exchange(sent, experts)
        expert_full = lax.all_gather(expert_pack[layer], "wshard", axis=0, tiled=True)
        pre, result = ffn_forward(received, expert_full)
        kept = (received, pre, expert_full)
        returned = exchange(result, experts)
        picked = [matmul(select[k], returned) for k in range(2)]
        state = middle + gates[:, :1] * picked[0] + gates[:, 1:] * picked[1]
        picked = [entry.astype(jnp.bfloat16) for entry in picked]
        saved.append(
            (
                gathered,
                normed_one,
                inverse_one,
                attn_in,
                query,
                keys,
                values,
                log_total,
                mixed,
                normed_two,
                inverse_two,
                moe_in,
                router_probs,
                choice_mask,
                gates,
                select,
                picked,
                kept,
            )
        )
    grad = cotangent[0]
    layer_parts = []
    expert_parts = []
    for layer in reversed(range(depth)):
        (
            gathered,
            normed_one,
            inverse_one,
            attn_in,
            query,
            keys,
            values,
            log_total,
            mixed,
            normed_two,
            inverse_two,
            moe_in,
            router_probs,
            choice_mask,
            gates,
            select,
            picked,
            kept,
        ) = saved[layer]
        gain_one, bias_one, qkv_full, proj_full, gain_two, bias_two, router_full = gathered
        gate_grad = jnp.stack(
            [jnp.sum(grad * picked[k].astype(jnp.float32), axis=-1) for k in range(2)], axis=-1
        )
        routed_grad = [(gates[:, k : k + 1] * grad).astype(jnp.bfloat16) for k in range(2)]
        grad_sent = dot_tn(
            jnp.concatenate([select[0], select[1]], axis=0), jnp.concatenate(routed_grad, axis=0)
        ).astype(jnp.bfloat16)
        grad_received = exchange(grad_sent, experts)
        rows_kept, pre, expert_full = kept
        expert_grad, row_grad = ffn_backward(rows_kept, grad_received, pre, expert_full)
        expert_part = lax.psum_scatter(expert_grad, "wshard", scatter_dimension=0, tiled=True)
        back = matmul(select[0] + select[1], exchange(row_grad, experts))
        prob_grad = jnp.sum(choice_mask * gate_grad[..., None], axis=1)
        logit_grad = router_probs * (
            prob_grad - jnp.sum(router_probs * prob_grad, axis=-1, keepdims=True)
        )
        logit_grad = logit_grad.astype(jnp.bfloat16)
        router_grad = matmul(moe_in.T, logit_grad)
        moe_in_grad = back + matmul(logit_grad, router_full.T)
        second_gain_grad = jnp.sum(moe_in_grad * normed_two, axis=0)
        second_bias_grad = jnp.sum(moe_in_grad, axis=0)
        middle_grad = grad + norm_backward(moe_in_grad, normed_two, inverse_two, gain_two)
        middle_low = middle_grad.astype(jnp.bfloat16)
        proj_grad = matmul(mixed.T, middle_low)
        mixed_grad = (
            matmul(middle_low, proj_full.T).astype(jnp.bfloat16).reshape(length, HEADS, head_size)
        )
        scores = jnp.einsum("shd,thd->hst", query, keys, preferred_element_type=jnp.float32) * scale
        probs = jnp.exp(scores - log_total)
        probs_low = probs.astype(jnp.bfloat16)
        values_grad = jnp.einsum(
            "hst,shd->thd", probs_low, mixed_grad, preferred_element_type=jnp.float32
        )
        prob_grad_att = jnp.einsum(
            "shd,thd->hst", mixed_grad, values, preferred_element_type=jnp.float32
        )
        score_grad = probs * (
            prob_grad_att - jnp.sum(probs * prob_grad_att, axis=-1, keepdims=True)
        )
        score_low = (score_grad * scale).astype(jnp.bfloat16)
        query_grad = jnp.einsum("hst,thd->shd", score_low, keys, preferred_element_type=jnp.float32)
        keys_grad = jnp.einsum("hst,shd->thd", score_low, query, preferred_element_type=jnp.float32)
        qkv_grad = jnp.concatenate(
            [
                query_grad.reshape(length, width),
                keys_grad.reshape(length, width),
                values_grad.reshape(length, width),
            ],
            axis=-1,
        ).astype(jnp.bfloat16)
        qkv_grad_weight = matmul(attn_in.T, qkv_grad)
        attn_in_grad = matmul(qkv_grad, qkv_full.T)
        first_gain_grad = jnp.sum(attn_in_grad * normed_one, axis=0)
        first_bias_grad = jnp.sum(attn_in_grad, axis=0)
        grad = middle_grad + norm_backward(attn_in_grad, normed_one, inverse_one, gain_one)
        vectors = jnp.stack(
            [first_gain_grad, first_bias_grad, second_gain_grad, second_bias_grad], axis=1
        )
        attn_grad = jnp.concatenate(
            [
                qkv_grad_weight.astype(jnp.bfloat16),
                proj_grad.astype(jnp.bfloat16),
                router_grad.astype(jnp.bfloat16),
                vectors.astype(jnp.bfloat16),
                jnp.zeros((width, MISC - experts - 4), jnp.bfloat16),
            ],
            axis=1,
        )
        share = lax.psum_scatter(attn_grad, "wshard", scatter_dimension=0, tiled=True)
        layer_parts.append(unpack_attn(sum_over_experts(share, experts), width, experts))
        expert_parts.append(
            (
                expert_part[:, :width].T.astype(jnp.float32),
                expert_part[:, width:].astype(jnp.float32),
            )
        )
    layer_parts = list(reversed(layer_parts))
    expert_parts = list(reversed(expert_parts))
    stacked = [jnp.stack([entry[index] for entry in layer_parts]) for index in range(7)]
    hidden_grads = jnp.stack([entry[0] for entry in expert_parts])[:, None]
    output_grads = jnp.stack([entry[1] for entry in expert_parts])[:, None]
    return (
        state[None],
        grad[None],
        stacked[0],
        stacked[1],
        stacked[2],
        stacked[3],
        stacked[4],
        stacked[5],
        stacked[6],
        hidden_grads,
        output_grads,
    )


def solution(mesh):
    in_specs = (
        P(("expert", "wshard"), None, None),
        P(None, ("expert", "wshard"), None, None),
        P(None, "wshard"),
        P(None, "wshard"),
        P(None, "wshard", None),
        P(None, "wshard", None),
        P(None, "wshard"),
        P(None, "wshard"),
        P(None, "wshard", None),
        P(None, "expert", None, "wshard"),
        P(None, "expert", "wshard", None),
        P(("expert", "wshard"), None, None),
    )
    out_specs = (
        P(("expert", "wshard"), None, None),
        P(("expert", "wshard"), None, None),
        P(None, "wshard"),
        P(None, "wshard"),
        P(None, "wshard", None),
        P(None, "wshard", None),
        P(None, "wshard"),
        P(None, "wshard"),
        P(None, "wshard", None),
        P(None, "expert", None, "wshard"),
        P(None, "expert", "wshard", None),
    )
    return jax.shard_map(
        per_device, mesh=mesh, in_specs=in_specs, out_specs=out_specs, check_vma=False
    )
```

time: 879 us -> 620 us (0.71)
  the two profiles are of different devices: /device:TPU:24 before, /device:TPU:1 now
where the time goes in v1:
time: 620 us; the launch traced here: 610 us
  waiting for transfers between devices  264 us (43%)
  matrix products  104 us (17%)
  Pallas kernels  66.8 us (11%)
  local copies, waits for them, and re-layouts  62.7 us (10%)
  starting transfers between devices  58.2 us (9%)
  other arithmetic  21.7 us (4%)
  blocking collectives  16.3 us (3%)
  between operations  15.5 us (2%)
    reduce_scatter x2, waiting for transfers between devices, per_device(): lax.psum_scatter(expert_grad, 'wshard', scatter_dimension=0, tiled=True)  78.1 us
    all_gather x2, waiting for transfers between devices, per_device(): lax.all_gather(expert_pack[layer], 'wshard', axis=0, tiled=True)  48.9 us
    all_to_all x7, waiting for transfers between devices, exchange(): lax.all_to_all(rows.reshape(experts, count // experts, width), 'expert',...  46.9 us
    dot_general x26, matrix products, matmul(): return jnp.dot(left, right, preferred_element_type=jnp.float32)  46.8 us
    all_gather x2, waiting for transfers between devices, per_device(): attn_full = lax.all_gather(attn_pack[layer], 'wshard', axis=0, tiled=True)  46 us
    all_to_all x7, starting transfers between devices, exchange(): lax.all_to_all(rows.reshape(experts, count // experts, width), 'expert',...  39.6 us
    pallas_call x2, Pallas kernels, ffn_backward(): pl.pallas_call(ffn_backward_kernel, grid=(BLOCKS,), in_specs=[pl.BlockSpe...  38.9 us
    pallas_call x2, Pallas kernels, ffn_forward(): pl.pallas_call(ffn_forward_kernel, grid=(BLOCKS,), in_specs=[pl.BlockSpec...  27.9 us
  transfers between devices with their start and end apart: 19, of which 16 were waited for; matrix products, arithmetic and copies ran while one was open for 20% of the time, Pallas kernels for 5%

profile of v1, /device:TPU:1, one launch (start us, length us, event | category | flops | bytes accessed | tf_op | source)
XLA Modules:
  0.0 609.6 jit_solution(7754363744700597469)
XLA Ops:
  22.8 30.1 %all-gather.5.cloned.1.call-done = bf16[768,3200]{1,0:T(8,128)(2,1)} async-done(((bf16[96,3200]{1,0:T(8,128)(2,1)}), bf16[768,3200]{1,0:T(8,128)(2,1)}) %all-gather.5.cloned.1.call-update) | async-done | bytes 4915216 | tf_op jit(solution)/shard_map/all_gather | solution.py:251
  60.0 3.4 convolution_convert_fusion.13
  67.3 6.7 %all-to-all-start = ((bf16[16,32,768]{2,1,0:T(8,128)(2,1)}), bf16[16,32,768]{2,1,0:T(8,128)(2,1)S(1)}, u32[]{:S(2)}, u32[]{:S(2)}) async-start(bf16[16,32,768]{2,1,0:T(8,128)(2,1)} %bitcast.21), calls=%async_computation | async-start | bytes 1572864 | tf_op jit(solution)/shard_map/all_to_all | solution.py:151
  76.1 11.4 %all-to-all-done = bf16[16,32,768]{2,1,0:T(8,128)(2,1)S(1)} async-done(((bf16[16,32,768]{2,1,0:T(8,128)(2,1)}), bf16[16,32,768]{2,1,0:T(8,128)(2,1)S(1)}, u32[]{:S(2)}, u32[]{:S(2)}) %all-to-all-start) | async-done | bytes 786464 | tf_op jit(solution)/shard_map/all_to_all | solution.py:151
  87.6 21.7 %all-gather.7.cloned.1.call-done.weight_ref = bf16[3072,1536]{1,0:T(8,128)(2,1)} async-done(((bf16[384,1536]{1,0:T(8,128)(2,1)}), bf16[3072,1536]{1,0:T(8,128)(2,1)}) %all-gather.7.cloned.1.call-update) | async-done | bytes 9437200 | tf_op jit(solution)/shard_map/all_gather | solution.py:282
  109.3 14.0 %ffn_forward.2 = (f32[512,3072]{1,0:T(8,128)}, bf16[512,768]{1,0:T(8,128)(2,1)}) custom-call(bf16[512,768]{1,0:T(8,128)(2,1)} %bitcast.282, bf16[3072,1536]{1,0:T(8,128)(2,1)} %all-gather.7.cloned.1.call-done.weight_ref), custom_call_target="tpu_custom_call" | custom-call | tf_op jit(solution)/shard_map/ffn_forward/pallas_call | solution.py:76
  123.3 7.1 %all-to-all-start.1 = ((bf16[16,32,768]{2,1,0:T(8,128)(2,1)}), bf16[16,32,768]{2,1,0:T(8,128)(2,1)S(1)}, u32[]{:S(2)}, u32[]{:S(2)}) async-start(bf16[16,32,768]{2,1,0:T(8,128)(2,1)} %bitcast.316), calls=%async_computation.1 | async-start | bytes 1572864 | tf_op jit(solution)/shard_map/all_to_all | solution.py:151
  130.4 15.9 %all-gather.9.cloned.1.call-done = bf16[768,3200]{1,0:T(8,128)(2,1)} async-done(((bf16[96,3200]{1,0:T(8,128)(2,1)}), bf16[768,3200]{1,0:T(8,128)(2,1)}) %all-gather.9.cloned.1.call-update) | async-done | bytes 4915216 | tf_op jit(solution)/shard_map/all_gather | solution.py:251
  160.6 4.4 convolution_convert_fusion.12
  168.7 6.8 %all-to-all-start.2 = ((bf16[16,32,768]{2,1,0:T(8,128)(2,1)}), bf16[16,32,768]{2,1,0:T(8,128)(2,1)}, u32[]{:S(2)}, u32[]{:S(2)}) async-start(bf16[16,32,768]{2,1,0:T(8,128)(2,1)} %bitcast.288), calls=%async_computation.2 | async-start | bytes 1572864 | tf_op jit(solution)/shard_map/all_to_all | solution.py:151
  175.5 27.2 %all-gather.11.cloned.1.call-done.weight_ref = bf16[3072,1536]{1,0:T(8,128)(2,1)} async-done(((bf16[384,1536]{1,0:T(8,128)(2,1)}), bf16[3072,1536]{1,0:T(8,128)(2,1)}) %all-gather.11.cloned.1.call-update) | async-done | bytes 9437200 | tf_op jit(solution)/shard_map/all_gather | solution.py:282
  202.7 13.9 %ffn_forward.3 = (f32[512,3072]{1,0:T(8,128)}, bf16[512,768]{1,0:T(8,128)(2,1)}) custom-call(bf16[512,768]{1,0:T(8,128)(2,1)} %bitcast.52.rows_ref, bf16[3072,1536]{1,0:T(8,128)(2,1)} %all-gather.11.cloned.1.call-done.weight_ref), custom_call_target="tpu_custom_call" | custom-call | tf_op jit(solution)/shard_map/ffn_forward/pallas_call | solution.py:76
  216.6 6.7 %all-to-all-start.3 = ((bf16[16,32,768]{2,1,0:T(8,128)(2,1)}), bf16[16,32,768]{2,1,0:T(8,128)(2,1)}, u32[]{:S(2)}, u32[]{:S(2)}) async-start(bf16[16,32,768]{2,1,0:T(8,128)(2,1)} %bitcast.318), calls=%async_computation.3 | async-start | bytes 1572864 | tf_op jit(solution)/shard_map/all_to_all | solution.py:151
  226.4 10.7 %all-to-all-done.3 = bf16[16,32,768]{2,1,0:T(8,128)(2,1)} async-done(((bf16[16,32,768]{2,1,0:T(8,128)(2,1)}), bf16[16,32,768]{2,1,0:T(8,128)(2,1)}, u32[]{:S(2)}, u32[]{:S(2)}) %all-to-all-start.3) | async-done | bytes 786464 | tf_op jit(solution)/shard_map/all_to_all | solution.py:151
  243.3 16.3 %all_to_all.60 = bf16[16,32,768]{2,1,0:T(8,128)(2,1)} all-to-all(bf16[16,32,768]{2,1,0:T(8,128)(2,1)S(1)} %bitcast.320), channel_id=1, replica_groups=mesh['expert'=16,'wshard'=8] {'expert'}, dimensions={0} | all-to-all | bytes 1572864 | tf_op jit(solution)/shard_map/all_to_all | solution.py:151
  259.6 19.4 %ffn_backward.2 = (bf16[3072,1536]{1,0:T(8,128)(2,1)}, bf16[512,768]{1,0:T(8,128)(2,1)}) custom-call(bf16[512,768]{1,0:T(8,128)(2,1)} %bitcast.52.rows_ref, bf16[512,768]{1,0:T(8,128)(2,1)} %bitcast.287, f32[512,3072]{1,0:T(8,128)} %get-tuple-element.21.pre_ref, bf16[3072,1536]{1,0:T(8,128)(2,1)} %all-gather.11.cloned.1.call-done.weight_ref), custom_call_target="tpu_custom_call" | custom-call | tf_op jit(solution)/shard_map/ffn_backward/pallas_call | solution.py:127
  279.0 4.3 all-to-all-start.5
  283.9 3.9 fusion.10
  288.8 6.4 %all-to-all-done.5 = bf16[16,32,768]{2,1,0:T(8,128)(2,1)} async-done(((bf16[16,32,768]{2,1,0:T(8,128)(2,1)}), bf16[16,32,768]{2,1,0:T(8,128)(2,1)}, u32[]{:S(2)}, u32[]{:S(2)}) %all-to-all-start.5) | async-done | bytes 786464 | tf_op jit(solution)/shard_map/all_to_all | solution.py:151
  303.7 3.1 fusion.196
  306.8 5.5 fusion.44
  312.2 5.4 fusion.47
  317.6 4.3 convolution_convert_fusion.11
  323.4 4.4 convolution_convert_fusion
  327.9 4.3 multiply_reduce_fusion.3
  334.9 8.6 %concatenate.51 = bf16[768,3200]{1,0:T(8,128)(2,1)} concatenate(bf16[768,2304]{1,0:T(8,128)(2,1)} %convolution_convert_fusion, bf16[768,768]{1,0:T(8,128)(2,1)} %convolution_convert_fusion.4, bf16[768,16]{1,0:T(8,128)(2,1)S(1)} %copy-done.36, bf16[768,1]{1,0:T(8,128)(2,1)S(1)} %stack.154, bf16[768,1]{1,0:T(8,128)(2,1)} %stack.155, bf16[768,1]{1,0:T(8,128)(2,1)} %stack.156, ...), dimensions={1} | concatenate | bytes 9830400 | tf_op jit(solution)/shard_map/concatenate | solution.py:394
  348.9 3.8 all-to-all-start.6
  355.3 8.4 %all-to-all-done.6 = bf16[16,32,768]{2,1,0:T(8,128)(2,1)S(1)} async-done(((bf16[16,32,768]{2,1,0:T(8,128)(2,1)}), bf16[16,32,768]{2,1,0:T(8,128)(2,1)S(1)}, u32[]{:S(2)}, u32[]{:S(2)}) %all-to-all-start.6) | async-done | bytes 786464 | tf_op jit(solution)/shard_map/all_to_all | solution.py:151
  364.6 19.5 %ffn_backward.3 = (bf16[3072,1536]{1,0:T(8,128)(2,1)}, bf16[512,768]{1,0:T(8,128)(2,1)}) custom-call(bf16[512,768]{1,0:T(8,128)(2,1)} %bitcast.283, bf16[512,768]{1,0:T(8,128)(2,1)} %bitcast.286, f32[512,3072]{1,0:T(8,128)} %get-tuple-element.23.pre_ref, bf16[3072,1536]{1,0:T(8,128)(2,1)} %all-gather.7.cloned.1.call-done.weight_ref), custom_call_target="tpu_custom_call" | custom-call | tf_op jit(solution)/shard_map/ffn_backward/pallas_call | solution.py:127
  384.1 4.3 all-to-all-start.7
  388.8 10.0 %all-to-all-done.7 = bf16[16,32,768]{2,1,0:T(8,128)(2,1)} async-done(((bf16[16,32,768]{2,1,0:T(8,128)(2,1)}), bf16[16,32,768]{2,1,0:T(8,128)(2,1)}, u32[]{:S(2)}, u32[]{:S(2)}) %all-to-all-start.7) | async-done | bytes 786464 | tf_op jit(solution)/shard_map/all_to_all | solution.py:151
  404.1 4.1 convolution_convert_fusion.10
  410.3 4.8 fusion.38
  415.1 4.9 fusion.41
  420.0 4.4 multiply_reduce_fusion.5
  426.3 3.1 convolution_convert_fusion.1
  429.4 8.2 %concatenate.50 = bf16[768,3200]{1,0:T(8,128)(2,1)} concatenate(bf16[768,2304]{1,0:T(8,128)(2,1)} %convolution_convert_fusion.1, bf16[768,768]{1,0:T(8,128)(2,1)S(1)} %convolution_convert_fusion.5, bf16[768,16]{1,0:T(8,128)(2,1)S(1)} %copy.277, bf16[768,1]{1,0:T(8,128)(2,1)S(1)} %stack.150, bf16[768,1]{1,0:T(8,128)(2,1)S(1)} %stack.151, bf16[768,1]{1,0:T(8,128)(2,1)S(1)} %stack.152, ...), dimensions={1} | concatenate | bytes 9830400 | tf_op jit(solution)/shard_map/concatenate | solution.py:394
  441.3 3.8 all-to-all-start.10
  446.6 9.3 %all-to-all-done.10 = bf16[16,6,3200]{2,1,0:T(8,128)(2,1)S(1)} async-done(((bf16[16,6,3200]{2,1,0:T(8,128)(2,1)}), bf16[16,6,3200]{2,1,0:T(8,128)(2,1)S(1)}, u32[]{:S(2)}, u32[]{:S(2)}) %all-to-all-start.10) | async-done | bytes 614432 | tf_op jit(solution)/shard_map/all_to_all | solution.py:163
  457.0 3.6 all-to-all-start.11
  463.4 7.8 %all-to-all-done.11 = bf16[16,6,3200]{2,1,0:T(8,128)(2,1)S(1)} async-done(((bf16[16,6,3200]{2,1,0:T(8,128)(2,1)}), bf16[16,6,3200]{2,1,0:T(8,128)(2,1)S(1)}, u32[]{:S(2)}, u32[]{:S(2)}) %all-to-all-start.11) | async-done | bytes 614432 | tf_op jit(solution)/shard_map/all_to_all | solution.py:171
  471.4 4.6 reduce-scatter.5.cloned.1.call-done
  478.0 6.6 %all-to-all-start.8 = ((bf16[16,6,3200]{2,1,0:T(8,128)(2,1)}), bf16[16,6,3200]{2,1,0:T(8,128)(2,1)S(1)}, u32[]{:S(2)}, u32[]{:S(2)}) async-start(bf16[16,6,3200]{2,1,0:T(8,128)(2,1)} %reshape.276), calls=%async_computation.9 | async-start | bytes 1638400 | tf_op jit(solution)/shard_map/all_to_all | solution.py:163
  485.3 10.5 %all-to-all-done.8 = bf16[16,6,3200]{2,1,0:T(8,128)(2,1)S(1)} async-done(((bf16[16,6,3200]{2,1,0:T(8,128)(2,1)}), bf16[16,6,3200]{2,1,0:T(8,128)(2,1)S(1)}, u32[]{:S(2)}, u32[]{:S(2)}) %all-to-all-start.8) | async-done | bytes 614432 | tf_op jit(solution)/shard_map/all_to_all | solution.py:163
  496.9 3.6 all-to-all-start.9
  500.6 10.8 %all-to-all-done.9 = bf16[16,6,3200]{2,1,0:T(8,128)(2,1)S(1)} async-done(((bf16[16,6,3200]{2,1,0:T(8,128)(2,1)}), bf16[16,6,3200]{2,1,0:T(8,128)(2,1)S(1)}, u32[]{:S(2)}, u32[]{:S(2)}) %all-to-all-start.9) | async-done | bytes 614432 | tf_op jit(solution)/shard_map/all_to_all | solution.py:171
  517.2 20.0 %reduce-scatter.11.cloned.1.call-done = bf16[384,1536]{1,0:T(8,128)(2,1)} async-done(((bf16[3072,1536]{1,0:T(8,128)(2,1)}), bf16[384,1536]{1,0:T(8,128)(2,1)}) %reduce-scatter.11.cloned.1.call-update) | async-done | bytes 1179664 | tf_op jit(solution)/shard_map/reduce_scatter | solution.py:346
  538.5 58.1 %reduce-scatter.9.cloned.1.call-done = bf16[384,1536]{1,0:T(8,128)(2,1)} async-done(((bf16[3072,1536]{1,0:T(8,128)(2,1)}), bf16[384,1536]{1,0:T(8,128)(2,1)}) %reduce-scatter.9.cloned.1.call-update) | async-done | bytes 1179664 | tf_op jit(solution)/shard_map/reduce_scatter | solution.py:346
  (302 shorter events, 114.0 us)
Async XLA Ops:
  7.2 4.9 copy-start.42
  7.2 5.1 copy-start.43
  7.2 6.8 %copy-start.34 = (bf16[2,1,768,384]{3,2,1,0:T(8,128)(2,1)S(1)}, bf16[2,1,768,384]{3,2,1,0:T(8,128)(2,1)}, u32[]{:S(2)}) copy-start(bf16[2,1,768,384]{3,2,1,0:T(8,128)(2,1)} %param.21) | copy-start | bytes 3538948
  7.2 45.7 %all-gather.5.cloned.1.call-start = ((), (), s32[]{:S(2)}) async-start(), calls=%async_computation.16 | async-start | bytes 5529600 | tf_op jit(solution)/shard_map/all_gather | solution.py:251
  13.9 95.4 %all-gather.7.cloned.1.call-start = ((), (), s32[]{:S(2)}) async-start(), calls=%async_computation.17 | async-start | bytes 10616832 | tf_op jit(solution)/shard_map/all_gather | solution.py:282
  16.9 129.5 %all-gather.9.cloned.1.call-start = ((), (), s32[]{:S(2)}) async-start(), calls=%async_computation.18 | async-start | bytes 5529600 | tf_op jit(solution)/shard_map/all_gather | solution.py:251
  18.6 184.1 %all-gather.11.cloned.1.call-start = ((), (), s32[]{:S(2)}) async-start(), calls=%async_computation.19 | async-start | bytes 10616832 | tf_op jit(solution)/shard_map/all_gather | solution.py:282
  22.8 43.2 %copy-start.10 = (bf16[2,197,512]{2,1,0:T(8,128)(2,1)}, bf16[2,197,512]{2,1,0:T(8,128)(2,1)S(1)}, u32[]{:S(2)}) copy-start(bf16[2,197,512]{2,1,0:T(8,128)(2,1)S(1)} %get-tuple-element.166) | copy-start | bytes 1210372
  57.6 5.8 copy-start.20
  57.8 5.6 copy-start.23
  58.0 5.4 copy-start.26
  67.3 20.3 %all-to-all-start = ((bf16[16,32,768]{2,1,0:T(8,128)(2,1)}), bf16[16,32,768]{2,1,0:T(8,128)(2,1)S(1)}, u32[]{:S(2)}, u32[]{:S(2)}) async-start(bf16[16,32,768]{2,1,0:T(8,128)(2,1)} %bitcast.21), calls=%async_computation | async-start | bytes 1572864 | tf_op jit(solution)/shard_map/all_to_all | solution.py:151
  87.6 21.7 %copy-start.1 = (bf16[16,32,768]{2,1,0:T(8,128)(2,1)}, bf16[16,32,768]{2,1,0:T(8,128)(2,1)S(1)}, u32[]{:S(2)}) copy-start(bf16[16,32,768]{2,1,0:T(8,128)(2,1)S(1)} %all-to-all-done) | copy-start | bytes 2359300
  123.3 24.6 %copy-start.35 = (pred[2,197,512]{2,1,0:T(8,128)(4,1)S(1)}, pred[2,197,512]{2,1,0:T(8,128)(4,1)}, u32[]{:S(2)}) copy-start(pred[2,197,512]{2,1,0:T(8,128)(4,1)} %get-tuple-element.165) | copy-start | bytes 605188
  123.3 24.6 %all-to-all-start.1 = ((bf16[16,32,768]{2,1,0:T(8,128)(2,1)}), bf16[16,32,768]{2,1,0:T(8,128)(2,1)S(1)}, u32[]{:S(2)}, u32[]{:S(2)}) async-start(bf16[16,32,768]{2,1,0:T(8,128)(2,1)} %bitcast.316), calls=%async_computation.1 | async-start | bytes 1572864 | tf_op jit(solution)/shard_map/all_to_all | solution.py:151
  148.3 4.8 copy-start.3
  155.2 9.8 %copy-start.28 = (bf16[197,768]{0,1:T(8,128)(2,1)}, bf16[197,768]{0,1:T(8,128)(2,1)S(1)}, u32[]{:S(2)}) copy-start(bf16[197,768]{0,1:T(8,128)(2,1)S(1)} %copy.264) | copy-start | bytes 907780
  156.5 8.5 %copy-start.30 = (bf16[197,768]{0,1:T(8,128)(2,1)}, bf16[197,768]{0,1:T(8,128)(2,1)S(1)}, u32[]{:S(2)}) copy-start(bf16[197,768]{0,1:T(8,128)(2,1)S(1)} %copy.265) | copy-start | bytes 907780
  167.4 57.8 %copy-start.8 = (bf16[197,768]{1,0:T(8,128)(2,1)}, bf16[197,768]{1,0:T(8,128)(2,1)S(1)}, u32[]{:S(2)}) copy-start(bf16[197,768]{1,0:T(8,128)(2,1)S(1)} %add_convert_fusion) | copy-start | bytes 907780
  168.7 33.9 %all-to-all-start.2 = ((bf16[16,32,768]{2,1,0:T(8,128)(2,1)}), bf16[16,32,768]{2,1,0:T(8,128)(2,1)}, u32[]{:S(2)}, u32[]{:S(2)}) async-start(bf16[16,32,768]{2,1,0:T(8,128)(2,1)} %bitcast.288), calls=%async_computation.2 | async-start | bytes 1572864 | tf_op jit(solution)/shard_map/all_to_all | solution.py:151
  216.6 20.4 %all-to-all-start.3 = ((bf16[16,32,768]{2,1,0:T(8,128)(2,1)}), bf16[16,32,768]{2,1,0:T(8,128)(2,1)}, u32[]{:S(2)}, u32[]{:S(2)}) async-start(bf16[16,32,768]{2,1,0:T(8,128)(2,1)} %bitcast.318), calls=%async_computation.3 | async-start | bytes 1572864 | tf_op jit(solution)/shard_map/all_to_all | solution.py:151
  237.0 5.6 copy-start.39
  237.0 5.6 copy-start.40
  238.6 40.4 %copy-start.7 = (f32[197,768]{1,0:T(8,128)}, f32[197,768]{1,0:T(8,128)S(1)}, u32[]{:S(2)}) copy-start(f32[197,768]{1,0:T(8,128)S(1)} %fusion.99) | copy-start | bytes 1815556
  279.0 16.3 %all-to-all-start.5 = ((bf16[16,32,768]{2,1,0:T(8,128)(2,1)}), bf16[16,32,768]{2,1,0:T(8,128)(2,1)}, u32[]{:S(2)}, u32[]{:S(2)}) async-start(bf16[16,32,768]{2,1,0:T(8,128)(2,1)} %bitcast.317), calls=%async_computation.5 | async-start | bytes 1572864 | tf_op jit(solution)/shard_map/all_to_all | solution.py:151
  283.3 4.6 copy-start.9
  283.3 155.9 %reduce-scatter.7.cloned.1.call-start = ((), (), s32[]{:S(2)}) async-start(), calls=%async_computation.21 | async-start | bytes 5529600 | tf_op jit(solution)/shard_map/reduce_scatter | solution.py:404
  303.7 8.6 %copy-start.29 = (bf16[197,768]{0,1:T(8,128)(2,1)S(1)}, bf16[197,768]{0,1:T(8,128)(2,1)}, u32[]{:S(2)}) copy-start(bf16[197,768]{0,1:T(8,128)(2,1)} %copy-done.28) | copy-start | bytes 907780
  327.8 7.0 %copy-start.36 = (bf16[768,16]{1,0:T(8,128)(2,1)S(1)}, bf16[768,16]{1,0:T(8,128)(2,1)}, u32[]{:S(2)}) copy-start(bf16[768,16]{1,0:T(8,128)(2,1)} %copy.283) | copy-start | bytes 73732
  334.9 8.6 %copy-start.18 = (bf16[768,108]{1,0:T(8,128)(2,1)}, bf16[768,108]{1,0:T(8,128)(2,1)S(1)}, u32[]{:S(2)}) copy-start(bf16[768,108]{1,0:T(8,128)(2,1)S(1)} %broadcast.170) | copy-start | bytes 497668
  347.4 5.3 copy-start.21
  347.4 5.3 copy-start.24
  348.9 14.8 %all-to-all-start.6 = ((bf16[16,32,768]{2,1,0:T(8,128)(2,1)}), bf16[16,32,768]{2,1,0:T(8,128)(2,1)S(1)}, u32[]{:S(2)}, u32[]{:S(2)}) async-start(bf16[16,32,768]{2,1,0:T(8,128)(2,1)} %bitcast.319), calls=%async_computation.6 | async-start | bytes 1572864 | tf_op jit(solution)/shard_map/all_to_all | solution.py:151
  364.6 34.2 %copy-start.11 = (bf16[2,197,512]{2,1,0:T(8,128)(2,1)S(1)}, bf16[2,197,512]{2,1,0:T(8,128)(2,1)}, u32[]{:S(2)}) copy-start(bf16[2,197,512]{2,1,0:T(8,128)(2,1)} %copy-done.10) | copy-start | bytes 1210372
  384.1 14.7 %all-to-all-start.7 = ((bf16[16,32,768]{2,1,0:T(8,128)(2,1)}), bf16[16,32,768]{2,1,0:T(8,128)(2,1)}, u32[]{:S(2)}, u32[]{:S(2)}) async-start(bf16[16,32,768]{2,1,0:T(8,128)(2,1)} %bitcast.315), calls=%async_computation.7 | async-start | bytes 1572864 | tf_op jit(solution)/shard_map/all_to_all | solution.py:151
  388.4 13.4 %copy-start.6 = (f32[197,768]{1,0:T(8,128)S(1)}, f32[197,768]{1,0:T(8,128)}, u32[]{:S(2)}) copy-start(f32[197,768]{1,0:T(8,128)} %copy-done.5) | copy-start | bytes 1815556
  388.4 87.6 %reduce-scatter.5.cloned.1.call-start = ((), (), s32[]{:S(2)}) async-start(), calls=%async_computation.20 | async-start | bytes 5529600 | tf_op jit(solution)/shard_map/reduce_scatter | solution.py:404
  408.2 6.9 %copy-start.25 = (bf16[197,768]{0,1:T(8,128)(2,1)S(1)}, bf16[197,768]{0,1:T(8,128)(2,1)}, u32[]{:S(2)}) copy-start(bf16[197,768]{0,1:T(8,128)(2,1)} %copy-done.23) | copy-start | bytes 907780
  410.3 9.7 %copy-start.45 = (bf16[12,64,197]{2,1,0:T(8,128)(2,1)S(1)}, bf16[12,64,197]{2,1,0:T(8,128)(2,1)}, u32[]{:S(2)}) copy-start(bf16[12,64,197]{2,1,0:T(8,128)(2,1)} %convolution_convert_fusion.10) | copy-start | bytes 907780
  415.1 9.3 %copy-start.47 = (bf16[12,64,197]{2,1,0:T(8,128)(2,1)}, bf16[12,64,197]{2,1,0:T(8,128)(2,1)S(1)}, u32[]{:S(2)}) copy-start(bf16[12,64,197]{2,1,0:T(8,128)(2,1)S(1)} %fusion.38) | copy-start | bytes 907780
  420.0 5.8 copy-start.32
  437.6 99.6 %reduce-scatter.11.cloned.1.call-start = ((), (), s32[]{:S(2)}) async-start(), calls=%async_computation.23 | async-start | bytes 10616832 | tf_op jit(solution)/shard_map/reduce_scatter | solution.py:346
  438.4 158.3 %reduce-scatter.9.cloned.1.call-start = ((), (), s32[]{:S(2)}) async-start(), calls=%async_computation.22 | async-start | bytes 10616832 | tf_op jit(solution)/shard_map/reduce_scatter | solution.py:346
  439.1 6.0 copy-start.14
  441.3 14.5 %all-to-all-start.10 = ((bf16[16,6,3200]{2,1,0:T(8,128)(2,1)}), bf16[16,6,3200]{2,1,0:T(8,128)(2,1)S(1)}, u32[]{:S(2)}, u32[]{:S(2)}) async-start(bf16[16,6,3200]{2,1,0:T(8,128)(2,1)} %reshape.277), calls=%async_computation.12 | async-start | bytes 1638400 | tf_op jit(solution)/shard_map/all_to_all | solution.py:163
  457.0 14.2 %all-to-all-start.11 = ((bf16[16,6,3200]{2,1,0:T(8,128)(2,1)}), bf16[16,6,3200]{2,1,0:T(8,128)(2,1)S(1)}, u32[]{:S(2)}, u32[]{:S(2)}) async-start(bf16[16,6,3200]{2,1,0:T(8,128)(2,1)} %broadcast_in_dim.27), calls=%async_computation.13 | async-start | bytes 1638400 | tf_op jit(solution)/shard_map/all_to_all | solution.py:171
  478.0 17.8 %all-to-all-start.8 = ((bf16[16,6,3200]{2,1,0:T(8,128)(2,1)}), bf16[16,6,3200]{2,1,0:T(8,128)(2,1)S(1)}, u32[]{:S(2)}, u32[]{:S(2)}) async-start(bf16[16,6,3200]{2,1,0:T(8,128)(2,1)} %reshape.276), calls=%async_computation.9 | async-start | bytes 1638400 | tf_op jit(solution)/shard_map/all_to_all | solution.py:163
  496.9 14.5 %all-to-all-start.9 = ((bf16[16,6,3200]{2,1,0:T(8,128)(2,1)}), bf16[16,6,3200]{2,1,0:T(8,128)(2,1)S(1)}, u32[]{:S(2)}, u32[]{:S(2)}) async-start(bf16[16,6,3200]{2,1,0:T(8,128)(2,1)} %broadcast_in_dim.26), calls=%async_computation.10 | async-start | bytes 1638400 | tf_op jit(solution)/shard_map/all_to_all | solution.py:171
  (25 other events, 67.9 us)
Sparse Core Ops, SparseCore 0:
  14.1 38.7 all-gather.4
  55.1 54.1 all-gather.6
  111.0 35.3 all-gather.8
  148.5 54.1 all-gather.10
  343.6 36.1 reduce-scatter.6
  437.7 38.1 reduce-scatter.4
  478.3 58.8 reduce-scatter.10
  539.6 57.0 reduce-scatter.8

commit v2 on v1

--- a/solution.py
+++ b/solution.py
@@ -311,6 +311,7 @@
     grad = cotangent[0]
     layer_parts = []
     expert_parts = []
+    share = None
     for layer in reversed(range(depth)):
         (
             gathered,
@@ -343,6 +344,8 @@
         grad_received = exchange(grad_sent, experts)
         rows_kept, pre, expert_full = kept
         expert_grad, row_grad = ffn_backward(rows_kept, grad_received, pre, expert_full)
+        if share is not None:
+            expert_grad, share = lax.optimization_barrier((expert_grad, share))
         expert_part = lax.psum_scatter(expert_grad, "wshard", scatter_dimension=0, tiled=True)
         back = matmul(select[0] + select[1], exchange(row_grad, experts))
         prob_grad = jnp.sum(choice_mask * gate_grad[..., None], axis=1)
@@ -401,14 +404,18 @@
             ],
             axis=1,
         )
+        attn_grad, expert_part = lax.optimization_barrier((attn_grad, expert_part))
+        if share is not None:
+            attn_grad, share = lax.optimization_barrier((attn_grad, share))
+            layer_parts.append(unpack_attn(sum_over_experts(share, experts), width, experts))
         share = lax.psum_scatter(attn_grad, "wshard", scatter_dimension=0, tiled=True)
-        layer_parts.append(unpack_attn(sum_over_experts(share, experts), width, experts))
         expert_parts.append(
             (
                 expert_part[:, :width].T.astype(jnp.float32),
                 expert_part[:, width:].astype(jnp.float32),
             )
         )
+    layer_parts.append(unpack_attn(sum_over_experts(share, experts), width, experts))
     layer_parts = list(reversed(layer_parts))
     expert_parts = list(reversed(expert_parts))
     stacked = [jnp.stack([entry[index] for entry in layer_parts]) for index in range(7)]

time: 620 us -> 548 us (0.88)
  the two profiles are of different devices: /device:TPU:1 before, /device:TPU:24 now
where the time goes in v2:
time: 548 us; the launch traced here: 538 us
  waiting for transfers between devices  177 us (32%)
  matrix products  104 us (19%)
  Pallas kernels  66.7 us (12%)
  local copies, waits for them, and re-layouts  65 us (12%)
  starting transfers between devices  52.6 us (10%)
  blocking collectives  32.5 us (6%)
  other arithmetic  24.7 us (5%)
  between operations  15.8 us (3%)
    all_gather x2, waiting for transfers between devices, per_device(): lax.all_gather(expert_pack[layer], 'wshard', axis=0, tiled=True)  46.9 us
    dot_general x26, matrix products, matmul(): return jnp.dot(left, right, preferred_element_type=jnp.float32)  46.5 us
    all_to_all x6, waiting for transfers between devices, exchange(): lax.all_to_all(rows.reshape(experts, count // experts, width), 'expert',...  45 us
    all_gather x2, waiting for transfers between devices, per_device(): attn_full = lax.all_gather(attn_pack[layer], 'wshard', axis=0, tiled=True)  40.6 us
    pallas_call x2, Pallas kernels, ffn_backward(): pl.pallas_call(ffn_backward_kernel, grid=(BLOCKS,), in_specs=[pl.BlockSpe...  38.9 us
    all_to_all x6, starting transfers between devices, exchange(): lax.all_to_all(rows.reshape(experts, count // experts, width), 'expert',...  37.1 us
    all_to_all x2, blocking collectives, exchange(): lax.all_to_all(rows.reshape(experts, count // experts, width), 'expert',...  32.5 us
    pallas_call x2, Pallas kernels, ffn_forward(): pl.pallas_call(ffn_forward_kernel, grid=(BLOCKS,), in_specs=[pl.BlockSpec...  27.9 us
  transfers between devices with their start and end apart: 18, of which 12 were waited for; matrix products, arithmetic and copies ran while one was open for 31% of the time, Pallas kernels for 6%

profile of v2, /device:TPU:24, one launch (start us, length us, event | category | flops | bytes accessed | tf_op | source)
XLA Modules:
  0.0 538.2 jit_solution(2602833536700920109)
XLA Ops:
  23.2 25.6 %all-gather.5.cloned.1.call-done = bf16[768,3200]{1,0:T(8,128)(2,1)} async-done(((bf16[96,3200]{1,0:T(8,128)(2,1)}), bf16[768,3200]{1,0:T(8,128)(2,1)}) %all-gather.5.cloned.1.call-update) | async-done | bytes 4915216 | tf_op jit(solution)/shard_map/all_gather | solution.py:251
  50.9 3.0 convolution_convert_fusion.3
  56.5 3.4 convolution_convert_fusion.13
  63.7 7.0 %all-to-all-start = ((bf16[16,32,768]{2,1,0:T(8,128)(2,1)}), bf16[16,32,768]{2,1,0:T(8,128)(2,1)S(1)}, u32[]{:S(2)}, u32[]{:S(2)}) async-start(bf16[16,32,768]{2,1,0:T(8,128)(2,1)} %bitcast.21), calls=%async_computation | async-start | bytes 1572864 | tf_op jit(solution)/shard_map/all_to_all | solution.py:151
  74.1 11.4 %all-to-all-done = bf16[16,32,768]{2,1,0:T(8,128)(2,1)S(1)} async-done(((bf16[16,32,768]{2,1,0:T(8,128)(2,1)}), bf16[16,32,768]{2,1,0:T(8,128)(2,1)S(1)}, u32[]{:S(2)}, u32[]{:S(2)}) %all-to-all-start) | async-done | bytes 786464 | tf_op jit(solution)/shard_map/all_to_all | solution.py:151
  85.4 19.8 %all-gather.7.cloned.1.call-done.weight_ref = bf16[3072,1536]{1,0:T(8,128)(2,1)} async-done(((bf16[384,1536]{1,0:T(8,128)(2,1)}), bf16[3072,1536]{1,0:T(8,128)(2,1)}) %all-gather.7.cloned.1.call-update) | async-done | bytes 9437200 | tf_op jit(solution)/shard_map/all_gather | solution.py:282
  105.2 13.9 %ffn_forward.2 = (f32[512,3072]{1,0:T(8,128)}, bf16[512,768]{1,0:T(8,128)(2,1)}) custom-call(bf16[512,768]{1,0:T(8,128)(2,1)} %bitcast.282, bf16[3072,1536]{1,0:T(8,128)(2,1)} %all-gather.7.cloned.1.call-done.weight_ref), custom_call_target="tpu_custom_call" | custom-call | tf_op jit(solution)/shard_map/ffn_forward/pallas_call | solution.py:76
  119.2 7.3 %all-to-all-start.1 = ((bf16[16,32,768]{2,1,0:T(8,128)(2,1)}), bf16[16,32,768]{2,1,0:T(8,128)(2,1)S(1)}, u32[]{:S(2)}, u32[]{:S(2)}) async-start(bf16[16,32,768]{2,1,0:T(8,128)(2,1)} %bitcast.318), calls=%async_computation.1 | async-start | bytes 1572864 | tf_op jit(solution)/shard_map/all_to_all | solution.py:151
  127.3 15.1 %all-gather.9.cloned.1.call-done = bf16[768,3200]{1,0:T(8,128)(2,1)} async-done(((bf16[96,3200]{1,0:T(8,128)(2,1)}), bf16[768,3200]{1,0:T(8,128)(2,1)}) %all-gather.9.cloned.1.call-update) | async-done | bytes 4915216 | tf_op jit(solution)/shard_map/all_gather | solution.py:251
  155.2 4.9 convolution_convert_fusion.12
  164.5 7.0 %all-to-all-start.2 = ((bf16[16,32,768]{2,1,0:T(8,128)(2,1)}), bf16[16,32,768]{2,1,0:T(8,128)(2,1)}, u32[]{:S(2)}, u32[]{:S(2)}) async-start(bf16[16,32,768]{2,1,0:T(8,128)(2,1)} %bitcast.290), calls=%async_computation.2 | async-start | bytes 1572864 | tf_op jit(solution)/shard_map/all_to_all | solution.py:151
  171.5 27.1 %all-gather.11.cloned.1.call-done.weight_ref = bf16[3072,1536]{1,0:T(8,128)(2,1)} async-done(((bf16[384,1536]{1,0:T(8,128)(2,1)}), bf16[3072,1536]{1,0:T(8,128)(2,1)}) %all-gather.11.cloned.1.call-update) | async-done | bytes 9437200 | tf_op jit(solution)/shard_map/all_gather | solution.py:282
  198.6 13.9 %ffn_forward.3 = (f32[512,3072]{1,0:T(8,128)}, bf16[512,768]{1,0:T(8,128)(2,1)}) custom-call(bf16[512,768]{1,0:T(8,128)(2,1)} %bitcast.52.rows_ref, bf16[3072,1536]{1,0:T(8,128)(2,1)} %all-gather.11.cloned.1.call-done.weight_ref), custom_call_target="tpu_custom_call" | custom-call | tf_op jit(solution)/shard_map/ffn_forward/pallas_call | solution.py:76
  212.5 7.1 %all-to-all-start.3 = ((bf16[16,32,768]{2,1,0:T(8,128)(2,1)}), bf16[16,32,768]{2,1,0:T(8,128)(2,1)S(1)}, u32[]{:S(2)}, u32[]{:S(2)}) async-start(bf16[16,32,768]{2,1,0:T(8,128)(2,1)} %bitcast.319), calls=%async_computation.3 | async-start | bytes 1572864 | tf_op jit(solution)/shard_map/all_to_all | solution.py:151
  224.0 10.4 %all-to-all-done.3 = bf16[16,32,768]{2,1,0:T(8,128)(2,1)S(1)} async-done(((bf16[16,32,768]{2,1,0:T(8,128)(2,1)}), bf16[16,32,768]{2,1,0:T(8,128)(2,1)S(1)}, u32[]{:S(2)}, u32[]{:S(2)}) %all-to-all-start.3) | async-done | bytes 786464 | tf_op jit(solution)/shard_map/all_to_all | solution.py:151
  239.8 17.2 %all_to_all.60 = bf16[16,32,768]{2,1,0:T(8,128)(2,1)} all-to-all(bf16[16,32,768]{2,1,0:T(8,128)(2,1)S(1)} %bitcast.320), channel_id=1, replica_groups=mesh['expert'=16,'wshard'=8] {'expert'}, dimensions={0} | all-to-all | bytes 1572864 | tf_op jit(solution)/shard_map/all_to_all | solution.py:151
  257.0 19.4 %ffn_backward.2 = (bf16[3072,1536]{1,0:T(8,128)(2,1)}, bf16[512,768]{1,0:T(8,128)(2,1)}) custom-call(bf16[512,768]{1,0:T(8,128)(2,1)} %bitcast.52.rows_ref, bf16[512,768]{1,0:T(8,128)(2,1)} %bitcast.288, f32[512,3072]{1,0:T(8,128)} %get-tuple-element.29.pre_ref, bf16[3072,1536]{1,0:T(8,128)(2,1)} %all-gather.11.cloned.1.call-done.weight_ref), custom_call_target="tpu_custom_call" | custom-call | tf_op jit(solution)/shard_map/ffn_backward/pallas_call | solution.py:127
  276.4 4.3 all-to-all-start.5
  281.3 3.9 fusion.10
  286.2 7.3 %all-to-all-done.5 = bf16[16,32,768]{2,1,0:T(8,128)(2,1)} async-done(((bf16[16,32,768]{2,1,0:T(8,128)(2,1)}), bf16[16,32,768]{2,1,0:T(8,128)(2,1)}, u32[]{:S(2)}, u32[]{:S(2)}) %all-to-all-start.5) | async-done | bytes 786464 | tf_op jit(solution)/shard_map/all_to_all | solution.py:151
  299.1 2.6 convolution_convert_fusion.15
  303.6 4.2 convolution_convert_fusion.11
  307.8 3.1 fusion.196
  310.9 5.7 %fusion.44 = bf16[12,64,197]{2,1,0:T(8,128)(2,1)} fusion(bf16[197,12,64]{0,2,1:T(8,128)(2,1)} %bitcast.306, f32[12,197,197]{1,2,0:T(8,128)} %fusion.10, f32[12,197,197]{1,2,0:T(8,128)} %fusion.196), kind=kOutput, calls=%fused_computation.47 | convolution fusion | flops 62093020 | bytes 4330848 | tf_op jit(solution)/shard_map/hst,thd->shd/dot_general | solution.py:379
  316.6 5.6 %fusion.47 = bf16[12,64,197]{2,1,0:T(8,128)(2,1)} fusion(bf16[197,12,64]{0,2,1:T(8,128)(2,1)S(1)} %bitcast.303, f32[12,197,197]{1,2,0:T(8,128)} %fusion.10, f32[12,197,197]{1,2,0:T(8,128)} %fusion.196), kind=kOutput, calls=%fused_computation.48 | convolution fusion | flops 62093020 | bytes 4330848 | tf_op jit(solution)/shard_map/hst,shd->thd/dot_general | solution.py:380
  322.3 4.7 multiply_reduce_fusion.3
  331.2 3.1 convolution_convert_fusion
  334.3 8.6 %concatenate.51 = bf16[768,3200]{1,0:T(8,128)(2,1)} concatenate(bf16[768,2304]{1,0:T(8,128)(2,1)} %convolution_convert_fusion, bf16[768,768]{1,0:T(8,128)(2,1)} %convolution_convert_fusion.4, bf16[768,16]{1,0:T(8,128)(2,1)S(1)} %copy-done.35, bf16[768,1]{1,0:T(8,128)(2,1)S(1)} %stack.154, bf16[768,1]{1,0:T(8,128)(2,1)} %stack.155, bf16[768,1]{1,0:T(8,128)(2,1)} %stack.156, ...), dimensions={1} | concatenate | bytes 9830400 | tf_op jit(solution)/shard_map/concatenate | solution.py:397
  346.7 15.3 %all_to_all.61 = bf16[16,32,768]{2,1,0:T(8,128)(2,1)} all-to-all(bf16[16,32,768]{2,1,0:T(8,128)(2,1)S(1)} %bitcast.321), channel_id=1, replica_groups=mesh['expert'=16,'wshard'=8] {'expert'}, dimensions={0} | all-to-all | bytes 1572864 | tf_op jit(solution)/shard_map/all_to_all | solution.py:151
  362.0 19.5 %ffn_backward.3 = (bf16[3072,1536]{1,0:T(8,128)(2,1)}, bf16[512,768]{1,0:T(8,128)(2,1)}) custom-call(bf16[512,768]{1,0:T(8,128)(2,1)} %bitcast.283, bf16[512,768]{1,0:T(8,128)(2,1)} %bitcast.289, f32[512,3072]{1,0:T(8,128)} %get-tuple-element.31.pre_ref, bf16[3072,1536]{1,0:T(8,128)(2,1)} %all-gather.7.cloned.1.call-done.weight_ref), custom_call_target="tpu_custom_call" | custom-call | tf_op jit(solution)/shard_map/ffn_backward/pallas_call | solution.py:127
  382.6 2.6 fusion.11
  385.2 4.4 all-to-all-start.7
  390.3 15.9 %all-to-all-done.7 = bf16[16,32,768]{2,1,0:T(8,128)(2,1)} async-done(((bf16[16,32,768]{2,1,0:T(8,128)(2,1)}), bf16[16,32,768]{2,1,0:T(8,128)(2,1)}, u32[]{:S(2)}, u32[]{:S(2)}) %all-to-all-start.7) | async-done | bytes 786464 | tf_op jit(solution)/shard_map/all_to_all | solution.py:151
  411.6 4.2 convolution_convert_fusion.10
  417.8 4.9 fusion.38
  422.7 5.0 fusion.41
  427.7 4.4 multiply_reduce_fusion.5
  434.8 3.1 convolution_convert_fusion.1
  437.9 8.2 %concatenate.50 = bf16[768,3200]{1,0:T(8,128)(2,1)} concatenate(bf16[768,2304]{1,0:T(8,128)(2,1)} %convolution_convert_fusion.1, bf16[768,768]{1,0:T(8,128)(2,1)S(1)} %convolution_convert_fusion.5, bf16[768,16]{1,0:T(8,128)(2,1)S(1)} %copy.277, bf16[768,1]{1,0:T(8,128)(2,1)S(1)} %stack.150, bf16[768,1]{1,0:T(8,128)(2,1)S(1)} %stack.151, bf16[768,1]{1,0:T(8,128)(2,1)S(1)} %copy-done.36, ...), dimensions={1} | concatenate | bytes 9830400 | tf_op jit(solution)/shard_map/concatenate | solution.py:397
  449.7 3.6 all-to-all-start.10
  456.2 12.2 %all-to-all-done.10 = bf16[16,6,3200]{2,1,0:T(8,128)(2,1)S(1)} async-done(((bf16[16,6,3200]{2,1,0:T(8,128)(2,1)}), bf16[16,6,3200]{2,1,0:T(8,128)(2,1)S(1)}, u32[]{:S(2)}, u32[]{:S(2)}) %all-to-all-start.10) | async-done | bytes 614432 | tf_op jit(solution)/shard_map/all_to_all | solution.py:163
  469.5 3.6 all-to-all-start.11
  477.2 2.8 fusion.57
  480.0 7.1 %all-to-all-done.11 = bf16[16,6,3200]{2,1,0:T(8,128)(2,1)S(1)} async-done(((bf16[16,6,3200]{2,1,0:T(8,128)(2,1)}), bf16[16,6,3200]{2,1,0:T(8,128)(2,1)S(1)}, u32[]{:S(2)}, u32[]{:S(2)}) %all-to-all-start.11) | async-done | bytes 614432 | tf_op jit(solution)/shard_map/all_to_all | solution.py:171
  489.4 3.6 all-to-all-start.8
  493.6 12.8 %all-to-all-done.8 = bf16[16,6,3200]{2,1,0:T(8,128)(2,1)S(1)} async-done(((bf16[16,6,3200]{2,1,0:T(8,128)(2,1)}), bf16[16,6,3200]{2,1,0:T(8,128)(2,1)S(1)}, u32[]{:S(2)}, u32[]{:S(2)}) %all-to-all-start.8) | async-done | bytes 614432 | tf_op jit(solution)/shard_map/all_to_all | solution.py:163
  507.5 3.6 all-to-all-start.9
  511.2 12.4 %all-to-all-done.9 = bf16[16,6,3200]{2,1,0:T(8,128)(2,1)S(1)} async-done(((bf16[16,6,3200]{2,1,0:T(8,128)(2,1)}), bf16[16,6,3200]{2,1,0:T(8,128)(2,1)S(1)}, u32[]{:S(2)}, u32[]{:S(2)}) %all-to-all-start.9) | async-done | bytes 614432 | tf_op jit(solution)/shard_map/all_to_all | solution.py:171
  (367 shorter events, 106.7 us)
Async XLA Ops:
  7.2 41.6 %all-gather.5.cloned.1.call-start = ((), (), s32[]{:S(2)}) async-start(), calls=%async_computation.16 | async-start | bytes 5529600 | tf_op jit(solution)/shard_map/all_gather | solution.py:251
  13.3 91.9 %all-gather.7.cloned.1.call-start = ((), (), s32[]{:S(2)}) async-start(), calls=%async_computation.17 | async-start | bytes 10616832 | tf_op jit(solution)/shard_map/all_gather | solution.py:282
  17.4 124.9 %all-gather.9.cloned.1.call-start = ((), (), s32[]{:S(2)}) async-start(), calls=%async_computation.18 | async-start | bytes 5529600 | tf_op jit(solution)/shard_map/all_gather | solution.py:251
  19.1 179.5 %all-gather.11.cloned.1.call-start = ((), (), s32[]{:S(2)}) async-start(), calls=%async_computation.19 | async-start | bytes 10616832 | tf_op jit(solution)/shard_map/all_gather | solution.py:282
  22.2 105.0 %copy-start.47 = (s32[197,2]{0,1:T(2,128)}, s32[197,2]{0,1:T(2,128)S(1)}, u32[]{:S(2)}) copy-start(s32[197,2]{0,1:T(2,128)S(1)} %get-tuple-element.172) | copy-start | bytes 4732
  22.7 27.6 %copy-start.62 = (f32[197]{0:T(256)}, f32[197]{0:T(256)S(1)}, u32[]{:S(2)}) copy-start(f32[197]{0:T(256)S(1)} %broadcast_multiply_fusion.11) | copy-start | bytes 2368
  23.0 27.4 %copy-start.68 = (f32[197]{0:T(256)}, f32[197]{0:T(256)S(1)}, u32[]{:S(2)}) copy-start(f32[197]{0:T(256)S(1)} %add_rsqrt_fusion.3) | copy-start | bytes 2368
  23.2 39.1 %copy-start.10 = (bf16[2,197,512]{2,1,0:T(8,128)(2,1)}, bf16[2,197,512]{2,1,0:T(8,128)(2,1)S(1)}, u32[]{:S(2)}) copy-start(bf16[2,197,512]{2,1,0:T(8,128)(2,1)S(1)} %get-tuple-element.182) | copy-start | bytes 1210372
  63.7 21.8 %all-to-all-start = ((bf16[16,32,768]{2,1,0:T(8,128)(2,1)}), bf16[16,32,768]{2,1,0:T(8,128)(2,1)S(1)}, u32[]{:S(2)}, u32[]{:S(2)}) async-start(bf16[16,32,768]{2,1,0:T(8,128)(2,1)} %bitcast.21), calls=%async_computation | async-start | bytes 1572864 | tf_op jit(solution)/shard_map/all_to_all | solution.py:151
  71.6 91.0 %copy-start.12 = (bf16[2,197,512]{2,1,0:T(8,128)(2,1)}, bf16[2,197,512]{2,1,0:T(8,128)(2,1)S(1)}, u32[]{:S(2)}) copy-start(bf16[2,197,512]{2,1,0:T(8,128)(2,1)S(1)} %get-tuple-element.178) | copy-start | bytes 1210372
  85.4 19.8 %copy-start.1 = (bf16[16,32,768]{2,1,0:T(8,128)(2,1)}, bf16[16,32,768]{2,1,0:T(8,128)(2,1)S(1)}, u32[]{:S(2)}) copy-start(bf16[16,32,768]{2,1,0:T(8,128)(2,1)S(1)} %all-to-all-done) | copy-start | bytes 2359300
  119.2 25.8 %all-to-all-start.1 = ((bf16[16,32,768]{2,1,0:T(8,128)(2,1)}), bf16[16,32,768]{2,1,0:T(8,128)(2,1)S(1)}, u32[]{:S(2)}, u32[]{:S(2)}) async-start(bf16[16,32,768]{2,1,0:T(8,128)(2,1)} %bitcast.318), calls=%async_computation.1 | async-start | bytes 1572864 | tf_op jit(solution)/shard_map/all_to_all | solution.py:151
  149.9 10.2 %copy-start.26 = (bf16[197,768]{0,1:T(8,128)(2,1)}, bf16[197,768]{0,1:T(8,128)(2,1)S(1)}, u32[]{:S(2)}) copy-start(bf16[197,768]{0,1:T(8,128)(2,1)S(1)} %copy.264) | copy-start | bytes 907780
  151.2 8.9 %copy-start.28 = (bf16[197,768]{0,1:T(8,128)(2,1)}, bf16[197,768]{0,1:T(8,128)(2,1)S(1)}, u32[]{:S(2)}) copy-start(bf16[197,768]{0,1:T(8,128)(2,1)S(1)} %copy.265) | copy-start | bytes 907780
  162.1 50.5 %copy-start.45 = (f32[197]{0:T(256)}, f32[197]{0:T(256)S(1)}, u32[]{:S(2)}) copy-start(f32[197]{0:T(256)S(1)} %broadcast_multiply_fusion.8) | copy-start | bytes 2368
  162.3 50.2 %copy-start.56 = (f32[197]{0:T(256)}, f32[197]{0:T(256)S(1)}, u32[]{:S(2)}) copy-start(f32[197]{0:T(256)S(1)} %add_rsqrt_fusion) | copy-start | bytes 2368
  164.5 34.1 %all-to-all-start.2 = ((bf16[16,32,768]{2,1,0:T(8,128)(2,1)}), bf16[16,32,768]{2,1,0:T(8,128)(2,1)}, u32[]{:S(2)}, u32[]{:S(2)}) async-start(bf16[16,32,768]{2,1,0:T(8,128)(2,1)} %bitcast.290), calls=%async_computation.2 | async-start | bytes 1572864 | tf_op jit(solution)/shard_map/all_to_all | solution.py:151
  212.5 21.9 %all-to-all-start.3 = ((bf16[16,32,768]{2,1,0:T(8,128)(2,1)}), bf16[16,32,768]{2,1,0:T(8,128)(2,1)S(1)}, u32[]{:S(2)}, u32[]{:S(2)}) async-start(bf16[16,32,768]{2,1,0:T(8,128)(2,1)} %bitcast.319), calls=%async_computation.3 | async-start | bytes 1572864 | tf_op jit(solution)/shard_map/all_to_all | solution.py:151
  219.7 123.3 %reduce-scatter.5.cloned.1.call-start = ((), (), s32[]{:S(2)}) async-start(), calls=%async_computation.20 | async-start | bytes 10616832 | tf_op jit(solution)/shard_map/reduce_scatter | solution.py:349
  276.4 17.2 %all-to-all-start.5 = ((bf16[16,32,768]{2,1,0:T(8,128)(2,1)}), bf16[16,32,768]{2,1,0:T(8,128)(2,1)}, u32[]{:S(2)}, u32[]{:S(2)}) async-start(bf16[16,32,768]{2,1,0:T(8,128)(2,1)} %bitcast.64), calls=%async_computation.5 | async-start | bytes 1572864 | tf_op jit(solution)/shard_map/all_to_all | solution.py:151
  280.7 12.8 %copy-start.13 = (bf16[2,197,512]{2,1,0:T(8,128)(2,1)S(1)}, bf16[2,197,512]{2,1,0:T(8,128)(2,1)}, u32[]{:S(2)}) copy-start(bf16[2,197,512]{2,1,0:T(8,128)(2,1)} %copy-done.12) | copy-start | bytes 1210372
  280.7 14.4 %copy-start.46 = (f32[197]{0:T(256)S(1)}, f32[197]{0:T(256)}, u32[]{:S(2)}) copy-start(f32[197]{0:T(256)} %copy-done.45) | copy-start | bytes 2368
  280.7 14.4 %copy-start.57 = (f32[197]{0:T(256)S(1)}, f32[197]{0:T(256)}, u32[]{:S(2)}) copy-start(f32[197]{0:T(256)} %copy-done.56) | copy-start | bytes 2368
  280.8 100.7 %reduce-scatter.7.cloned.1.call-start = ((), (), s32[]{:S(2)}) async-start(), calls=%async_computation.21 | async-start | bytes 5529600 | tf_op jit(solution)/shard_map/reduce_scatter | solution.py:411
  307.8 8.8 %copy-start.27 = (bf16[197,768]{0,1:T(8,128)(2,1)S(1)}, bf16[197,768]{0,1:T(8,128)(2,1)}, u32[]{:S(2)}) copy-start(bf16[197,768]{0,1:T(8,128)(2,1)} %copy-done.26) | copy-start | bytes 907780
  310.9 11.3 %copy-start.54 = (f32[768]{0:T(1024)S(1)}, f32[768]{0:T(1024)}, u32[]{:S(2)}) copy-start(f32[768]{0:T(1024)} %get-tuple-element.121) | copy-start | bytes 9220
  310.9 11.3 %copy-start.67 = (f32[197]{0:T(256)S(1)}, f32[197]{0:T(256)}, u32[]{:S(2)}) copy-start(f32[197]{0:T(256)} %copy-done.66) | copy-start | bytes 2368
  310.9 11.3 %copy-start.75 = (f32[197]{0:T(256)S(1)}, f32[197]{0:T(256)}, u32[]{:S(2)}) copy-start(f32[197]{0:T(256)} %copy-done.74) | copy-start | bytes 2368
  322.3 7.4 %copy-start.32 = (bf16[12,64,197]{2,1,0:T(8,128)(2,1)S(1)}, bf16[12,64,197]{2,1,0:T(8,128)(2,1)}, u32[]{:S(2)}) copy-start(bf16[12,64,197]{2,1,0:T(8,128)(2,1)} %convolution_convert_fusion.12) | copy-start | bytes 907780
  334.3 8.6 %copy-start.17 = (bf16[768,108]{1,0:T(8,128)(2,1)}, bf16[768,108]{1,0:T(8,128)(2,1)S(1)}, u32[]{:S(2)}) copy-start(bf16[768,108]{1,0:T(8,128)(2,1)S(1)} %broadcast.170) | copy-start | bytes 497668
  343.1 103.1 %reduce-scatter.9.cloned.1.call-start = ((), (), s32[]{:S(2)}) async-start(), calls=%async_computation.22 | async-start | bytes 10616832 | tf_op jit(solution)/shard_map/reduce_scatter | solution.py:349
  345.9 16.1 %copy-start.5 = (f32[197,768]{1,0:T(8,128)}, f32[197,768]{1,0:T(8,128)S(1)}, u32[]{:S(2)}) copy-start(f32[197,768]{1,0:T(8,128)S(1)} %get-tuple-element.128) | copy-start | bytes 1815556
  382.6 7.3 %copy-start.58 = (f32[197]{0:T(256)S(1)}, f32[197]{0:T(256)}, u32[]{:S(2)}) copy-start(f32[197]{0:T(256)} %get-tuple-element.193) | copy-start | bytes 2368
  382.6 23.6 %copy-start.11 = (bf16[2,197,512]{2,1,0:T(8,128)(2,1)S(1)}, bf16[2,197,512]{2,1,0:T(8,128)(2,1)}, u32[]{:S(2)}) copy-start(bf16[2,197,512]{2,1,0:T(8,128)(2,1)} %copy-done.10) | copy-start | bytes 1210372
  385.2 22.5 %copy-start.50 = (f32[197]{0:T(256)S(1)}, f32[197]{0:T(256)}, u32[]{:S(2)}) copy-start(f32[197]{0:T(256)} %copy-done.49) | copy-start | bytes 2368
  385.2 21.0 %all-to-all-start.7 = ((bf16[16,32,768]{2,1,0:T(8,128)(2,1)}), bf16[16,32,768]{2,1,0:T(8,128)(2,1)}, u32[]{:S(2)}, u32[]{:S(2)}) async-start(bf16[16,32,768]{2,1,0:T(8,128)(2,1)} %bitcast.317), calls=%async_computation.7 | async-start | bytes 1572864 | tf_op jit(solution)/shard_map/all_to_all | solution.py:151
  389.7 19.6 %copy-start.6 = (f32[197,768]{1,0:T(8,128)S(1)}, f32[197,768]{1,0:T(8,128)}, u32[]{:S(2)}) copy-start(f32[197,768]{1,0:T(8,128)} %copy-done.5) | copy-start | bytes 1815556
  389.7 97.6 %reduce-scatter.11.cloned.1.call-start = ((), (), s32[]{:S(2)}) async-start(), calls=%async_computation.23 | async-start | bytes 5529600 | tf_op jit(solution)/shard_map/reduce_scatter | solution.py:411
  417.8 9.9 %copy-start.52 = (f32[768]{0:T(1024)S(1)}, f32[768]{0:T(1024)}, u32[]{:S(2)}) copy-start(f32[768]{0:T(1024)} %copy-done.51) | copy-start | bytes 9220
  417.8 9.9 %copy-start.63 = (f32[197]{0:T(256)S(1)}, f32[197]{0:T(256)}, u32[]{:S(2)}) copy-start(f32[197]{0:T(256)} %copy-done.62) | copy-start | bytes 2368
  417.8 9.9 %copy-start.69 = (f32[197]{0:T(256)S(1)}, f32[197]{0:T(256)}, u32[]{:S(2)}) copy-start(f32[197]{0:T(256)} %copy-done.68) | copy-start | bytes 2368
  417.8 9.9 %copy-start.79 = (bf16[12,64,197]{2,1,0:T(8,128)(2,1)S(1)}, bf16[12,64,197]{2,1,0:T(8,128)(2,1)}, u32[]{:S(2)}) copy-start(bf16[12,64,197]{2,1,0:T(8,128)(2,1)} %convolution_convert_fusion.10) | copy-start | bytes 907780
  422.7 9.5 %copy-start.82 = (bf16[12,64,197]{2,1,0:T(8,128)(2,1)}, bf16[12,64,197]{2,1,0:T(8,128)(2,1)S(1)}, u32[]{:S(2)}) copy-start(bf16[12,64,197]{2,1,0:T(8,128)(2,1)S(1)} %fusion.38) | copy-start | bytes 907780
  449.7 18.6 %all-to-all-start.10 = ((bf16[16,6,3200]{2,1,0:T(8,128)(2,1)}), bf16[16,6,3200]{2,1,0:T(8,128)(2,1)S(1)}, u32[]{:S(2)}, u32[]{:S(2)}) async-start(bf16[16,6,3200]{2,1,0:T(8,128)(2,1)} %reshape.277), calls=%async_computation.14 | async-start | bytes 1638400 | tf_op jit(solution)/shard_map/all_to_all | solution.py:163
  455.1 18.0 %copy-start.34 = (bf16[384,1536]{1,0:T(8,128)(2,1)S(1)}, bf16[384,1536]{1,0:T(8,128)(2,1)}, u32[]{:S(2)}) copy-start(bf16[384,1536]{1,0:T(8,128)(2,1)} %reduce-scatter.9.cloned.1.call-done) | copy-start | bytes 3538948
  469.5 17.6 %all-to-all-start.11 = ((bf16[16,6,3200]{2,1,0:T(8,128)(2,1)}), bf16[16,6,3200]{2,1,0:T(8,128)(2,1)S(1)}, u32[]{:S(2)}, u32[]{:S(2)}) async-start(bf16[16,6,3200]{2,1,0:T(8,128)(2,1)} %broadcast_in_dim.27), calls=%async_computation.15 | async-start | bytes 1638400 | tf_op jit(solution)/shard_map/all_to_all | solution.py:171
  489.4 17.0 %all-to-all-start.8 = ((bf16[16,6,3200]{2,1,0:T(8,128)(2,1)}), bf16[16,6,3200]{2,1,0:T(8,128)(2,1)S(1)}, u32[]{:S(2)}, u32[]{:S(2)}) async-start(bf16[16,6,3200]{2,1,0:T(8,128)(2,1)} %reshape.276), calls=%async_computation.12 | async-start | bytes 1638400 | tf_op jit(solution)/shard_map/all_to_all | solution.py:163
  507.5 16.1 %all-to-all-start.9 = ((bf16[16,6,3200]{2,1,0:T(8,128)(2,1)}), bf16[16,6,3200]{2,1,0:T(8,128)(2,1)S(1)}, u32[]{:S(2)}, u32[]{:S(2)}) async-start(bf16[16,6,3200]{2,1,0:T(8,128)(2,1)} %broadcast_in_dim.26), calls=%async_computation.13 | async-start | bytes 1638400 | tf_op jit(solution)/shard_map/all_to_all | solution.py:171
  (57 other events, 189.8 us)
Sparse Core Ops, SparseCore 0:
  13.4 35.3 all-gather.4
  51.1 54.1 all-gather.6
  106.9 35.3 all-gather.8
  144.4 54.1 all-gather.10
  276.5 53.6 reduce-scatter.4
  343.1 34.4 reduce-scatter.6
  381.7 56.6 reduce-scatter.8
  446.3 33.1 reduce-scatter.10

commit v3 on v2

--- a/solution.py
+++ b/solution.py
@@ -1,3 +1,4 @@
+import functools
 import math
 
 import jax
@@ -146,6 +147,353 @@
     )(rows, grads, pre, weight)
 
 
+def ffn_both_kernel(rows_ref, grads_ref, weight_ref, weight_grad_ref, out_ref, back_ref, total, back):
+    step = pl.program_id(0)
+    width = rows_ref.shape[1]
+    rows = rows_ref[...]
+    grads = grads_ref[...]
+    pre = dot_nt(rows, weight_ref[:, :width])
+    act_grad = dot_nt(grads, weight_ref[:, width:])
+    phi = 0.5 * (1.0 + lax.erf(pre * ROOT_HALF))
+    act = (pre * phi).astype(jnp.bfloat16)
+    slope = phi + pre * jnp.exp(-0.5 * pre * pre) * INV_ROOT_TAU
+    pre_grad = (act_grad * slope).astype(jnp.bfloat16)
+    part = matmul(act, weight_ref[:, width:])
+    back_part = matmul(pre_grad, weight_ref[:, :width])
+    weight_grad_ref[:, :width] = dot_tn(pre_grad, rows).astype(jnp.bfloat16)
+    weight_grad_ref[:, width:] = dot_tn(act, grads).astype(jnp.bfloat16)
+
+    @pl.when(step == 0)
+    def _():
+        total[...] = part
+        back[...] = back_part
+
+    @pl.when(step > 0)
+    def _():
+        total[...] += part
+        back[...] += back_part
+
+    @pl.when(step == pl.num_programs(0) - 1)
+    def _():
+        out_ref[...] = total[...].astype(out_ref.dtype)
+        back_ref[...] = back[...].astype(back_ref.dtype)
+
+
+def ffn_both(pairs, weight):
+    count, width = pairs.shape[0], pairs.shape[1] // 2
+    hidden = weight.shape[0]
+    block = hidden // BLOCKS
+    return pl.pallas_call(
+        ffn_both_kernel,
+        grid=(BLOCKS,),
+        in_specs=[
+            pl.BlockSpec((count, width), lambda j: (0, 0)),
+            pl.BlockSpec((count, width), lambda j: (0, 1)),
+            pl.BlockSpec((block, 2 * width), lambda j: (j, 0)),
+        ],
+        out_specs=[
+            pl.BlockSpec((block, 2 * width), lambda j: (j, 0)),
+            pl.BlockSpec((count, width), lambda j: (0, 0)),
+            pl.BlockSpec((count, width), lambda j: (0, 0)),
+        ],
+        out_shape=[
+            jax.ShapeDtypeStruct((hidden, 2 * width), jnp.bfloat16),
+            jax.ShapeDtypeStruct((count, width), jnp.bfloat16),
+            jax.ShapeDtypeStruct((count, width), jnp.bfloat16),
+        ],
+        scratch_shapes=[
+            pltpu.VMEM((count, width), jnp.float32),
+            pltpu.VMEM((count, width), jnp.float32),
+        ],
+        name="ffn_both",
+    )(pairs, pairs, weight)
+
+
+def lanes_of(shape):
+    return lax.broadcasted_iota(jnp.int32, shape, len(shape) - 1)
+
+
+def gate_masks(chosen_ref):
+    length = chosen_ref.shape[0]
+    lane = lanes_of((length, MISC))
+    return [chosen_ref[:, k : k + 1] == lane for k in range(2)]
+
+
+def gates_of(masks, probs):
+    return [jnp.sum(jnp.where(mask, probs, 0.0), axis=-1, keepdims=True) for mask in masks]
+
+
+def small_params(weight_ref, width, experts):
+    flipped = weight_ref[:, 4 * width :].astype(jnp.float32).T
+    return [flipped[experts + i : experts + i + 1, :] for i in range(4)]
+
+
+def blocked(count, body):
+    lax.fori_loop(0, count, lambda i, carry: (body(i), carry)[1], 0)
+
+
+def block_of(i, size):
+    return pl.ds(pl.multiple_of(i * size, size), size)
+
+
+def send_grads(place_ref, gates, grad):
+    total = None
+    for k in range(2):
+        part = matmul(place_ref[k], (gates[k] * grad).astype(jnp.bfloat16))
+        total = part if total is None else total + part
+    return total.astype(jnp.bfloat16)
+
+
+def attn_forward_kernel(first, last, experts, *refs):
+    refs = list(refs)
+    if first:
+        state_in = refs.pop(0)
+    else:
+        middle_in, returned_ref, probs_in, chosen_in, pick_ref = refs[:5]
+        refs = refs[5:]
+    weight_ref, chosen_ref, place_ref = refs[:3]
+    refs = refs[3:]
+    if last:
+        grad_ref = refs.pop(0)
+    if not first:
+        state_out = refs.pop(0)
+    qkv_ref, mixed_ref, middle_ref, probs_ref, sent_ref = refs
+    width = weight_ref.shape[0]
+    scale = 1.0 / math.sqrt(width // HEADS)
+    if first:
+        state = state_in[...]
+    else:
+        gates = gates_of(gate_masks(chosen_in), probs_in[...])
+        returned = returned_ref[...]
+        state = middle_in[...]
+        added = [gates[k] * matmul(pick_ref[k], returned) for k in range(2)]
+        state = state + (added[0] + added[1])
+        state_out[...] = state
+    gain_one, bias_one, gain_two, bias_two = small_params(weight_ref, width, experts)
+    normed, _ = standardize(state)
+    attn_in = (normed * gain_one + bias_one).astype(jnp.bfloat16)
+
+    def project(i):
+        cols = block_of(i, 384)
+        qkv_ref[:, cols] = matmul(attn_in, weight_ref[:, cols]).astype(jnp.bfloat16)
+
+    blocked(3 * width // 384, project)
+    length = state.shape[0]
+    half = lanes_of((length, 128)) < 64
+
+    def heads(i):
+        query = qkv_ref[:, block_of(i, 128)]
+        keys = qkv_ref[:, pl.ds(pl.multiple_of(width + i * 128, 128), 128)]
+        values = qkv_ref[:, pl.ds(pl.multiple_of(2 * width + i * 128, 128), 128)]
+        out = []
+        for side in range(2):
+            mine = half if side == 0 else jnp.logical_not(half)
+            scores = dot_nt(jnp.where(mine, query, jnp.zeros_like(query)), keys) * scale
+            log_total = jnp.log(jnp.sum(jnp.exp(scores), axis=-1, keepdims=True))
+            probs_low = jnp.exp(scores - log_total).astype(jnp.bfloat16)
+            out.append(matmul(probs_low, values))
+        mixed_ref[:, block_of(i, 128)] = jnp.where(half, out[0], out[1]).astype(jnp.bfloat16)
+
+    blocked(HEADS // 2, heads)
+    mixed = mixed_ref[...]
+
+    def combine(i):
+        cols = block_of(i, 384)
+        middle_ref[:, cols] = matmul(
+            mixed, weight_ref[:, pl.ds(pl.multiple_of(3 * width + i * 384, 384), 384)]
+        )
+
+    blocked(width // 384, combine)
+    middle = state + middle_ref[...]
+    middle_ref[...] = middle
+    normed_two, _ = standardize(middle)
+    moe_in = (normed_two * gain_two + bias_two).astype(jnp.bfloat16)
+    logits = matmul(moe_in, weight_ref[:, 4 * width :])
+    raised = jnp.where(lanes_of(logits.shape) < experts, jnp.exp(logits), 0.0)
+    probs = raised / jnp.sum(raised, axis=-1, keepdims=True)
+    probs_ref[...] = probs
+    sent = matmul(place_ref[0] + place_ref[1], moe_in)
+    sent_ref[:, :width] = sent.astype(jnp.bfloat16)
+    if last:
+        sent_ref[:, width:] = send_grads(
+            place_ref, gates_of(gate_masks(chosen_ref), probs), grad_ref[...]
+        )
+
+
+def whole(count):
+    return [pl.BlockSpec(memory_space=pltpu.VMEM) for _ in range(count)]
+
+
+def attn_forward(source, weight, chosen, place, cotangent):
+    first, last = not isinstance(source, tuple), cotangent is not None
+    operands = [source] if first else list(source)
+    length, width = operands[0].shape
+    slots = place.shape[1]
+    operands += [weight, chosen, place] + ([cotangent] if last else [])
+    outs = [] if first else [jax.ShapeDtypeStruct((length, width), jnp.float32)]
+    outs += [
+        jax.ShapeDtypeStruct((length, 3 * width), jnp.bfloat16),
+        jax.ShapeDtypeStruct((length, width), jnp.bfloat16),
+        jax.ShapeDtypeStruct((length, width), jnp.float32),
+        jax.ShapeDtypeStruct((length, MISC), jnp.float32),
+        jax.ShapeDtypeStruct((slots, width * (2 if last else 1)), jnp.bfloat16),
+    ]
+    results = pl.pallas_call(
+        functools.partial(attn_forward_kernel, first, last, slots // SLOTS),
+        in_specs=whole(len(operands)),
+        out_specs=whole(len(outs)),
+        out_shape=outs,
+        name="attn_forward",
+    )(*operands)
+    return ([source] if first else []) + list(results)
+
+
+def attn_backward_kernel(last, first, experts, *refs):
+    refs = list(refs)
+    (
+        state_ref,
+        middle_ref,
+        qkv_ref,
+        mixed_ref,
+        probs_ref,
+        chosen_ref,
+        pick_ref,
+        returned_ref,
+        back_ref,
+        grad_ref,
+        weight_ref,
+    ) = refs[:11]
+    refs = refs[11:]
+    if not first:
+        probs_below, chosen_below, place_below = refs[:3]
+        refs = refs[3:]
+    grad_out, weight_grad = refs[:2]
+    refs = refs[2:]
+    if last:
+        output_ref = refs.pop(0)
+    if not first:
+        sent_ref = refs.pop(0)
+    mixed_grad_ref, qkv_grad_ref, work_ref = refs
+    width = weight_ref.shape[0]
+    scale = 1.0 / math.sqrt(width // HEADS)
+    grad = grad_ref[...]
+    length = grad.shape[0]
+    gain_one, bias_one, gain_two, bias_two = small_params(weight_ref, width, experts)
+    masks = gate_masks(chosen_ref)
+    probs = probs_ref[...]
+    middle = middle_ref[...]
+    gates = gates_of(masks, probs)
+    returned = returned_ref[...]
+    picked = [matmul(pick_ref[k], returned) for k in range(2)]
+    if last:
+        output_ref[...] = middle + (gates[0] * picked[0] + gates[1] * picked[1])
+    prob_grad = jnp.zeros_like(probs)
+    for k in range(2):
+        gate_grad = jnp.sum(grad * picked[k], axis=-1, keepdims=True)
+        prob_grad = prob_grad + jnp.where(masks[k], gate_grad, 0.0)
+    logit_grad = (
+        probs * (prob_grad - jnp.sum(probs * prob_grad, axis=-1, keepdims=True))
+    ).astype(jnp.bfloat16)
+    normed_two, inverse_two = standardize(middle)
+    moe_in = (normed_two * gain_two + bias_two).astype(jnp.bfloat16)
+    router_grad = dot_tn(moe_in, logit_grad)
+    moe_in_grad = matmul(pick_ref[0] + pick_ref[1], back_ref[...]) + dot_nt(
+        logit_grad, weight_ref[:, 4 * width :]
+    )
+    second_gain_grad = jnp.sum(moe_in_grad * normed_two, axis=0, keepdims=True)
+    second_bias_grad = jnp.sum(moe_in_grad, axis=0, keepdims=True)
+    middle_grad = grad + norm_backward(moe_in_grad, normed_two, inverse_two, gain_two)
+    work_ref[...] = middle_grad
+    middle_low = middle_grad.astype(jnp.bfloat16)
+    weight_grad[:, 3 * width : 4 * width] = dot_tn(mixed_ref[...], middle_low).astype(jnp.bfloat16)
+    mixed_grad_ref[...] = dot_nt(middle_low, weight_ref[:, 3 * width : 4 * width]).astype(
+        jnp.bfloat16
+    )
+    half = lanes_of((length, 128)) < 64
+
+    def heads(i):
+        query_cols = block_of(i, 128)
+        keys_cols = pl.ds(pl.multiple_of(width + i * 128, 128), 128)
+        values_cols = pl.ds(pl.multiple_of(2 * width + i * 128, 128), 128)
+        query, keys, values = qkv_ref[:, query_cols], qkv_ref[:, keys_cols], qkv_ref[:, values_cols]
+        mixed_grad = mixed_grad_ref[:, query_cols]
+        parts = []
+        for side in range(2):
+            mine = half if side == 0 else jnp.logical_not(half)
+            scores = dot_nt(jnp.where(mine, query, jnp.zeros_like(query)), keys) * scale
+            log_total = jnp.log(jnp.sum(jnp.exp(scores), axis=-1, keepdims=True))
+            probs_att = jnp.exp(scores - log_total)
+            prob_grad_att = dot_nt(jnp.where(mine, mixed_grad, jnp.zeros_like(mixed_grad)), values)
+            row_total = jnp.sum(probs_att * prob_grad_att, axis=-1, keepdims=True)
+            score_low = (probs_att * (prob_grad_att - row_total) * scale).astype(jnp.bfloat16)
+            parts.append(
+                (
+                    matmul(score_low, keys),
+                    dot_tn(score_low, query),
+                    dot_tn(probs_att.astype(jnp.bfloat16), mixed_grad),
+                )
+            )
+        for cols, index in ((query_cols, 0), (keys_cols, 1), (values_cols, 2)):
+            qkv_grad_ref[:, cols] = jnp.where(half, parts[0][index], parts[1][index]).astype(
+                jnp.bfloat16
+            )
+
+    blocked(HEADS // 2, heads)
+    normed_one, inverse_one = standardize(state_ref[...])
+    attn_in = (normed_one * gain_one + bias_one).astype(jnp.bfloat16)
+
+    def weights(i):
+        cols = block_of(i, 384)
+        weight_grad[:, cols] = dot_tn(attn_in, qkv_grad_ref[:, cols]).astype(jnp.bfloat16)
+
+    blocked(3 * width // 384, weights)
+    attn_in_grad = dot_nt(qkv_grad_ref[...], weight_ref[:, : 3 * width])
+    first_gain_grad = jnp.sum(attn_in_grad * normed_one, axis=0, keepdims=True)
+    first_bias_grad = jnp.sum(attn_in_grad, axis=0, keepdims=True)
+    below = work_ref[...] + norm_backward(attn_in_grad, normed_one, inverse_one, gain_one)
+    grad_out[...] = below
+    row = lax.broadcasted_iota(jnp.int32, (MISC, width), 0)
+    vectors = jnp.zeros((MISC, width), jnp.float32)
+    for i, entry in enumerate(
+        (first_gain_grad, first_bias_grad, second_gain_grad, second_bias_grad)
+    ):
+        vectors = jnp.where(row == experts + i, entry, vectors)
+    weight_grad[:, 4 * width :] = (router_grad + vectors.T).astype(jnp.bfloat16)
+    if not first:
+        sent_ref[...] = send_grads(
+            place_below, gates_of(gate_masks(chosen_below), probs_below[...]), below
+        )
+
+
+def attn_backward(kept, returned, back, grad, weight, below):
+    last, first = below is not None, below is None
+    state, qkv, mixed, middle, probs, chosen, pick = kept
+    operands = [state, middle, qkv, mixed, probs, chosen, pick, returned, back, grad, weight]
+    operands += [] if first else list(below)
+    length, width = state.shape
+    slots = returned.shape[0]
+    outs = [
+        jax.ShapeDtypeStruct((length, width), jnp.float32),
+        jax.ShapeDtypeStruct(weight.shape, jnp.bfloat16),
+    ]
+    if last:
+        outs.append(jax.ShapeDtypeStruct((length, width), jnp.float32))
+    if not first:
+        outs.append(jax.ShapeDtypeStruct((slots, width), jnp.bfloat16))
+    return pl.pallas_call(
+        functools.partial(attn_backward_kernel, last, first, slots // SLOTS),
+        in_specs=whole(len(operands)),
+        out_specs=whole(len(outs)),
+        out_shape=outs,
+        scratch_shapes=[
+            pltpu.VMEM((length, width), jnp.bfloat16),
+            pltpu.VMEM((length, 3 * width), jnp.bfloat16),
+            pltpu.VMEM((length, width), jnp.float32),
+        ],
+        name="attn_backward",
+    )(*operands)
+
+
 def exchange(rows, experts):
     count, width = rows.shape
     moved = lax.all_to_all(
@@ -186,9 +534,10 @@
     before = matmul(earlier, named)
     slots = jnp.sum(before[None] * masks.astype(jnp.float32), axis=-1).astype(jnp.int32)
     position = chosen.T * SLOTS + slots
-    return (position[:, :, None] == jnp.arange(experts * SLOTS, dtype=jnp.int32)).astype(
-        jnp.bfloat16
-    )
+    every = jnp.arange(experts * SLOTS, dtype=jnp.int32)
+    pick = (position[:, :, None] == every).astype(jnp.bfloat16)
+    place = (position[:, None, :] == every[:, None]).astype(jnp.bfloat16)
+    return pick, place
 
 
 def unpack_attn(packed, width, experts):
@@ -220,10 +569,8 @@
     cotangent,
 ):
     experts = lax.axis_size("expert")
-    state = inputs[0]
-    length, width = state.shape
-    head_size = width // HEADS
-    scale = 1.0 / math.sqrt(head_size)
+    length, width = inputs.shape[1:]
+    depth = routes.shape[0]
     attn_pack = [
         jnp.concatenate(
             [
@@ -245,165 +592,48 @@
         for layer in range(routes.shape[0])
     ]
     depth = routes.shape[0]
-    expert_ids = jnp.arange(experts, dtype=jnp.int32)
+    source = inputs[0]
     saved = []
     for layer in range(depth):
-        attn_full = lax.all_gather(attn_pack[layer], "wshard", axis=0, tiled=True)
-        gathered = unpack_attn(attn_full, width, experts)
-        gain_one, bias_one, qkv_full, proj_full, gain_two, bias_two, router_full = gathered
-        normed_one, inverse_one = standardize(state)
-        attn_in = (normed_one * gain_one.astype(jnp.float32) + bias_one.astype(jnp.float32)).astype(
-            jnp.bfloat16
+        last = layer == depth - 1
+        weight = lax.all_gather(attn_pack[layer], "wshard", axis=0, tiled=True)
+        chosen = routes[layer, 0]
+        pick, place = routing(chosen, experts)
+        state, qkv, mixed, middle, probs, sent = attn_forward(
+            source, weight, chosen, place, cotangent[0] if last else None
         )
-        qkv = matmul(attn_in, qkv_full).astype(jnp.bfloat16)
-        query = qkv[:, :width].reshape(length, HEADS, head_size)
-        keys = qkv[:, width : 2 * width].reshape(length, HEADS, head_size)
-        values = qkv[:, 2 * width :].reshape(length, HEADS, head_size)
-        scores = jnp.einsum("shd,thd->hst", query, keys, preferred_element_type=jnp.float32) * scale
-        log_total = jnp.log(jnp.sum(jnp.exp(scores), axis=-1, keepdims=True))
-        probs_low = jnp.exp(scores - log_total).astype(jnp.bfloat16)
-        mixed = jnp.einsum("hst,thd->shd", probs_low, values, preferred_element_type=jnp.float32)
-        mixed = mixed.reshape(length, width).astype(jnp.bfloat16)
-        middle = state + matmul(mixed, proj_full)
-        normed_two, inverse_two = standardize(middle)
-        moe_in = (normed_two * gain_two.astype(jnp.float32) + bias_two.astype(jnp.float32)).astype(
-            jnp.bfloat16
-        )
-        logits = matmul(moe_in, router_full)
-        raised = jnp.exp(logits)
-        router_probs = raised / jnp.sum(raised, axis=-1, keepdims=True)
-        chosen = routes[layer, 0]
-        choice_mask = (chosen[..., None] == expert_ids).astype(jnp.float32)
-        gates = jnp.sum(choice_mask * router_probs[:, None, :], axis=-1)
-        select = routing(chosen, experts)
-        select_any = select[0] + select[1]
-        sent = dot_tn(select_any, moe_in).astype(jnp.bfloat16)
         received = exchange(sent, experts)
         expert_full = lax.all_gather(expert_pack[layer], "wshard", axis=0, tiled=True)
-        pre, result = ffn_forward(received, expert_full)
-        kept = (received, pre, expert_full)
+        if last:
+            expert_grad, result, row_grad = ffn_both(received, expert_full)
+            pre = None
+        else:
+            pre, result = ffn_forward(received, expert_full)
         returned = exchange(result, experts)
-        picked = [matmul(select[k], returned) for k in range(2)]
-        state = middle + gates[:, :1] * picked[0] + gates[:, 1:] * picked[1]
-        picked = [entry.astype(jnp.bfloat16) for entry in picked]
-        saved.append(
-            (
-                gathered,
-                normed_one,
-                inverse_one,
-                attn_in,
-                query,
-                keys,
-                values,
-                log_total,
-                mixed,
-                normed_two,
-                inverse_two,
-                moe_in,
-                router_probs,
-                choice_mask,
-                gates,
-                select,
-                picked,
-                kept,
-            )
-        )
+        source = (middle, returned, probs, chosen, pick)
+        kept = (state, qkv, mixed, middle, probs, chosen, pick)
+        saved.append((kept, weight, returned, received, pre, expert_full, place))
     grad = cotangent[0]
     layer_parts = []
     expert_parts = []
     share = None
     for layer in reversed(range(depth)):
-        (
-            gathered,
-            normed_one,
-            inverse_one,
-            attn_in,
-            query,
-            keys,
-            values,
-            log_total,
-            mixed,
-            normed_two,
-            inverse_two,
-            moe_in,
-            router_probs,
-            choice_mask,
-            gates,
-            select,
-            picked,
-            kept,
-        ) = saved[layer]
-        gain_one, bias_one, qkv_full, proj_full, gain_two, bias_two, router_full = gathered
-        gate_grad = jnp.stack(
-            [jnp.sum(grad * picked[k].astype(jnp.float32), axis=-1) for k in range(2)], axis=-1
-        )
-        routed_grad = [(gates[:, k : k + 1] * grad).astype(jnp.bfloat16) for k in range(2)]
-        grad_sent = dot_tn(
-            jnp.concatenate([select[0], select[1]], axis=0), jnp.concatenate(routed_grad, axis=0)
-        ).astype(jnp.bfloat16)
-        grad_received = exchange(grad_sent, experts)
-        rows_kept, pre, expert_full = kept
-        expert_grad, row_grad = ffn_backward(rows_kept, grad_received, pre, expert_full)
+        kept, weight, returned, received, pre, expert_full, _ = saved[layer]
+        if layer < depth - 1:
+            expert_grad, row_grad = ffn_backward(received, exchange(sent, experts), pre, expert_full)
         if share is not None:
             expert_grad, share = lax.optimization_barrier((expert_grad, share))
         expert_part = lax.psum_scatter(expert_grad, "wshard", scatter_dimension=0, tiled=True)
-        back = matmul(select[0] + select[1], exchange(row_grad, experts))
-        prob_grad = jnp.sum(choice_mask * gate_grad[..., None], axis=1)
-        logit_grad = router_probs * (
-            prob_grad - jnp.sum(router_probs * prob_grad, axis=-1, keepdims=True)
-        )
-        logit_grad = logit_grad.astype(jnp.bfloat16)
-        router_grad = matmul(moe_in.T, logit_grad)
-        moe_in_grad = back + matmul(logit_grad, router_full.T)
-        second_gain_grad = jnp.sum(moe_in_grad * normed_two, axis=0)
-        second_bias_grad = jnp.sum(moe_in_grad, axis=0)
-        middle_grad = grad + norm_backward(moe_in_grad, normed_two, inverse_two, gain_two)
-        middle_low = middle_grad.astype(jnp.bfloat16)
-        proj_grad = matmul(mixed.T, middle_low)
-        mixed_grad = (
-            matmul(middle_low, proj_full.T).astype(jnp.bfloat16).reshape(length, HEADS, head_size)
-        )
-        scores = jnp.einsum("shd,thd->hst", query, keys, preferred_element_type=jnp.float32) * scale
-        probs = jnp.exp(scores - log_total)
-        probs_low = probs.astype(jnp.bfloat16)
-        values_grad = jnp.einsum(
-            "hst,shd->thd", probs_low, mixed_grad, preferred_element_type=jnp.float32
-        )
-        prob_grad_att = jnp.einsum(
-            "shd,thd->hst", mixed_grad, values, preferred_element_type=jnp.float32
-        )
-        score_grad = probs * (
-            prob_grad_att - jnp.sum(probs * prob_grad_att, axis=-1, keepdims=True)
-        )
-        score_low = (score_grad * scale).astype(jnp.bfloat16)
-        query_grad = jnp.einsum("hst,thd->shd", score_low, keys, preferred_element_type=jnp.float32)
-        keys_grad = jnp.einsum("hst,shd->thd", score_low, query, preferred_element_type=jnp.float32)
-        qkv_grad = jnp.concatenate(
-            [
-                query_grad.reshape(length, width),
-                keys_grad.reshape(length, width),
-                values_grad.reshape(length, width),
-            ],
-            axis=-1,
-        ).astype(jnp.bfloat16)
-        qkv_grad_weight = matmul(attn_in.T, qkv_grad)
-        attn_in_grad = matmul(qkv_grad, qkv_full.T)
-        first_gain_grad = jnp.sum(attn_in_grad * normed_one, axis=0)
-        first_bias_grad = jnp.sum(attn_in_grad, axis=0)
-        grad = middle_grad + norm_backward(attn_in_grad, normed_one, inverse_one, gain_one)
-        vectors = jnp.stack(
-            [first_gain_grad, first_bias_grad, second_gain_grad, second_bias_grad], axis=1
-        )
-        attn_grad = jnp.concatenate(
-            [
-                qkv_grad_weight.astype(jnp.bfloat16),
-                proj_grad.astype(jnp.bfloat16),
-                router_grad.astype(jnp.bfloat16),
-                vectors.astype(jnp.bfloat16),
-                jnp.zeros((width, MISC - experts - 4), jnp.bfloat16),
-            ],
-            axis=1,
-        )
+        below = None
+        if layer > 0:
+            kept_below, place_below = saved[layer - 1][0], saved[layer - 1][-1]
+            below = (kept_below[4], kept_below[5], place_below)
+        results = attn_backward(kept, returned, exchange(row_grad, experts), grad, weight, below)
+        grad, attn_grad = results[:2]
+        if layer == depth - 1:
+            outputs = results[2]
+        if layer > 0:
+            sent = results[-1]
         attn_grad, expert_part = lax.optimization_barrier((attn_grad, expert_part))
         if share is not None:
             attn_grad, share = lax.optimization_barrier((attn_grad, share))
@@ -422,7 +652,7 @@
     hidden_grads = jnp.stack([entry[0] for entry in expert_parts])[:, None]
     output_grads = jnp.stack([entry[1] for entry in expert_parts])[:, None]
     return (
-        state[None],
+        outputs[None],
         grad[None],
         stacked[0],
         stacked[1],

time: 548 us -> 482 us (0.88); the launches traced: 538 us -> 480 us
  matrix products: 104 us -> 0.45 us
  Pallas kernels: 66.7 us -> 125 us
  local copies, waits for them, and re-layouts: 65 us -> 31.8 us
  blocking collectives: 32.5 us -> 57.6 us
  waiting for transfers between devices: 177 us -> 193 us
  other arithmetic: 24.7 us -> 14.2 us
  starting transfers between devices: 52.6 us -> 43.7 us
    pallas_call x0 -> x5, Pallas kernels: none -> 91.5 us  [the longest x2 41 us: attn_backward(): pl.pallas_call(functools.partial(attn_backward_kernel, last, first, slots...]
    dot_general x16 -> x0, matrix products: 50.8 us -> none  [the longest x2 10.6 us: per_device(): jnp.einsum('hst,shd->thd', score_low, query, preferred_element_type=jnp.f...]
    dot_general x26 -> x2, matrix products: 46.5 us -> 0.45 us  [matmul(): return jnp.dot(left, right, preferred_element_type=jnp.float32)]
    all_to_all x2 -> x3, blocking collectives: 32.5 us -> 57.6 us  [exchange(): lax.all_to_all(rows.reshape(experts, count // experts, width), 'expert',...]
    pallas_call x2 -> x1, Pallas kernels: 38.9 us -> 19.5 us  [ffn_backward(): pl.pallas_call(ffn_backward_kernel, grid=(BLOCKS,), in_specs=[pl.BlockSpe...]
    reduce_scatter x2, waiting for transfers between devices: 0.03 us -> 18.3 us  [per_device(): lax.psum_scatter(expert_grad, 'wshard', scatter_dimension=0, tiled=True)]
    all_to_all x6 -> x4, waiting for transfers between devices: 45 us -> 27.3 us  [exchange(): lax.all_to_all(rows.reshape(experts, count // experts, width), 'expert',...]
    concatenate x2 -> x0, local copies, waits for them, and re-layouts: 16.8 us -> none  [per_device(): jnp.concatenate([qkv_grad_weight.astype(jnp.bfloat16), proj_grad.astype(j...]
  transfers between devices with their start and end apart: 18 -> 16, of which waited for: 12 -> 11; matrix products, arithmetic and copies ran while one was open for 31% -> 5% of each run, Pallas kernels for 6% -> 21%
where the time goes in v3:
time: 482 us; the launch traced here: 480 us
  waiting for transfers between devices  193 us (40%)
  Pallas kernels  125 us (26%)
  blocking collectives  57.6 us (12%)
  starting transfers between devices  43.7 us (9%)
  local copies, waits for them, and re-layouts  31.8 us (7%)
  between operations  14.7 us (3%)
  other arithmetic  14.2 us (3%)
    all_gather x2, waiting for transfers between devices, per_device(): lax.all_gather(expert_pack[layer], 'wshard', axis=0, tiled=True)  57.7 us
    all_to_all x3, blocking collectives, exchange(): lax.all_to_all(rows.reshape(experts, count // experts, width), 'expert',...  57.6 us
    pallas_call x2, Pallas kernels, attn_backward(): pl.pallas_call(functools.partial(attn_backward_kernel, last, first, slots...  41 us
    all_gather x2, waiting for transfers between devices, per_device(): weight = lax.all_gather(attn_pack[layer], 'wshard', axis=0, tiled=True)  39.4 us
    all_to_all x4, waiting for transfers between devices, exchange(): lax.all_to_all(rows.reshape(experts, count // experts, width), 'expert',...  27.3 us
    pallas_call x1, Pallas kernels, ffn_both(): pl.pallas_call(ffn_both_kernel, grid=(BLOCKS,), in_specs=[pl.BlockSpec((c...  25.4 us
    all_to_all x2, waiting for transfers between devices, sum_over_experts(): lax.all_to_all(share.reshape(experts, count // experts, width), 'expert',...  25.2 us
    pallas_call x2, Pallas kernels, attn_forward(): pl.pallas_call(functools.partial(attn_forward_kernel, first, last, slots...  25.1 us
  transfers between devices with their start and end apart: 16, of which 11 were waited for; matrix products, arithmetic and copies ran while one was open for 5% of the time, Pallas kernels for 21%

profile of v3, /device:TPU:24, one launch (start us, length us, event | category | flops | bytes accessed | tf_op | source)
XLA Modules:
  0.0 479.9 jit_solution(2799907812071578897)
XLA Ops:
  7.3 1.3 slice_bitcast_fusion.8
  9.8 1.0 concatenate.12
  11.3 1.3 slice_bitcast_fusion.6
  12.7 1.1 pad_maximum_fusion.1
  15.9 1.1 pad_maximum_fusion.2
  19.9 26.5 %all-gather.5.cloned.1.call-done.refs_1_.refs_10_ = bf16[768,3200]{1,0:T(8,128)(2,1)} async-done(((bf16[96,3200]{1,0:T(8,128)(2,1)}), bf16[768,3200]{1,0:T(8,128)(2,1)}) %all-gather.5.cloned.1.call-update) | async-done | bytes 4915216 | tf_op jit(solution)/shard_map/all_gather | solution.py:599
  46.4 11.6 %attn_forward.2 = (bf16[197,2304]{1,0:T(8,128)(2,1)}, bf16[197,768]{1,0:T(8,128)(2,1)}, f32[197,768]{1,0:T(8,128)}, f32[197,128]{1,0:T(8,128)}, bf16[512,768]{1,0:T(8,128)(2,1)}) custom-call(f32[197,768]{1,0:T(8,128)} %bitcast.119, bf16[768,3200]{1,0:T(8,128)(2,1)} %all-gather.5.cloned.1.call-done.refs_1_.refs_10_, s32[197,2]{1,0:T(8,128)} %bitcast.124, ...), custom_call_target="tpu_custom_call" | custom-call | tf_op jit(solution)/shard_map/attn_forward/pallas_call | solution.py:341
  58.0 6.9 %all-to-all-start = ((bf16[16,32,768]{2,1,0:T(8,128)(2,1)}), bf16[16,32,768]{2,1,0:T(8,128)(2,1)S(1)}, u32[]{:S(2)}, u32[]{:S(2)}) async-start(bf16[16,32,768]{2,1,0:T(8,128)(2,1)} %bitcast.141), calls=%async_computation | async-start | bytes 1572864 | tf_op jit(solution)/shard_map/all_to_all | solution.py:499
  65.4 14.3 %all-to-all-done = bf16[16,32,768]{2,1,0:T(8,128)(2,1)S(1)} async-done(((bf16[16,32,768]{2,1,0:T(8,128)(2,1)}), bf16[16,32,768]{2,1,0:T(8,128)(2,1)S(1)}, u32[]{:S(2)}, u32[]{:S(2)}) %all-to-all-start) | async-done | bytes 786464 | tf_op jit(solution)/shard_map/all_to_all | solution.py:499
  79.7 23.1 %all-gather.7.cloned.1.call-done.weight_ref = bf16[3072,1536]{1,0:T(8,128)(2,1)} async-done(((bf16[384,1536]{1,0:T(8,128)(2,1)}), bf16[3072,1536]{1,0:T(8,128)(2,1)}) %all-gather.7.cloned.1.call-update) | async-done | bytes 9437200 | tf_op jit(solution)/shard_map/all_gather | solution.py:606
  102.8 13.9 %ffn_forward.1 = (f32[512,3072]{1,0:T(8,128)}, bf16[512,768]{1,0:T(8,128)(2,1)}) custom-call(bf16[512,768]{1,0:T(8,128)(2,1)} %bitcast.115, bf16[3072,1536]{1,0:T(8,128)(2,1)} %all-gather.7.cloned.1.call-done.weight_ref), custom_call_target="tpu_custom_call" | custom-call | tf_op jit(solution)/shard_map/ffn_forward/pallas_call | solution.py:77
  116.7 7.2 %all-to-all-start.1 = ((bf16[16,32,768]{2,1,0:T(8,128)(2,1)}), bf16[16,32,768]{2,1,0:T(8,128)(2,1)S(1)}, u32[]{:S(2)}, u32[]{:S(2)}) async-start(bf16[16,32,768]{2,1,0:T(8,128)(2,1)} %bitcast.139), calls=%async_computation.1 | async-start | bytes 1572864 | tf_op jit(solution)/shard_map/all_to_all | solution.py:499
  127.0 12.9 %all-gather.9.cloned.1.call-done.refs_5_.refs_10_ = bf16[768,3200]{1,0:T(8,128)(2,1)} async-done(((bf16[96,3200]{1,0:T(8,128)(2,1)}), bf16[768,3200]{1,0:T(8,128)(2,1)}) %all-gather.9.cloned.1.call-update) | async-done | bytes 4915216 | tf_op jit(solution)/shard_map/all_gather | solution.py:599
  140.8 13.6 %attn_forward.3 = (f32[197,768]{1,0:T(8,128)}, bf16[197,2304]{1,0:T(8,128)(2,1)}, bf16[197,768]{1,0:T(8,128)(2,1)}, f32[197,768]{1,0:T(8,128)}, f32[197,128]{1,0:T(8,128)}, /*index=5*/bf16[512,1536]{1,0:T(8,128)(2,1)}) custom-call(f32[197,768]{1,0:T(8,128)} %get-tuple-element.43.refs_0_.refs_1_, bf16[512,768]{1,0:T(8,128)(2,1)} %bitcast.117, ...), custom_call_target="tpu_custom_call" | custom-call | tf_op jit(solution)/shard_map/attn_forward/pallas_call | solution.py:341
  154.4 6.9 %all-to-all-start.2 = ((bf16[16,32,1536]{2,1,0:T(8,128)(2,1)}), bf16[16,32,1536]{2,1,0:T(8,128)(2,1)S(1)}, u32[]{:S(2)}, u32[]{:S(2)}) async-start(bf16[16,32,1536]{2,1,0:T(8,128)(2,1)} %bitcast.137), calls=%async_computation.2 | async-start | bytes 3145728 | tf_op jit(solution)/shard_map/all_to_all | solution.py:499
  161.5 34.6 %all-gather.11.cloned.1.call-done.weight_ref = bf16[3072,1536]{1,0:T(8,128)(2,1)} async-done(((bf16[384,1536]{1,0:T(8,128)(2,1)}), bf16[3072,1536]{1,0:T(8,128)(2,1)}) %all-gather.11.cloned.1.call-update) | async-done | bytes 9437200 | tf_op jit(solution)/shard_map/all_gather | solution.py:606
  196.2 1.1 copy-done
  197.3 25.4 %ffn_both.1 = (bf16[3072,1536]{1,0:T(8,128)(2,1)}, bf16[512,768]{1,0:T(8,128)(2,1)}, bf16[512,768]{1,0:T(8,128)(2,1)}) custom-call(bf16[512,1536]{1,0:T(8,128)(2,1)} %bitcast.113, bf16[512,1536]{1,0:T(8,128)(2,1)} %bitcast.114, bf16[3072,1536]{1,0:T(8,128)(2,1)} %all-gather.11.cloned.1.call-done.weight_ref), custom_call_target="tpu_custom_call" | custom-call | tf_op jit(solution)/shard_map/ffn_both/pallas_call | solution.py:186
  222.7 1.1 copy-done.12
  223.9 21.8 %all_to_all.55 = bf16[16,32,768]{2,1,0:T(8,128)(2,1)} all-to-all(bf16[16,32,768]{2,1,0:T(8,128)(2,1)S(1)} %bitcast.142), channel_id=1, replica_groups=mesh['expert'=16,'wshard'=8] {'expert'}, dimensions={0} | all-to-all | bytes 1572864 | tf_op jit(solution)/shard_map/all_to_all | solution.py:499
  245.6 3.6 all-to-all-start.4
  250.2 13.0 %all-to-all-done.4 = bf16[16,32,768]{2,1,0:T(8,128)(2,1)S(1)} async-done(((bf16[16,32,768]{2,1,0:T(8,128)(2,1)}), bf16[16,32,768]{2,1,0:T(8,128)(2,1)S(1)}, u32[]{:S(2)}, u32[]{:S(2)}) %all-to-all-start.4) | async-done | bytes 786464 | tf_op jit(solution)/shard_map/all_to_all | solution.py:499
  264.0 21.3 %attn_backward.2 = (f32[197,768]{1,0:T(8,128)}, bf16[768,3200]{1,0:T(8,128)(2,1)}, f32[197,768]{1,0:T(8,128)}, bf16[512,768]{1,0:T(8,128)(2,1)}) custom-call(f32[197,768]{1,0:T(8,128)} %get-tuple-element.47.refs_0_, f32[197,768]{1,0:T(8,128)} %get-tuple-element.48.refs_1_, bf16[197,2304]{1,0:T(8,128)(2,1)} %get-tuple-element.49.refs_2_, ...), custom_call_target="tpu_custom_call" | custom-call | tf_op jit(solution)/shard_map/attn_backward/pallas_call | solution.py:483
  285.4 1.1 copy-done.10
  286.4 16.9 %all_to_all.56 = bf16[16,32,768]{2,1,0:T(8,128)(2,1)} all-to-all(bf16[16,32,768]{2,1,0:T(8,128)(2,1)S(1)} %bitcast.138), channel_id=1, replica_groups=mesh['expert'=16,'wshard'=8] {'expert'}, dimensions={0} | all-to-all | bytes 1572864 | tf_op jit(solution)/shard_map/all_to_all | solution.py:499
  303.3 19.5 %ffn_backward.1 = (bf16[3072,1536]{1,0:T(8,128)(2,1)}, bf16[512,768]{1,0:T(8,128)(2,1)}) custom-call(bf16[512,768]{1,0:T(8,128)(2,1)} %bitcast.116, bf16[512,768]{1,0:T(8,128)(2,1)} %bitcast.128, f32[512,3072]{1,0:T(8,128)} %get-tuple-element.59.pre_ref, bf16[3072,1536]{1,0:T(8,128)(2,1)} %all-gather.7.cloned.1.call-done.weight_ref), custom_call_target="tpu_custom_call" | custom-call | tf_op jit(solution)/shard_map/ffn_backward/pallas_call | solution.py:128
  322.9 1.1 copy-done.11
  323.9 18.9 %all_to_all.57 = bf16[16,32,768]{2,1,0:T(8,128)(2,1)} all-to-all(bf16[16,32,768]{2,1,0:T(8,128)(2,1)S(1)} %bitcast.140), channel_id=1, replica_groups=mesh['expert'=16,'wshard'=8] {'expert'}, dimensions={0} | all-to-all | bytes 1572864 | tf_op jit(solution)/shard_map/all_to_all | solution.py:499
  342.8 19.7 %attn_backward.3 = (f32[197,768]{1,0:T(8,128)}, bf16[768,3200]{1,0:T(8,128)(2,1)}) custom-call(f32[197,768]{1,0:T(8,128)} %bitcast.120, f32[197,768]{1,0:T(8,128)} %get-tuple-element.43.refs_0_.refs_1_, bf16[197,2304]{1,0:T(8,128)(2,1)} %get-tuple-element.56.refs_2_, bf16[197,768]{1,0:T(8,128)(2,1)} %get-tuple-element.57.refs_3_, ...), custom_call_target="tpu_custom_call" | custom-call | tf_op jit(solution)/shard_map/attn_backward/pallas_call | solution.py:483
  362.6 18.3 %reduce-scatter.9.cloned.1.call-done = bf16[384,1536]{1,0:T(8,128)(2,1)} async-done(((bf16[3072,1536]{1,0:T(8,128)(2,1)}), bf16[384,1536]{1,0:T(8,128)(2,1)}) %reduce-scatter.9.cloned.1.call-update) | async-done | bytes 1179664 | tf_op jit(solution)/shard_map/reduce_scatter | solution.py:626
  380.9 1.0 copy-done.14
  381.9 1.1 reshape.103
  383.0 7.1 %all-to-all-start.9 = ((bf16[16,6,3200]{2,1,0:T(8,128)(2,1)}), bf16[16,6,3200]{2,1,0:T(8,128)(2,1)S(1)}, u32[]{:S(2)}, u32[]{:S(2)}) async-start(bf16[16,6,3200]{2,1,0:T(8,128)(2,1)} %reshape.103), calls=%async_computation.13 | async-start | bytes 1638400 | tf_op jit(solution)/shard_map/all_to_all | solution.py:511
  390.1 1.4 copy.188
  391.6 1.4 copy.189
  393.0 1.1 slice_bitcast_fusion.2
  394.1 10.9 %all-to-all-done.9 = bf16[16,6,3200]{2,1,0:T(8,128)(2,1)S(1)} async-done(((bf16[16,6,3200]{2,1,0:T(8,128)(2,1)}), bf16[16,6,3200]{2,1,0:T(8,128)(2,1)S(1)}, u32[]{:S(2)}, u32[]{:S(2)}) %all-to-all-start.9) | async-done | bytes 614432 | tf_op jit(solution)/shard_map/all_to_all | solution.py:511
  406.2 3.6 all-to-all-start.10
  411.3 2.0 copy.190
  413.2 2.8 fusion.1
  416.0 7.4 %all-to-all-done.10 = bf16[16,6,3200]{2,1,0:T(8,128)(2,1)S(1)} async-done(((bf16[16,6,3200]{2,1,0:T(8,128)(2,1)}), bf16[16,6,3200]{2,1,0:T(8,128)(2,1)S(1)}, u32[]{:S(2)}, u32[]{:S(2)}) %all-to-all-start.10) | async-done | bytes 614432 | tf_op jit(solution)/shard_map/all_to_all | solution.py:519
  423.6 2.1 reshape.102
  425.7 3.7 all-to-all-start.7
  430.0 14.3 %all-to-all-done.7 = bf16[16,6,3200]{2,1,0:T(8,128)(2,1)S(1)} async-done(((bf16[16,6,3200]{2,1,0:T(8,128)(2,1)}), bf16[16,6,3200]{2,1,0:T(8,128)(2,1)S(1)}, u32[]{:S(2)}, u32[]{:S(2)}) %all-to-all-start.7) | async-done | bytes 614432 | tf_op jit(solution)/shard_map/all_to_all | solution.py:511
  445.5 4.0 all-to-all-start.8
  449.5 17.1 %all-to-all-done.8 = bf16[16,6,3200]{2,1,0:T(8,128)(2,1)S(1)} async-done(((bf16[16,6,3200]{2,1,0:T(8,128)(2,1)}), bf16[16,6,3200]{2,1,0:T(8,128)(2,1)S(1)}, u32[]{:S(2)}, u32[]{:S(2)}) %all-to-all-start.8) | async-done | bytes 614432 | tf_op jit(solution)/shard_map/all_to_all | solution.py:519
  468.8 1.8 pad_maximum_fusion.3
  470.6 1.3 pad_maximum_fusion
  (150 shorter events, 20.9 us)
Async XLA Ops:
  7.2 1.4 copy-start.18
  7.2 1.4 copy-start.21
  7.2 1.5 copy-start.23
  7.2 1.7 copy-start.24
  7.2 1.8 copy-start.25
  7.2 1.9 copy-start.26
  7.2 39.1 %all-gather.5.cloned.1.call-start = ((), (), s32[]{:S(2)}) async-start(), calls=%async_computation.15 | async-start | bytes 5529600 | tf_op jit(solution)/shard_map/all_gather | solution.py:599
  8.6 2.3 copy-start.7
  9.8 1.2 copy-start.19
  10.9 91.9 %all-gather.7.cloned.1.call-start = ((), (), s32[]{:S(2)}) async-start(), calls=%async_computation.16 | async-start | bytes 10616832 | tf_op jit(solution)/shard_map/all_gather | solution.py:606
  13.8 0.7 copy-start.27
  13.8 0.8 copy-start.20
  13.8 126.1 %all-gather.9.cloned.1.call-start = ((), (), s32[]{:S(2)}) async-start(), calls=%async_computation.17 | async-start | bytes 5529600 | tf_op jit(solution)/shard_map/all_gather | solution.py:599
  15.6 180.6 %all-gather.11.cloned.1.call-start = ((), (), s32[]{:S(2)}) async-start(), calls=%async_computation.18 | async-start | bytes 10616832 | tf_op jit(solution)/shard_map/all_gather | solution.py:606
  15.9 1.1 copy-start.22
  17.0 1.1 copy-start.16
  17.2 2.7 copy-start.3
  58.0 21.7 %all-to-all-start = ((bf16[16,32,768]{2,1,0:T(8,128)(2,1)}), bf16[16,32,768]{2,1,0:T(8,128)(2,1)S(1)}, u32[]{:S(2)}, u32[]{:S(2)}) async-start(bf16[16,32,768]{2,1,0:T(8,128)(2,1)} %bitcast.141), calls=%async_computation | async-start | bytes 1572864 | tf_op jit(solution)/shard_map/all_to_all | solution.py:499
  65.0 59.1 %copy-start.5 = (s32[1,1,197,2]{3,2,1,0:T(8,128)}, s32[1,1,197,2]{3,2,1,0:T(8,128)S(1)}, u32[]{:S(2)}) copy-start(s32[1,1,197,2]{3,2,1,0:T(8,128)S(1)} %copy.198) | copy-start | bytes 4732
  79.7 23.1 %copy-start.1 = (bf16[16,32,768]{2,1,0:T(8,128)(2,1)}, bf16[16,32,768]{2,1,0:T(8,128)(2,1)S(1)}, u32[]{:S(2)}) copy-start(bf16[16,32,768]{2,1,0:T(8,128)(2,1)S(1)} %all-to-all-done) | copy-start | bytes 2359300
  116.7 7.5 %copy-start.17 = (f32[1,197,768]{2,0,1:T(1,128)S(1)}, f32[1,197,768]{2,0,1:T(1,128)}, u32[]{:S(2)}) copy-start(f32[1,197,768]{2,0,1:T(1,128)} %param.23) | copy-start | bytes 1815556
  116.7 23.2 %all-to-all-start.1 = ((bf16[16,32,768]{2,1,0:T(8,128)(2,1)}), bf16[16,32,768]{2,1,0:T(8,128)(2,1)S(1)}, u32[]{:S(2)}, u32[]{:S(2)}) async-start(bf16[16,32,768]{2,1,0:T(8,128)(2,1)} %bitcast.139), calls=%async_computation.1 | async-start | bytes 1572864 | tf_op jit(solution)/shard_map/all_to_all | solution.py:499
  139.9 0.9 copy-start.2
  154.4 41.8 %all-to-all-start.2 = ((bf16[16,32,1536]{2,1,0:T(8,128)(2,1)}), bf16[16,32,1536]{2,1,0:T(8,128)(2,1)S(1)}, u32[]{:S(2)}, u32[]{:S(2)}) async-start(bf16[16,32,1536]{2,1,0:T(8,128)(2,1)} %bitcast.137), calls=%async_computation.2 | async-start | bytes 3145728 | tf_op jit(solution)/shard_map/all_to_all | solution.py:499
  161.3 124.0 %reduce-scatter.5.cloned.1.call-start = ((), (), s32[]{:S(2)}) async-start(), calls=%async_computation.19 | async-start | bytes 10616832 | tf_op jit(solution)/shard_map/reduce_scatter | solution.py:626
  196.2 1.1 copy-start
  222.7 1.1 copy-start.12
  245.6 17.5 %all-to-all-start.4 = ((bf16[16,32,768]{2,1,0:T(8,128)(2,1)}), bf16[16,32,768]{2,1,0:T(8,128)(2,1)S(1)}, u32[]{:S(2)}, u32[]{:S(2)}) async-start(bf16[16,32,768]{2,1,0:T(8,128)(2,1)} %bitcast.36), calls=%async_computation.4 | async-start | bytes 1572864 | tf_op jit(solution)/shard_map/all_to_all | solution.py:499
  249.2 73.6 %reduce-scatter.7.cloned.1.call-start = ((), (), s32[]{:S(2)}) async-start(), calls=%async_computation.20 | async-start | bytes 5529600 | tf_op jit(solution)/shard_map/reduce_scatter | solution.py:641
  263.2 0.9 copy-start.4
  285.3 1.1 copy-start.10
  285.3 95.5 %reduce-scatter.9.cloned.1.call-start = ((), (), s32[]{:S(2)}) async-start(), calls=%async_computation.21 | async-start | bytes 10616832 | tf_op jit(solution)/shard_map/reduce_scatter | solution.py:626
  322.8 1.1 copy-start.11
  322.8 100.8 %reduce-scatter.11.cloned.1.call-start = ((), (), s32[]{:S(2)}) async-start(), calls=%async_computation.22 | async-start | bytes 5529600 | tf_op jit(solution)/shard_map/reduce_scatter | solution.py:641
  380.9 1.1 copy-start.14
  381.9 8.2 %copy-start.13 = (f32[197,768]{1,0:T(8,128)S(1)}, f32[197,768]{1,0:T(8,128)}, u32[]{:S(2)}) copy-start(f32[197,768]{1,0:T(8,128)} %get-tuple-element.55) | copy-start | bytes 1815556
  383.0 8.5 %copy-start.15 = (f32[197,768]{1,0:T(8,128)S(1)}, f32[197,768]{1,0:T(8,128)}, u32[]{:S(2)}) copy-start(f32[197,768]{1,0:T(8,128)} %get-tuple-element.62) | copy-start | bytes 1815556
  383.0 22.0 %all-to-all-start.9 = ((bf16[16,6,3200]{2,1,0:T(8,128)(2,1)}), bf16[16,6,3200]{2,1,0:T(8,128)(2,1)S(1)}, u32[]{:S(2)}, u32[]{:S(2)}) async-start(bf16[16,6,3200]{2,1,0:T(8,128)(2,1)} %reshape.103), calls=%async_computation.13 | async-start | bytes 1638400 | tf_op jit(solution)/shard_map/all_to_all | solution.py:511
  390.1 2.9 copy-start.8
  405.2 4.6 copy-start.9
  406.2 17.2 %all-to-all-start.10 = ((bf16[16,6,3200]{2,1,0:T(8,128)(2,1)}), bf16[16,6,3200]{2,1,0:T(8,128)(2,1)S(1)}, u32[]{:S(2)}, u32[]{:S(2)}) async-start(bf16[16,6,3200]{2,1,0:T(8,128)(2,1)} %broadcast_in_dim.51), calls=%async_computation.14 | async-start | bytes 1638400 | tf_op jit(solution)/shard_map/all_to_all | solution.py:519
  409.8 1.3 copy-start.6
  425.7 18.7 %all-to-all-start.7 = ((bf16[16,6,3200]{2,1,0:T(8,128)(2,1)}), bf16[16,6,3200]{2,1,0:T(8,128)(2,1)S(1)}, u32[]{:S(2)}, u32[]{:S(2)}) async-start(bf16[16,6,3200]{2,1,0:T(8,128)(2,1)} %reshape.102), calls=%async_computation.11 | async-start | bytes 1638400 | tf_op jit(solution)/shard_map/all_to_all | solution.py:511
  445.5 21.2 %all-to-all-start.8 = ((bf16[16,6,3200]{2,1,0:T(8,128)(2,1)}), bf16[16,6,3200]{2,1,0:T(8,128)(2,1)S(1)}, u32[]{:S(2)}, u32[]{:S(2)}) async-start(bf16[16,6,3200]{2,1,0:T(8,128)(2,1)} %broadcast_in_dim.50), calls=%async_computation.12 | async-start | bytes 1638400 | tf_op jit(solution)/shard_map/all_to_all | solution.py:519
Sparse Core Ops, SparseCore 0:
  11.0 35.3 all-gather.4
  48.6 54.1 all-gather.6
  104.5 35.3 all-gather.8
  142.0 54.1 all-gather.10
  222.9 57.6 reduce-scatter.4
  285.5 34.8 reduce-scatter.6
  323.0 57.8 reduce-scatter.8
  383.3 37.5 reduce-scatter.10

commit v4 on v3

--- a/solution.py
+++ b/solution.py
@@ -94,7 +94,9 @@
     )(rows, weight)
 
 
-def ffn_backward_kernel(rows_ref, grads_ref, pre_ref, weight_ref, weight_grad_ref, out_ref, total):
+def ffn_backward_kernel(
+    rows_ref, grads_ref, pre_ref, weight_ref, hidden_grad_ref, output_grad_ref, out_ref, total
+):
     step = pl.program_id(0)
     width = rows_ref.shape[1]
     pre = pre_ref[...]
@@ -104,8 +106,8 @@
     act_grad = dot_nt(grads, weight_ref[:, width:])
     slope = phi + pre * jnp.exp(-0.5 * pre * pre) * INV_ROOT_TAU
     pre_grad = (act_grad * slope).astype(jnp.bfloat16)
-    weight_grad_ref[:, :width] = dot_tn(pre_grad, rows_ref[...]).astype(jnp.bfloat16)
-    weight_grad_ref[:, width:] = dot_tn(act, grads).astype(jnp.bfloat16)
+    hidden_grad_ref[...] = dot_tn(pre_grad, rows_ref[...]).astype(jnp.bfloat16)
+    output_grad_ref[...] = dot_tn(act, grads).astype(jnp.bfloat16)
     part = matmul(pre_grad, weight_ref[:, :width])
 
     @pl.when(step == 0)
@@ -135,11 +137,13 @@
             pl.BlockSpec((block, 2 * width), lambda j: (j, 0)),
         ],
         out_specs=[
-            pl.BlockSpec((block, 2 * width), lambda j: (j, 0)),
+            pl.BlockSpec((block, width), lambda j: (j, 0)),
+            pl.BlockSpec((block, width), lambda j: (j, 0)),
             pl.BlockSpec((count, width), lambda j: (0, 0)),
         ],
         out_shape=[
-            jax.ShapeDtypeStruct((hidden, 2 * width), jnp.bfloat16),
+            jax.ShapeDtypeStruct((hidden, width), jnp.bfloat16),
+            jax.ShapeDtypeStruct((hidden, width), jnp.bfloat16),
             jax.ShapeDtypeStruct((count, width), jnp.bfloat16),
         ],
         scratch_shapes=[pltpu.VMEM((count, width), jnp.float32)],
@@ -620,7 +624,9 @@
     for layer in reversed(range(depth)):
         kept, weight, returned, received, pre, expert_full, _ = saved[layer]
         if layer < depth - 1:
-            expert_grad, row_grad = ffn_backward(received, exchange(sent, experts), pre, expert_full)
+            expert_grad, output_grad, row_grad = ffn_backward(
+                received, exchange(sent, experts), pre, expert_full
+            )
         if share is not None:
             expert_grad, share = lax.optimization_barrier((expert_grad, share))
         expert_part = lax.psum_scatter(expert_grad, "wshard", scatter_dimension=0, tiled=True)
@@ -639,10 +645,17 @@
             attn_grad, share = lax.optimization_barrier((attn_grad, share))
             layer_parts.append(unpack_attn(sum_over_experts(share, experts), width, experts))
         share = lax.psum_scatter(attn_grad, "wshard", scatter_dimension=0, tiled=True)
+        if layer < depth - 1:
+            output_grad, share = lax.optimization_barrier((output_grad, share))
+            output_part = lax.psum_scatter(
+                output_grad, "wshard", scatter_dimension=0, tiled=True
+            )
+        else:
+            output_part = expert_part[:, width:]
         expert_parts.append(
             (
                 expert_part[:, :width].T.astype(jnp.float32),
-                expert_part[:, width:].astype(jnp.float32),
+                output_part.astype(jnp.float32),
             )
         )
     layer_parts.append(unpack_attn(sum_over_experts(share, experts), width, experts))

time: 482 us -> 501 us (1.039)
  blocking collectives: 57.6 us -> 79.4 us
  waiting for transfers between devices: 193 us -> 203 us
  starting transfers between devices: 43.7 us -> 36.3 us
    reduce_scatter x2, waiting for transfers between devices: 0.02 us -> 38.7 us  [per_device(): lax.psum_scatter(attn_grad, 'wshard', scatter_dimension=0, tiled=True)]
    all_to_all x0 -> x1, blocking collectives: none -> 21.9 us  [sum_over_experts(): lax.all_to_all(share.reshape(experts, count // experts, width), 'expert',...]
    reduce_scatter x2, waiting for transfers between devices: 18.3 us -> 0.01 us  [per_device(): lax.psum_scatter(expert_grad, 'wshard', scatter_dimension=0, tiled=True)]
    all_to_all x2 -> x1, waiting for transfers between devices: 25.2 us -> 14.4 us  [sum_over_experts(): lax.all_to_all(share.reshape(experts, count // experts, width), 'expert',...]
    all_to_all x2 -> x1, starting transfers between devices: 10.8 us -> 3.62 us  [sum_over_experts(): lax.all_to_all(share.reshape(experts, count // experts, width), 'expert',...]
    unnamed x67 -> x69, local copies, waits for them, and re-layouts: 15.6 us -> 15.6 us
  transfers between devices with their start and end apart: 16 -> 16, of which waited for: 11 -> 10; matrix products, arithmetic and copies ran while one was open for 5% -> 6% of each run, Pallas kernels for 21% -> 20%
where the time goes in v4:
time: 501 us; the launch traced here: 500 us
  waiting for transfers between devices  203 us (41%)
  Pallas kernels  125 us (25%)
  blocking collectives  79.4 us (16%)
  starting transfers between devices  36.3 us (7%)
  local copies, waits for them, and re-layouts  28.2 us (6%)
  between operations  14.4 us (3%)
  other arithmetic  13.1 us (3%)
    all_gather x2, waiting for transfers between devices, per_device(): lax.all_gather(expert_pack[layer], 'wshard', axis=0, tiled=True)  57.9 us
    all_to_all x3, blocking collectives, exchange(): lax.all_to_all(rows.reshape(experts, count // experts, width), 'expert',...  57.5 us
    pallas_call x2, Pallas kernels, attn_backward(): pl.pallas_call(functools.partial(attn_backward_kernel, last, first, slots...  41.1 us
    all_gather x2, waiting for transfers between devices, per_device(): weight = lax.all_gather(attn_pack[layer], 'wshard', axis=0, tiled=True)  39.4 us
    reduce_scatter x2, waiting for transfers between devices, per_device(): lax.psum_scatter(attn_grad, 'wshard', scatter_dimension=0, tiled=True)  38.7 us
    all_to_all x4, waiting for transfers between devices, exchange(): lax.all_to_all(rows.reshape(experts, count // experts, width), 'expert',...  27.3 us
    pallas_call x1, Pallas kernels, ffn_both(): pl.pallas_call(ffn_both_kernel, grid=(BLOCKS,), in_specs=[pl.BlockSpec((c...  25.5 us
    pallas_call x2, Pallas kernels, attn_forward(): pl.pallas_call(functools.partial(attn_forward_kernel, first, last, slots...  25 us
  transfers between devices with their start and end apart: 16, of which 10 were waited for; matrix products, arithmetic and copies ran while one was open for 6% of the time, Pallas kernels for 20%

profile of v4, /device:TPU:24, one launch (start us, length us, event | category | flops | bytes accessed | tf_op | source)
XLA Modules:
  0.0 499.5 jit_solution(12339182486282805533)
XLA Ops:
  7.3 1.3 slice_bitcast_fusion.6
  9.8 1.0 concatenate.12
  11.3 1.3 slice_bitcast_fusion.4
  12.7 1.1 pad_maximum_fusion.1
  14.5 1.0 concatenate.14
  15.9 1.1 pad_maximum_fusion.2
  19.9 26.5 %all-gather.5.cloned.1.call-done.refs_1_.refs_10_ = bf16[768,3200]{1,0:T(8,128)(2,1)} async-done(((bf16[96,3200]{1,0:T(8,128)(2,1)}), bf16[768,3200]{1,0:T(8,128)(2,1)}) %all-gather.5.cloned.1.call-update) | async-done | bytes 4915216 | tf_op jit(solution)/shard_map/all_gather | solution.py:603
  46.4 11.5 %attn_forward.2 = (bf16[197,2304]{1,0:T(8,128)(2,1)}, bf16[197,768]{1,0:T(8,128)(2,1)}, f32[197,768]{1,0:T(8,128)}, f32[197,128]{1,0:T(8,128)}, bf16[512,768]{1,0:T(8,128)(2,1)}) custom-call(f32[197,768]{1,0:T(8,128)} %bitcast.117, bf16[768,3200]{1,0:T(8,128)(2,1)} %all-gather.5.cloned.1.call-done.refs_1_.refs_10_, s32[197,2]{1,0:T(8,128)} %bitcast.122, ...), custom_call_target="tpu_custom_call" | custom-call | tf_op jit(solution)/shard_map/attn_forward/pallas_call | solution.py:345
  57.9 6.9 %all-to-all-start = ((bf16[16,32,768]{2,1,0:T(8,128)(2,1)}), bf16[16,32,768]{2,1,0:T(8,128)(2,1)S(1)}, u32[]{:S(2)}, u32[]{:S(2)}) async-start(bf16[16,32,768]{2,1,0:T(8,128)(2,1)} %bitcast.139), calls=%async_computation | async-start | bytes 1572864 | tf_op jit(solution)/shard_map/all_to_all | solution.py:503
  65.3 14.3 %all-to-all-done = bf16[16,32,768]{2,1,0:T(8,128)(2,1)S(1)} async-done(((bf16[16,32,768]{2,1,0:T(8,128)(2,1)}), bf16[16,32,768]{2,1,0:T(8,128)(2,1)S(1)}, u32[]{:S(2)}, u32[]{:S(2)}) %all-to-all-start) | async-done | bytes 786464 | tf_op jit(solution)/shard_map/all_to_all | solution.py:503
  79.6 23.1 %all-gather.7.cloned.1.call-done.weight_ref = bf16[3072,1536]{1,0:T(8,128)(2,1)} async-done(((bf16[384,1536]{1,0:T(8,128)(2,1)}), bf16[3072,1536]{1,0:T(8,128)(2,1)}) %all-gather.7.cloned.1.call-update) | async-done | bytes 9437200 | tf_op jit(solution)/shard_map/all_gather | solution.py:610
  102.8 13.9 %ffn_forward.1 = (f32[512,3072]{1,0:T(8,128)}, bf16[512,768]{1,0:T(8,128)(2,1)}) custom-call(bf16[512,768]{1,0:T(8,128)(2,1)} %bitcast.113, bf16[3072,1536]{1,0:T(8,128)(2,1)} %all-gather.7.cloned.1.call-done.weight_ref), custom_call_target="tpu_custom_call" | custom-call | tf_op jit(solution)/shard_map/ffn_forward/pallas_call | solution.py:77
  116.7 7.2 %all-to-all-start.1 = ((bf16[16,32,768]{2,1,0:T(8,128)(2,1)}), bf16[16,32,768]{2,1,0:T(8,128)(2,1)S(1)}, u32[]{:S(2)}, u32[]{:S(2)}) async-start(bf16[16,32,768]{2,1,0:T(8,128)(2,1)} %bitcast.137), calls=%async_computation.1 | async-start | bytes 1572864 | tf_op jit(solution)/shard_map/all_to_all | solution.py:503
  126.0 0.9 fusion.3.refs_7_
  127.0 12.9 %all-gather.9.cloned.1.call-done.refs_5_.refs_10_ = bf16[768,3200]{1,0:T(8,128)(2,1)} async-done(((bf16[96,3200]{1,0:T(8,128)(2,1)}), bf16[768,3200]{1,0:T(8,128)(2,1)}) %all-gather.9.cloned.1.call-update) | async-done | bytes 4915216 | tf_op jit(solution)/shard_map/all_gather | solution.py:603
  140.8 13.5 %attn_forward.3 = (f32[197,768]{1,0:T(8,128)}, bf16[197,2304]{1,0:T(8,128)(2,1)}, bf16[197,768]{1,0:T(8,128)(2,1)}, f32[197,768]{1,0:T(8,128)}, f32[197,128]{1,0:T(8,128)}, /*index=5*/bf16[512,1536]{1,0:T(8,128)(2,1)}) custom-call(f32[197,768]{1,0:T(8,128)} %get-tuple-element.46.refs_0_.refs_1_, bf16[512,768]{1,0:T(8,128)(2,1)} %bitcast.115, ...), custom_call_target="tpu_custom_call" | custom-call | tf_op jit(solution)/shard_map/attn_forward/pallas_call | solution.py:345
  154.2 6.9 %all-to-all-start.2 = ((bf16[16,32,1536]{2,1,0:T(8,128)(2,1)}), bf16[16,32,1536]{2,1,0:T(8,128)(2,1)S(1)}, u32[]{:S(2)}, u32[]{:S(2)}) async-start(bf16[16,32,1536]{2,1,0:T(8,128)(2,1)} %bitcast.135), calls=%async_computation.2 | async-start | bytes 3145728 | tf_op jit(solution)/shard_map/all_to_all | solution.py:503
  161.4 34.8 %all-gather.11.cloned.1.call-done.weight_ref = bf16[3072,1536]{1,0:T(8,128)(2,1)} async-done(((bf16[384,1536]{1,0:T(8,128)(2,1)}), bf16[3072,1536]{1,0:T(8,128)(2,1)}) %all-gather.11.cloned.1.call-update) | async-done | bytes 9437200 | tf_op jit(solution)/shard_map/all_gather | solution.py:610
  196.2 1.1 copy-done
  197.4 25.5 %ffn_both.1 = (bf16[3072,1536]{1,0:T(8,128)(2,1)}, bf16[512,768]{1,0:T(8,128)(2,1)}, bf16[512,768]{1,0:T(8,128)(2,1)}) custom-call(bf16[512,1536]{1,0:T(8,128)(2,1)} %bitcast.111, bf16[512,1536]{1,0:T(8,128)(2,1)} %bitcast.112, bf16[3072,1536]{1,0:T(8,128)(2,1)} %all-gather.11.cloned.1.call-done.weight_ref), custom_call_target="tpu_custom_call" | custom-call | tf_op jit(solution)/shard_map/ffn_both/pallas_call | solution.py:190
  222.8 1.1 copy-done.11
  224.0 21.7 %all_to_all.55 = bf16[16,32,768]{2,1,0:T(8,128)(2,1)} all-to-all(bf16[16,32,768]{2,1,0:T(8,128)(2,1)S(1)} %bitcast.140), channel_id=1, replica_groups=mesh['expert'=16,'wshard'=8] {'expert'}, dimensions={0} | all-to-all | bytes 1572864 | tf_op jit(solution)/shard_map/all_to_all | solution.py:503
  245.7 3.6 all-to-all-start.4
  250.2 13.0 %all-to-all-done.4 = bf16[16,32,768]{2,1,0:T(8,128)(2,1)S(1)} async-done(((bf16[16,32,768]{2,1,0:T(8,128)(2,1)}), bf16[16,32,768]{2,1,0:T(8,128)(2,1)S(1)}, u32[]{:S(2)}, u32[]{:S(2)}) %all-to-all-start.4) | async-done | bytes 786464 | tf_op jit(solution)/shard_map/all_to_all | solution.py:503
  264.1 21.3 %attn_backward.2 = (f32[197,768]{1,0:T(8,128)}, bf16[768,3200]{1,0:T(8,128)(2,1)}, f32[197,768]{1,0:T(8,128)}, bf16[512,768]{1,0:T(8,128)(2,1)}) custom-call(f32[197,768]{1,0:T(8,128)} %get-tuple-element.50.refs_0_, f32[197,768]{1,0:T(8,128)} %get-tuple-element.51.refs_1_, bf16[197,2304]{1,0:T(8,128)(2,1)} %get-tuple-element.52.refs_2_, ...), custom_call_target="tpu_custom_call" | custom-call | tf_op jit(solution)/shard_map/attn_backward/pallas_call | solution.py:487
  285.4 1.1 copy-done.9
  286.5 16.9 %all_to_all.56 = bf16[16,32,768]{2,1,0:T(8,128)(2,1)} all-to-all(bf16[16,32,768]{2,1,0:T(8,128)(2,1)S(1)} %bitcast.136), channel_id=1, replica_groups=mesh['expert'=16,'wshard'=8] {'expert'}, dimensions={0} | all-to-all | bytes 1572864 | tf_op jit(solution)/shard_map/all_to_all | solution.py:503
  303.4 19.5 %ffn_backward.1 = (bf16[3072,768]{1,0:T(8,128)(2,1)}, bf16[3072,768]{1,0:T(8,128)(2,1)}, bf16[512,768]{1,0:T(8,128)(2,1)}) custom-call(bf16[512,768]{1,0:T(8,128)(2,1)} %bitcast.114, bf16[512,768]{1,0:T(8,128)(2,1)} %bitcast.126, f32[512,3072]{1,0:T(8,128)} %get-tuple-element.62.pre_ref, bf16[3072,1536]{1,0:T(8,128)(2,1)} %all-gather.7.cloned.1.call-done.weight_ref), custom_call_target="tpu_custom_call" | custom-call | tf_op jit(solution)/shard_map/ffn_backward/pallas_call | solution.py:130
  323.0 1.1 copy-done.10
  324.0 18.8 %all_to_all.57 = bf16[16,32,768]{2,1,0:T(8,128)(2,1)} all-to-all(bf16[16,32,768]{2,1,0:T(8,128)(2,1)S(1)} %bitcast.138), channel_id=1, replica_groups=mesh['expert'=16,'wshard'=8] {'expert'}, dimensions={0} | all-to-all | bytes 1572864 | tf_op jit(solution)/shard_map/all_to_all | solution.py:503
  342.9 19.8 %attn_backward.3 = (f32[197,768]{1,0:T(8,128)}, bf16[768,3200]{1,0:T(8,128)(2,1)}) custom-call(f32[197,768]{1,0:T(8,128)} %bitcast.118, f32[197,768]{1,0:T(8,128)} %get-tuple-element.46.refs_0_.refs_1_, bf16[197,2304]{1,0:T(8,128)(2,1)} %get-tuple-element.59.refs_2_, bf16[197,768]{1,0:T(8,128)(2,1)} %get-tuple-element.60.refs_3_, ...), custom_call_target="tpu_custom_call" | custom-call | tf_op jit(solution)/shard_map/attn_backward/pallas_call | solution.py:487
  362.7 38.7 %reduce-scatter.12.cloned.1.call-done = bf16[96,3200]{1,0:T(8,128)(2,1)} async-done(((bf16[768,3200]{1,0:T(8,128)(2,1)}), bf16[96,3200]{1,0:T(8,128)(2,1)}) %reduce-scatter.12.cloned.1.call-update) | async-done | bytes 614416 | tf_op jit(solution)/shard_map/reduce_scatter | solution.py:647
  401.4 1.0 copy-done.13
  402.7 21.9 %all_to_all.58 = bf16[16,6,3200]{2,1,0:T(8,128)(2,1)S(1)} all-to-all(bf16[16,6,3200]{2,1,0:T(8,128)(2,1)S(1)} %reshape.103), channel_id=1, replica_groups=mesh['expert'=16,'wshard'=8] {'expert'}, dimensions={0} | all-to-all | bytes 1228800 | tf_op jit(solution)/shard_map/all_to_all | solution.py:515
  424.8 0.9 broadcast_in_dim.51
  425.8 3.8 all-to-all-start.10
  429.5 1.4 copy.188
  431.0 1.4 copy.189
  433.9 2.0 copy.190
  435.8 11.0 %all-to-all-done.10 = bf16[16,6,3200]{2,1,0:T(8,128)(2,1)S(1)} async-done(((bf16[16,6,3200]{2,1,0:T(8,128)(2,1)}), bf16[16,6,3200]{2,1,0:T(8,128)(2,1)S(1)}, u32[]{:S(2)}, u32[]{:S(2)}) %all-to-all-start.10) | async-done | bytes 614432 | tf_op jit(solution)/shard_map/all_to_all | solution.py:523
  447.0 1.1 reshape.102
  448.1 3.6 all-to-all-start.7
  452.4 14.4 %all-to-all-done.7 = bf16[16,6,3200]{2,1,0:T(8,128)(2,1)S(1)} async-done(((bf16[16,6,3200]{2,1,0:T(8,128)(2,1)}), bf16[16,6,3200]{2,1,0:T(8,128)(2,1)S(1)}, u32[]{:S(2)}, u32[]{:S(2)}) %all-to-all-start.7) | async-done | bytes 614432 | tf_op jit(solution)/shard_map/all_to_all | solution.py:515
  467.0 0.9 broadcast_in_dim.50
  467.9 3.6 all-to-all-start.8
  471.6 14.0 %all-to-all-done.8 = bf16[16,6,3200]{2,1,0:T(8,128)(2,1)S(1)} async-done(((bf16[16,6,3200]{2,1,0:T(8,128)(2,1)}), bf16[16,6,3200]{2,1,0:T(8,128)(2,1)S(1)}, u32[]{:S(2)}, u32[]{:S(2)}) %all-to-all-start.8) | async-done | bytes 614432 | tf_op jit(solution)/shard_map/all_to_all | solution.py:523
  489.1 1.3 pad_maximum_fusion
  490.4 2.6 fusion.1
  (153 shorter events, 17.5 us)
Async XLA Ops:
  7.2 1.4 copy-start.19
  7.2 1.4 copy-start.22
  7.2 1.5 copy-start.24
  7.2 1.7 copy-start.25
  7.2 1.8 copy-start.26
  7.2 1.9 copy-start.27
  7.2 39.1 %all-gather.5.cloned.1.call-start = ((), (), s32[]{:S(2)}) async-start(), calls=%async_computation.16 | async-start | bytes 5529600 | tf_op jit(solution)/shard_map/all_gather | solution.py:603
  8.6 2.3 copy-start.7
  9.8 1.2 copy-start.20
  10.9 91.9 %all-gather.7.cloned.1.call-start = ((), (), s32[]{:S(2)}) async-start(), calls=%async_computation.17 | async-start | bytes 10616832 | tf_op jit(solution)/shard_map/all_gather | solution.py:610
  13.8 0.7 copy-start.28
  13.8 0.8 copy-start.21
  13.8 126.1 %all-gather.9.cloned.1.call-start = ((), (), s32[]{:S(2)}) async-start(), calls=%async_computation.18 | async-start | bytes 5529600 | tf_op jit(solution)/shard_map/all_gather | solution.py:603
  15.6 180.6 %all-gather.11.cloned.1.call-start = ((), (), s32[]{:S(2)}) async-start(), calls=%async_computation.19 | async-start | bytes 10616832 | tf_op jit(solution)/shard_map/all_gather | solution.py:610
  15.9 1.1 copy-start.23
  17.0 1.1 copy-start.16
  17.2 2.7 copy-start.3
  57.9 21.7 %all-to-all-start = ((bf16[16,32,768]{2,1,0:T(8,128)(2,1)}), bf16[16,32,768]{2,1,0:T(8,128)(2,1)S(1)}, u32[]{:S(2)}, u32[]{:S(2)}) async-start(bf16[16,32,768]{2,1,0:T(8,128)(2,1)} %bitcast.139), calls=%async_computation | async-start | bytes 1572864 | tf_op jit(solution)/shard_map/all_to_all | solution.py:503
  65.0 59.1 %copy-start.5 = (s32[1,1,197,2]{3,2,1,0:T(8,128)}, s32[1,1,197,2]{3,2,1,0:T(8,128)S(1)}, u32[]{:S(2)}) copy-start(s32[1,1,197,2]{3,2,1,0:T(8,128)S(1)} %copy.198) | copy-start | bytes 4732
  79.6 23.1 %copy-start.1 = (bf16[16,32,768]{2,1,0:T(8,128)(2,1)}, bf16[16,32,768]{2,1,0:T(8,128)(2,1)S(1)}, u32[]{:S(2)}) copy-start(bf16[16,32,768]{2,1,0:T(8,128)(2,1)S(1)} %all-to-all-done) | copy-start | bytes 2359300
  116.7 7.5 %copy-start.17 = (f32[1,197,768]{2,0,1:T(1,128)S(1)}, f32[1,197,768]{2,0,1:T(1,128)}, u32[]{:S(2)}) copy-start(f32[1,197,768]{2,0,1:T(1,128)} %param.23) | copy-start | bytes 1815556
  116.7 23.2 %all-to-all-start.1 = ((bf16[16,32,768]{2,1,0:T(8,128)(2,1)}), bf16[16,32,768]{2,1,0:T(8,128)(2,1)S(1)}, u32[]{:S(2)}, u32[]{:S(2)}) async-start(bf16[16,32,768]{2,1,0:T(8,128)(2,1)} %bitcast.137), calls=%async_computation.1 | async-start | bytes 1572864 | tf_op jit(solution)/shard_map/all_to_all | solution.py:503
  139.9 0.9 copy-start.2
  154.2 42.0 %all-to-all-start.2 = ((bf16[16,32,1536]{2,1,0:T(8,128)(2,1)}), bf16[16,32,1536]{2,1,0:T(8,128)(2,1)S(1)}, u32[]{:S(2)}, u32[]{:S(2)}) async-start(bf16[16,32,1536]{2,1,0:T(8,128)(2,1)} %bitcast.135), calls=%async_computation.2 | async-start | bytes 3145728 | tf_op jit(solution)/shard_map/all_to_all | solution.py:503
  161.2 124.1 %reduce-scatter.6.cloned.1.call-start = ((), (), s32[]{:S(2)}) async-start(), calls=%async_computation.20 | async-start | bytes 10616832 | tf_op jit(solution)/shard_map/reduce_scatter | solution.py:632
  196.2 1.1 copy-start
  222.8 1.1 copy-start.11
  245.7 17.5 %all-to-all-start.4 = ((bf16[16,32,768]{2,1,0:T(8,128)(2,1)}), bf16[16,32,768]{2,1,0:T(8,128)(2,1)S(1)}, u32[]{:S(2)}, u32[]{:S(2)}) async-start(bf16[16,32,768]{2,1,0:T(8,128)(2,1)} %bitcast.36), calls=%async_computation.4 | async-start | bytes 1572864 | tf_op jit(solution)/shard_map/all_to_all | solution.py:503
  249.3 73.6 %reduce-scatter.8.cloned.1.call-start = ((), (), s32[]{:S(2)}) async-start(), calls=%async_computation.21 | async-start | bytes 5529600 | tf_op jit(solution)/shard_map/reduce_scatter | solution.py:647
  263.2 0.9 copy-start.4
  285.3 1.1 copy-start.9
  285.4 77.3 %reduce-scatter.10.cloned.1.call-start = ((), (), s32[]{:S(2)}) async-start(), calls=%async_computation.22 | async-start | bytes 5308416 | tf_op jit(solution)/shard_map/reduce_scatter | solution.py:632
  322.9 1.1 copy-start.10
  322.9 78.5 %reduce-scatter.12.cloned.1.call-start = ((), (), s32[]{:S(2)}) async-start(), calls=%async_computation.23 | async-start | bytes 5529600 | tf_op jit(solution)/shard_map/reduce_scatter | solution.py:647
  362.7 127.7 %reduce-scatter.14.cloned.1.call-start = ((), (), s32[]{:S(2)}) async-start(), calls=%async_computation.24 | async-start | bytes 5308416 | tf_op jit(solution)/shard_map/reduce_scatter | solution.py:650
  401.4 1.1 copy-start.13
  424.8 4.7 copy-start.12
  425.7 5.2 %copy-start.14 = (f32[197,768]{1,0:T(8,128)S(1)}, f32[197,768]{1,0:T(8,128)}, u32[]{:S(2)}) copy-start(f32[197,768]{1,0:T(8,128)} %get-tuple-element.65) | copy-start | bytes 1815556
  425.8 21.1 %all-to-all-start.10 = ((bf16[16,6,3200]{2,1,0:T(8,128)(2,1)}), bf16[16,6,3200]{2,1,0:T(8,128)(2,1)S(1)}, u32[]{:S(2)}, u32[]{:S(2)}) async-start(bf16[16,6,3200]{2,1,0:T(8,128)(2,1)} %broadcast_in_dim.51), calls=%async_computation.14 | async-start | bytes 1638400 | tf_op jit(solution)/shard_map/all_to_all | solution.py:523
  429.5 2.9 copy-start.8
  432.4 1.3 copy-start.18
  435.8 11.2 %copy-start.15 = (bf16[96,3200]{1,0:T(8,128)(2,1)S(1)}, bf16[96,3200]{1,0:T(8,128)(2,1)}, u32[]{:S(2)}) copy-start(bf16[96,3200]{1,0:T(8,128)(2,1)} %reduce-scatter.12.cloned.1.call-done) | copy-start | bytes 1843204
  448.1 18.7 %all-to-all-start.7 = ((bf16[16,6,3200]{2,1,0:T(8,128)(2,1)}), bf16[16,6,3200]{2,1,0:T(8,128)(2,1)S(1)}, u32[]{:S(2)}, u32[]{:S(2)}) async-start(bf16[16,6,3200]{2,1,0:T(8,128)(2,1)} %reshape.102), calls=%async_computation.11 | async-start | bytes 1638400 | tf_op jit(solution)/shard_map/all_to_all | solution.py:515
  467.9 17.7 %all-to-all-start.8 = ((bf16[16,6,3200]{2,1,0:T(8,128)(2,1)}), bf16[16,6,3200]{2,1,0:T(8,128)(2,1)S(1)}, u32[]{:S(2)}, u32[]{:S(2)}) async-start(bf16[16,6,3200]{2,1,0:T(8,128)(2,1)} %broadcast_in_dim.50), calls=%async_computation.12 | async-start | bytes 1638400 | tf_op jit(solution)/shard_map/all_to_all | solution.py:523
  489.0 1.3 copy-start.6
Sparse Core Ops, SparseCore 0:
  11.0 35.3 all-gather.4
  48.6 54.1 all-gather.6
  104.5 35.3 all-gather.8
  142.0 54.1 all-gather.10
  223.0 57.5 reduce-scatter.5
  285.5 34.8 reduce-scatter.7
  323.1 37.9 reduce-scatter.9
  363.5 37.8 reduce-scatter.11
  403.8 38.6 reduce-scatter.13
